TPU v7x, 128 devices: a whole 4x4x4 slice. The times are simulated.
128 devices in a mesh: row: 8 (over z, x_hi), col: 16 (over y, x_lo, core).
Axes of the slice: x: 4 (x_hi: 2, x_lo: 2; x = x_hi * 2 + x_lo), y: 4, z: 4, core: 2. Of those that a mesh axis runs over, the one named last changes fastest.
Arguments:
- patches: bfloat16 [98304, 1536], P(('row', 'col')), may hold values from -6 to 6
- dest: int32 [98304], P(('row', 'col')), may hold values from -1 to 511, as said below
- background: bfloat16 [1536], replicated, may hold values from -6 to 6
- conv_weight: float32 [7, 7, 1536], replicated, may hold values from -0.875 to 0.875
- conv_bias: float32 [1536], replicated, may hold values from -3 to 3
- norm_gain: float32 [1536], replicated, may hold values from 0.1 to 1.9
- norm_bias: float32 [1536], replicated, may hold values from -3 to 3
- w_in: bfloat16 [6144, 1536], P('col'), may hold values from -0.15625 to 0.15625
- b_in: bfloat16 [6144], P('col'), may hold values from -3 to 3
- w_out: bfloat16 [6144, 1536], P('col'), may hold values from -0.078125 to 0.078125
- b_out: float32 [1536], replicated, may hold values from -3 to 3
- layer_scale: float32 [1536], replicated, may hold values from 0.3 to 1.5
Outputs:
- features: bfloat16 [256, 256, 1536], P('row', 'col')
Inputs may be any that keep to these rules, and one draw needn't show every extreme that they name: `dest`: -1 marks an empty slot; no cell is named twice among all slots sent to one device; in every draw some device fills all 48 slots it sends to some device, and some device receives a patch for every one of its cells.
All inputs are finite; a program needn't handle non-finite values.
Results may differ from a plain program's by a relative error of at most 0.0046.
Values may be sent and summed in bfloat16 or wider, within the bound.
No kernel may reach another device: no remote copies, remote signals or barrier semaphores. Data moves between devices by JAX's collectives and lax.ppermute only.
A program may use at most 128 MiB of HBM per device.

v0:
```python
import functools

import jax
import jax.numpy as jnp
from jax import lax
from jax.experimental import pallas as pl
from jax.experimental.pallas import tpu as pltpu
from jax.sharding import PartitionSpec as P


TH = 32
TW = 16
SHARD = 384
HALF = SHARD // 2
LANES = 128
BAND = 8
ROWS = 256
UNITS = 256

VMEM = pltpu.VMEM


def device_index(x, y, z, core):
    x, y, z = x % 4, y % 4, z % 4
    return (z * 2 + x // 2) * 16 + y * 4 + (x % 2) * 2 + core


def routes(move):
    return [
        (device_index(x, y, z, core), device_index(*move(x, y, z, core)))
        for x in range(4)
        for y in range(4)
        for z in range(4)
        for core in range(2)
    ]


def send(value, move):
    return lax.ppermute(value, ("row", "col"), routes(move))


def to_partner(x, y, z, core):
    return x, y, z, 1 - core


def along_y(x, y, z, core):
    return x, y + 1 - 2 * core, z, core


def along_z(x, y, z, core):
    return x, y, z + 1 - 2 * core, core


def along_x(x, y, z, core):
    return x + 1 - 2 * core, y, z, core


def back_x(x, y, z, core):
    return x - 1 + 2 * core, y, z, core


def halo(cells, axis, dim, width):
    count = lax.axis_size(axis)
    ends = count - 1
    head = lax.slice_in_dim(cells, 0, width, axis=dim)
    tail = lax.slice_in_dim(cells, cells.shape[dim] - width, cells.shape[dim], axis=dim)
    return (
        lax.ppermute(tail, axis, [(i, i + 1) for i in range(ends)]),
        lax.ppermute(head, axis, [(i + 1, i) for i in range(ends)]),
    )


def whole(space=VMEM):
    return pl.BlockSpec(memory_space=space)


def join_kernel(left_ref, right_ref, out_ref):
    split = left_ref.shape[1]
    out_ref[:, :split] = left_ref[...]
    out_ref[:, split:] = right_ref[...]


def join(left, right):
    rows, a = left.shape
    b = right.shape[1]
    block = 128
    return pl.pallas_call(
        join_kernel,
        out_shape=jax.ShapeDtypeStruct((rows, a + b), left.dtype),
        grid=(rows // block,),
        in_specs=[pl.BlockSpec((block, a), lambda i: (i, 0)), pl.BlockSpec((block, b), lambda i: (i, 0))],
        out_specs=pl.BlockSpec((block, a + b), lambda i: (i, 0)),
        cost_estimate=pl.CostEstimate(flops=0, bytes_accessed=4 * rows * (a + b), transcendentals=0),
        name="join",
    )(left, right)


def stack_kernel(half_ref, *refs):
    *sources, out_ref, sems = refs
    start = pl.multiple_of(half_ref[0] * HALF, HALF)
    copies = [
        pltpu.make_async_copy(source.at[pl.ds(start, HALF)], out_ref.at[pl.ds(k * HALF, HALF)], sems.at[k])
        for k, source in enumerate(sources)
    ]
    for copy in copies:
        copy.start()
    for copy in copies:
        copy.wait()


def stack(half, *sources):
    channels = sources[0].shape[1]
    return pl.pallas_call(
        stack_kernel,
        out_shape=jax.ShapeDtypeStruct((len(sources) * HALF, channels), jnp.bfloat16),
        in_specs=[whole(pltpu.SMEM)] + [whole(pl.ANY)] * len(sources),
        out_specs=whole(),
        scratch_shapes=[pltpu.SemaphoreType.DMA((len(sources),))],
        cost_estimate=pl.CostEstimate(flops=0, bytes_accessed=4 * len(sources) * HALF * channels, transcendentals=0),
        name="stack",
    )(half, *sources)


def conv_kernel(first, count, ends, *refs):
    grid_ref, top_ref, bottom_ref, left_ref, right_ref, weight_ref, bias_ref = refs[:7]
    if ends:
        gain_ref, shift_ref, before, out_ref, stage, conv = refs[7:]
    else:
        conv, stage = refs[7:]

    def tile(t, carry):
        at = pl.ds(pl.multiple_of((first + t) * LANES, LANES), LANES)
        stage[3 : 3 + TH, 8:24, :] = grid_ref[:, :, at].astype(jnp.float32)
        stage[0:3, 8:24, :] = top_ref[:, :, at].astype(jnp.float32)
        stage[3 + TH : 6 + TH, 8:24, :] = bottom_ref[:, :, at].astype(jnp.float32)
        stage[:, 5:8, :] = left_ref[:, :, at].astype(jnp.float32)
        stage[:, 24:27, :] = right_ref[:, :, at].astype(jnp.float32)
        base = jnp.broadcast_to(bias_ref[0:1, at], (TW, LANES))

        def band(b, carry):
            acc = [base] * BAND
            for along in range(7):
                taps = [
                    jnp.broadcast_to(weight_ref[across * 7 + along : across * 7 + along + 1, at], (TW, LANES))
                    for across in range(7)
                ]
                for r in range(BAND + 6):
                    value = stage[b * BAND + r, 5 + along : 5 + along + TW, :]
                    for across in range(7):
                        o = r - across
                        if 0 <= o < BAND:
                            acc[o] = acc[o] + value * taps[across]
            for o in range(BAND):
                conv[t, pl.ds(pl.multiple_of((b * BAND + o) * TW, TW), TW), :] = acc[o]
            return carry

        return lax.fori_loop(0, TH // BAND, band, carry)

    lax.fori_loop(0, count, tile, 0)
    if not ends:
        return
    tiles = first + count
    channels = tiles * LANES

    def norm(b, carry):
        rows = pl.ds(pl.multiple_of(b * 16, 16), 16)
        values = [before[t, rows, :] for t in range(first)] + [conv[t, rows, :] for t in range(count)]
        mean = jnp.sum(sum(values), axis=-1, keepdims=True) * (1.0 / channels)
        centred = [v - mean for v in values]
        var = jnp.sum(sum(v * v for v in centred), axis=-1, keepdims=True) * (1.0 / channels)
        inverse = lax.rsqrt(var + 1e-06)
        for t in range(tiles):
            at = slice(t * LANES, (t + 1) * LANES)
            out_ref[rows, at] = (centred[t] * inverse * gain_ref[0:1, at] + shift_ref[0:1, at]).astype(
                jnp.bfloat16
            )
        return carry

    lax.fori_loop(0, TH * TW // 16, norm, 0)


def conv_call(first, count, inputs, ends=None):
    tiles = VMEM((count, TH * TW, LANES), jnp.float32)
    stage = VMEM((TH + 6, 32, LANES), jnp.float32)
    if ends is None:
        out, scratch, more = jax.ShapeDtypeStruct(tiles.shape, jnp.float32), [stage], ()
    else:
        out = jax.ShapeDtypeStruct((TH * TW, (first + count) * LANES), jnp.bfloat16)
        scratch, more = [stage, tiles], ends
    return pl.pallas_call(
        functools.partial(conv_kernel, first, count, ends is not None),
        out_shape=out,
        in_specs=[whole()] * (7 + len(more)),
        out_specs=whole(),
        scratch_shapes=scratch,
        cost_estimate=pl.CostEstimate(
            flops=100 * TH * TW * count * LANES, bytes_accessed=8 * TH * TW * count * LANES, transcendentals=0
        ),
        name="conv",
    )(*inputs, *more)


PHI = (
    0.7978849411010742, 0.03633308410644531, -3.259496588725597e-05, -5.5306198191829026e-05,
    3.964745246776147e-06, -1.3226342332472996e-07, 1.7561730958348676e-09,
)


def gelu(pre):
    x = jnp.clip(pre, -5.3, 5.3)
    s = x * x
    p = PHI[-1]
    for c in PHI[-2::-1]:
        p = p * s + c
    half = 0.5 * pre
    return half + half * jnp.tanh(x * p)


def mlp_kernel(plan, count, adds, *refs):
    x_ref, bias_ref = refs[:2]
    pieces = refs[2 : 2 + count]
    acc_ref = refs[2 + count] if adds else None
    out_ref, w_in, w_out, hid, sems = refs[2 + count + adds :]
    blocks = w_in.shape[0] // UNITS
    bands = x_ref.shape[0] // ROWS
    ins, outs, at = [], [], 0
    for k, (a, row_a, b, row_b, size) in enumerate(plan):
        ins.append(pltpu.make_async_copy(pieces[a].at[pl.ds(row_a, size)], w_in.at[pl.ds(at, size)], sems.at[k, 0]))
        outs.append(pltpu.make_async_copy(pieces[b].at[pl.ds(row_b, size)], w_out.at[pl.ds(at, size)], sems.at[k, 1]))
        at += size
    for copy in ins + outs:
        copy.start()
    early = next(k for k in range(len(plan) + 1) if sum(p[4] for p in plan[:k]) >= 3 * UNITS)

    def first(r, h):
        return lax.dot_general(
            x_ref[r * ROWS : (r + 1) * ROWS, :],
            w_in[h * UNITS : (h + 1) * UNITS, :],
            (((1,), (1,)), ((), ())),
            preferred_element_type=jnp.float32,
        )

    def middle(r, h, pre):
        at = slice(h * UNITS, (h + 1) * UNITS)
        hid[r * ROWS : (r + 1) * ROWS, at] = gelu(pre + bias_ref[0:1, at]).astype(jnp.bfloat16)

    def second(r, n):
        rows, at = slice(r * ROWS, (r + 1) * ROWS), slice(n * UNITS, (n + 1) * UNITS)
        total = jnp.dot(hid[rows, :], w_out[:, at], preferred_element_type=jnp.float32)
        if adds:
            total = total + acc_ref[rows, at]
        out_ref[rows, at] = total.astype(out_ref.dtype)

    tasks = [(r, h) for r in range(bands) for h in range(blocks)]
    done = [(r, n) for r in range(bands) for n in range(w_out.shape[1] // UNITS)]
    for copy in ins[:early]:
        copy.wait()
    waiting, sent = None, 0
    for k, (r, h) in enumerate(tasks):
        if k == 3:
            for copy in ins[early:] + outs:
                copy.wait()
        pre = first(r, h)
        if waiting is not None:
            middle(*waiting)
        waiting = (r, h, pre)
        if r > 0 and h > 0:
            second(*done[sent])
            sent += 1
    middle(*waiting)
    for item in done[sent:]:
        second(*item)


def mlp(x, bias, pieces, plan, acc=None, out_dtype=jnp.float32):
    m, channels = x.shape
    hidden = sum(p[4] for p in plan)
    adds = acc is not None
    return pl.pallas_call(
        functools.partial(mlp_kernel, plan, len(pieces), int(adds)),
        out_shape=jax.ShapeDtypeStruct((m, channels), out_dtype),
        in_specs=[whole()] * 2 + [whole(pl.ANY)] * len(pieces) + [whole()] * adds,
        out_specs=whole(),
        scratch_shapes=[
            VMEM((hidden, channels), jnp.bfloat16),
            VMEM((hidden, channels), jnp.bfloat16),
            VMEM((m, hidden), jnp.bfloat16),
            pltpu.SemaphoreType.DMA((len(plan), 2)),
        ],
        cost_estimate=pl.CostEstimate(
            flops=4 * m * hidden * channels, bytes_accessed=4 * hidden * channels, transcendentals=m * hidden
        ),
        name="mlp",
    )(x, bias.reshape(1, hidden), *pieces, *([acc] if adds else []))


def local(
    patches,
    dest,
    background,
    conv_weight,
    conv_bias,
    norm_gain,
    norm_bias,
    w_in,
    b_in,
    w_out,
    b_out,
    layer_scale,
):
    cells = TH * TW
    channels = patches.shape[1]
    row, col = lax.axis_index("row"), lax.axis_index("col")
    my_y, my_lo, my_core, my_h = col // 4, (col // 2) % 2, col % 2, (row // 2) % 2

    lane = lax.broadcasted_iota(jnp.int32, (768, 128), 1)
    high, low = (dest >> 4)[:, None], (dest & 15)[:, None]
    spread = jnp.pad(b_in.reshape(48, 8), ((0, 0), (8, 112)))
    extra = jnp.where(
        lane == 0,
        high.astype(jnp.bfloat16),
        jnp.where(lane == 1, low.astype(jnp.bfloat16), jnp.tile(spread, (16, 1))),
    )
    moved = lax.all_to_all(join(patches, extra), "col", split_axis=0, concat_axis=0, tiled=True)

    w_in_p, w_out_p = send(w_in, to_partner), send(w_out, to_partner)
    half = my_h.astype(jnp.int32).reshape(1)
    near_a = send(stack(half, w_in, w_out), along_y)
    near_b = send(stack(half, w_in_p, w_out_p), along_y)
    near_a_z = send(near_a, along_z)
    far = send(near_a, along_y)
    near_a_p = send(near_a, to_partner)
    near_b_z = send(near_b, along_z)
    near_b_p = send(near_b, to_partner)
    far_z = send(far, along_z)
    far_p = send(far, to_partner)
    near_a_zp = send(near_a_z, to_partner)
    near_b_zp = send(near_b_z, to_partner)
    far_zp = send(far_z, to_partner)

    bias = moved[:, channels + 8 : channels + 16].reshape(4, 2, 2, 2, HALF)
    bias = lax.dynamic_index_in_dim(bias, my_lo, axis=1, keepdims=False)
    bias = jnp.where(my_core == 1, bias[:, ::-1], bias)
    turned = jnp.where(my_h == 1, bias[:, :, ::-1], bias)
    ahead = 2 * my_core - 1

    def at(array, step):
        return lax.dynamic_index_in_dim(array, (my_y + step + 4) % 4, axis=0, keepdims=False)

    b_one, b_two, b_far = at(turned, ahead), at(turned, -ahead), at(turned, 2)
    b0 = at(bias, 0).reshape(-1)
    b1 = jnp.concatenate([b_one[0, 0], b_one[1, 0], b_two[1, 0], b_two[0, 0]])
    b2 = jnp.concatenate([b_one[0, 1], b_one[1, 1], b_two[1, 1], b_two[0, 1]])
    b3 = jnp.concatenate([b_far[0, 0], b_far[1, 0], b_far[0, 1], b_far[1, 1]])
    early = (w_in, w_out, w_in_p, w_out_p, near_a, near_b, near_a_p, near_b_p)
    early_plan = ((0, 0, 1, 0, SHARD), (2, 0, 3, 0, SHARD)) + tuple((a, 0, a, HALF, HALF) for a in range(4, 8))
    early_bias = jnp.concatenate([b0, b1]).astype(jnp.float32)
    late = (near_a_z, near_b_z, near_a_zp, near_b_zp, far, far_p, far_z, far_zp)
    late_plan = tuple((a, 0, a, HALF, HALF) for a in range(8))
    late_bias = jnp.concatenate([b2, b3]).astype(jnp.float32)

    where = (moved[:, channels].astype(jnp.int32) << 4) + moved[:, channels + 1].astype(jnp.int32)
    onehot = where[None, :] == jnp.arange(cells, dtype=jnp.int32)[:, None]
    placed = jnp.dot(
        onehot.astype(jnp.bfloat16), moved[:, :channels], preferred_element_type=jnp.float32
    )
    present = jnp.any(onehot, axis=1)
    grid = jnp.where(present[:, None], placed, background.astype(jnp.float32)[None, :]).astype(
        jnp.bfloat16
    )
    block = grid.reshape(TH, TW, channels)
    top, bottom = halo(block, "row", 0, 3)
    tall = [
        jnp.concatenate([part[:, cut] for part in (top, block, bottom)], axis=0)
        for cut in (slice(TW - 3, TW), slice(0, 3))
    ]
    ends = lax.axis_size("col") - 1
    left = lax.ppermute(tall[0], "col", [(i, i + 1) for i in range(ends)])
    right = lax.ppermute(tall[1], "col", [(i + 1, i) for i in range(ends)])
    inputs = (block, top, bottom, left, right, conv_weight.reshape(49, channels), conv_bias[None])
    tiles = channels // LANES
    before = conv_call(0, tiles // 2, inputs)
    flat = conv_call(tiles // 2, tiles // 2, inputs, (norm_gain[None], norm_bias[None], before))

    other = send(flat, along_x)
    mine = mlp(flat, early_bias, early, early_plan)
    theirs = mlp(other, early_bias, early, early_plan)
    theirs = mlp(other, late_bias, late, late_plan, acc=theirs, out_dtype=jnp.bfloat16)
    returned = send(theirs, back_x)
    mine = mlp(flat, late_bias, late, late_plan, acc=mine)
    mixed = mine + returned.astype(jnp.float32)
    result = grid.astype(jnp.float32) + layer_scale * (mixed + b_out)
    return result.astype(jnp.bfloat16).reshape(TH, TW, channels)


def solution(mesh):
    placed = (
        P(("row", "col"), None),
        P(("row", "col")),
        P(),
        P(),
        P(),
        P(),
        P(),
        P("col", None),
        P("col"),
        P("col", None),
        P(),
        P(),
    )

    def step(*args):
        return local(*args)

    step = jax.shard_map(
        step, mesh=mesh, in_specs=placed, out_specs=P("row", "col", None), check_vma=False
    )
    return step
```

profile of v0, /device:TPU:1, one launch (start us, length us, event | category | flops | bytes accessed | tf_op | source)
XLA Modules:
  0.0 202.0 jit_solution(7764941559767158143)
XLA Ops:
  2.5 5.0 %join.1 = bf16[768,1664]{1,0:T(8,128)(2,1)} custom-call(bf16[768,1536]{1,0:T(8,128)(2,1)} %left_ref.1, bf16[768,128]{1,0:T(8,128)(2,1)} %fusion.4.right_ref), custom_call_target="tpu_custom_call" | custom-call | bytes 5111808 | tf_op jit(solution)/shard_map/join/pallas_call | solution.py:87
  7.5 6.9 %all-to-all-start = ((bf16[16,48,1664]{2,1,0:T(8,128)(2,1)}), bf16[16,48,1664]{2,1,0:T(8,128)(2,1)S(1)}, u32[]{:S(2)}, u32[]{:S(2)}) async-start(bf16[16,48,1664]{2,1,0:T(8,128)(2,1)} %bitcast.46), calls=%async_computation | async-start | bytes 5111808 | tf_op jit(solution)/shard_map/all_to_all | solution.py:324
  14.9 2.3 %stack.2 = bf16[384,1536]{1,0:T(8,128)(2,1)} custom-call(s32[1]{0:T(128)} %bitcast.18.half_ref, bf16[384,1536]{1,0:T(8,128)(2,1)} %refs_2_.3, bf16[384,1536]{1,0:T(8,128)(2,1)} %refs_3_.3), custom_call_target="tpu_custom_call" | custom-call | bytes 2359296 | tf_op jit(solution)/shard_map/stack/pallas_call | solution.py:113
  17.2 2.6 %collective-permute-start.4 = (bf16[384,1536]{1,0:T(8,128)(2,1)}, bf16[384,1536]{1,0:T(8,128)(2,1)}, u32[]{:S(2)}, u32[]{:S(2)}) collective-permute-start(bf16[384,1536]{1,0:T(8,128)(2,1)} %stack.2), channel_id=1, source_target_pairs={{0,4},{1,13},{32,36},{33,45},{64,68},{65,77},{96,100},{97,109},{4,... | collective-permute-start | bytes 3538952 | tf_op jit(solution)/shard_map/ppermute | solution.py:39
  19.8 2.3 %stack.3 = bf16[384,1536]{1,0:T(8,128)(2,1)} custom-call(s32[1]{0:T(128)} %bitcast.18.half_ref, bf16[384,1536]{1,0:T(8,128)(2,1)} %collective-permute-done.6.refs_0_.refs_4_, bf16[384,1536]{1,0:T(8,128)(2,1)} %collective-permute-done.7.refs_1_.refs_5_), custom_call_target="tpu_custom_call" | custom-call | bytes 2359296 | tf_op jit(solution)/shard_map/stack/pallas_call | solution.py:113
  22.1 2.2 %collective-permute-start.8 = (bf16[384,1536]{1,0:T(8,128)(2,1)}, bf16[384,1536]{1,0:T(8,128)(2,1)}, u32[]{:S(2)}, u32[]{:S(2)}) collective-permute-start(bf16[384,1536]{1,0:T(8,128)(2,1)} %stack.3), channel_id=1, source_target_pairs={{0,4},{1,13},{32,36},{33,45},{64,68},{65,77},{96,100},{97,109},{4,... | collective-permute-start | bytes 3538952 | tf_op jit(solution)/shard_map/ppermute | solution.py:39
  24.3 33.1 %collective-permute-done.4.refs_6_ = bf16[384,1536]{1,0:T(8,128)(2,1)} collective-permute-done((bf16[384,1536]{1,0:T(8,128)(2,1)}, bf16[384,1536]{1,0:T(8,128)(2,1)}, u32[]{:S(2)}, u32[]{:S(2)}) %collective-permute-start.4) | collective-permute-done | bytes 1179680 | tf_op jit(solution)/shard_map/ppermute | solution.py:39
  57.4 1.6 collective-permute-start.16
  62.8 5.5 %collective-permute-start = (bf16[3,16,1536]{2,1,0:T(8,128)(2,1)S(1)}, bf16[3,16,1536]{2,1,0:T(8,128)(2,1)S(1)}, u32[]{:S(2)}, u32[]{:S(2)}) collective-permute-start(bf16[3,16,1536]{2,1,0:T(8,128)(2,1)S(1)} %bitcast.50), channel_id=1, source_target_pairs={{0,16},{16,32},{32,48},{48,64},{64,80},{80,96},{96,112},{1,17},{17... | collective-permute-start | bytes 442376 | tf_op jit(solution)/shard_map/ppermute | solution.py:68
  68.7 1.9 collective-permute-done.1.refs_2_
  71.9 2.8 %collective-permute-start.3 = (bf16[38,3,1536]{2,1,0:T(4,128)(2,1)S(1)}, bf16[38,3,1536]{2,1,0:T(4,128)(2,1)S(1)}, u32[]{:S(2)}, u32[]{:S(2)}) collective-permute-start(bf16[38,3,1536]{2,1,0:T(4,128)(2,1)S(1)} %pad_maximum_fusion.1), channel_id=1, source_target_pairs={{1,0},{2,1},{3,2},{4,3},{5,4},{6,5},{7,6},{8,7},{9,8},{10,9},{11,1... | collective-permute-start | bytes 1050632 | tf_op jit(solution)/shard_map/ppermute | solution.py:379
  75.0 3.0 %collective-permute-start.2 = (bf16[38,3,1536]{2,1,0:T(4,128)(2,1)S(1)}, bf16[38,3,1536]{2,1,0:T(4,128)(2,1)S(1)}, u32[]{:S(2)}, u32[]{:S(2)}) collective-permute-start(bf16[38,3,1536]{2,1,0:T(4,128)(2,1)S(1)} %pad_maximum_fusion), channel_id=1, source_target_pairs={{0,1},{1,2},{2,3},{3,4},{4,5},{5,6},{6,7},{7,8},{8,9},{9,10},{10,1... | collective-permute-start | bytes 1050632 | tf_op jit(solution)/shard_map/ppermute | solution.py:378
  78.0 7.5 %collective-permute-start.5 = (bf16[384,1536]{1,0:T(8,128)(2,1)}, bf16[384,1536]{1,0:T(8,128)(2,1)}, u32[]{:S(2)}, u32[]{:S(2)}) collective-permute-start(bf16[384,1536]{1,0:T(8,128)(2,1)} %collective-permute-done.4.refs_6_), channel_id=1, source_target_pairs={{0,32},{1,97},{32,64},{33,1},{64,96},{65,33},{96,0},{97,65},{4,36}... | collective-permute-start | bytes 3538952 | tf_op jit(solution)/shard_map/ppermute | solution.py:39
  85.6 5.7 %collective-permute-start.9 = (bf16[384,1536]{1,0:T(8,128)(2,1)}, bf16[384,1536]{1,0:T(8,128)(2,1)}, u32[]{:S(2)}, u32[]{:S(2)}) collective-permute-start(bf16[384,1536]{1,0:T(8,128)(2,1)} %collective-permute-done.8.refs_7_), channel_id=1, source_target_pairs={{0,32},{1,97},{32,64},{33,1},{64,96},{65,33},{96,0},{97,65},{4,36}... | collective-permute-start | bytes 3538952 | tf_op jit(solution)/shard_map/ppermute | solution.py:39
  91.4 1.9 reshape.247.refs_5_
  95.1 10.7 %conv.2.refs_9_ = f32[6,512,128]{2,1,0:T(8,128)} custom-call(bf16[32,16,1536]{2,1,0:T(8,128)(2,1)} %bitcast.44, bf16[3,16,1536]{2,1,0:T(8,128)(2,1)} %copy-done.5, bf16[3,16,1536]{2,1,0:T(8,128)(2,1)} %copy-done.4, bf16[38,3,1536]{2,1,0:T(4,128)(2,1)} %copy-done.3, bf16[38,3,1536]{2,1,0:T(4,128)(2,1)} %copy-done.2, f32[49,1536]{1,0:T(8,128)} %reshape.247.refs_5_, ...), custom_call_target="tpu_custom_call" | custom-call | flops 39321600 | bytes 3145728 | tf_op jit(solution)/shard_map/conv/pallas_call | solution.py:190
  105.8 17.9 %conv.3.refs_0_ = bf16[512,1536]{1,0:T(8,128)(2,1)} custom-call(bf16[32,16,1536]{2,1,0:T(8,128)(2,1)} %bitcast.45, bf16[3,16,1536]{2,1,0:T(8,128)(2,1)} %copy-done.5, bf16[3,16,1536]{2,1,0:T(8,128)(2,1)} %copy-done.4, bf16[38,3,1536]{2,1,0:T(4,128)(2,1)} %copy-done.3, bf16[38,3,1536]{2,1,0:T(4,128)(2,1)} %copy-done.2, f32[49,1536]{1,0:T(8,128)} %reshape.247.refs_5_, ...), custom_call_target="tpu_custom_call" | custom-call | flops 39321600 | bytes 3145728 | tf_op jit(solution)/shard_map/conv/pallas_call | solution.py:190
  123.7 2.6 %collective-permute-start.18 = (bf16[512,1536]{1,0:T(8,128)(2,1)}, bf16[512,1536]{1,0:T(8,128)(2,1)}, u32[]{:S(2)}, u32[]{:S(2)}) collective-permute-start(bf16[512,1536]{1,0:T(8,128)(2,1)} %conv.3.refs_0_), channel_id=1, source_target_pairs={{0,2},{1,19},{32,34},{33,51},{64,66},{65,83},{96,98},{97,115},{4,6... | collective-permute-start | bytes 4718600 | tf_op jit(solution)/shard_map/ppermute | solution.py:39
  129.4 15.1 %collective-permute-done.18.refs_0_ = bf16[512,1536]{1,0:T(8,128)(2,1)} collective-permute-done((bf16[512,1536]{1,0:T(8,128)(2,1)}, bf16[512,1536]{1,0:T(8,128)(2,1)}, u32[]{:S(2)}, u32[]{:S(2)}) %collective-permute-start.18) | collective-permute-done | bytes 1572896 | tf_op jit(solution)/shard_map/ppermute | solution.py:39
  144.6 12.1 %mlp.6.refs_10_ = f32[512,1536]{1,0:T(8,128)} custom-call(bf16[512,1536]{1,0:T(8,128)(2,1)} %collective-permute-done.18.refs_0_, f32[1,1536]{1,0:T(1,128)} %convert_element_type.70.refs_1_, bf16[384,1536]{1,0:T(8,128)(2,1)} %refs_2_.3, bf16[384,1536]{1,0:T(8,128)(2,1)} %refs_3_.3, bf16[384,1536]{1,0:T(8,128)(2,1)} %collective-permute-done.6.refs_0_.refs_4_, ...), custom_call_target="tpu_custom_call" | custom-call | flops 4831838208 | bytes 9437184 | tf_op jit(solution)/shard_map/mlp/pallas_call | solution.py:279
  158.1 12.7 %mlp.7 = bf16[512,1536]{1,0:T(8,128)(2,1)} custom-call(bf16[512,1536]{1,0:T(8,128)(2,1)} %collective-permute-done.18.refs_0_, f32[1,1536]{1,0:T(1,128)} %convert_element_type.69.refs_1_, bf16[384,1536]{1,0:T(8,128)(2,1)} %collective-permute-done.5.refs_2_, bf16[384,1536]{1,0:T(8,128)(2,1)} %collective-permute-done.9.refs_3_, bf16[384,1536]{1,0:T(8,128)(2,1)} %copy-done.12, ...), custom_call_target="tpu_custom_call" | custom-call | flops 4831838208 | bytes 9437184 | tf_op jit(solution)/shard_map/mlp/pallas_call | solution.py:279
  172.2 12.1 %mlp.4.refs_10_ = f32[512,1536]{1,0:T(8,128)} custom-call(bf16[512,1536]{1,0:T(8,128)(2,1)} %conv.3.refs_0_, f32[1,1536]{1,0:T(1,128)} %convert_element_type.70.refs_1_, bf16[384,1536]{1,0:T(8,128)(2,1)} %refs_2_.3, bf16[384,1536]{1,0:T(8,128)(2,1)} %refs_3_.3, bf16[384,1536]{1,0:T(8,128)(2,1)} %collective-permute-done.6.refs_0_.refs_4_, ...), custom_call_target="tpu_custom_call" | custom-call | flops 4831838208 | bytes 9437184 | tf_op jit(solution)/shard_map/mlp/pallas_call | solution.py:279
  184.4 13.3 %mlp.5 = f32[512,1536]{1,0:T(8,128)} custom-call(bf16[512,1536]{1,0:T(8,128)(2,1)} %conv.3.refs_0_, f32[1,1536]{1,0:T(1,128)} %convert_element_type.69.refs_1_, bf16[384,1536]{1,0:T(8,128)(2,1)} %collective-permute-done.5.refs_2_, bf16[384,1536]{1,0:T(8,128)(2,1)} %collective-permute-done.9.refs_3_, bf16[384,1536]{1,0:T(8,128)(2,1)} %copy-done.12, ...), custom_call_target="tpu_custom_call" | custom-call | flops 4831838208 | bytes 9437184 | tf_op jit(solution)/shard_map/mlp/pallas_call | solution.py:279
  197.8 4.2 %add_convert_fusion = bf16[512,1536]{1,0:T(8,128)(2,1)} fusion(f32[512,1536]{1,0:T(8,128)} %mlp.5, bf16[512,1536]{1,0:T(8,128)(2,1)} %collective-permute-done.19, bf16[512,1536]{1,0:T(8,128)(2,1)S(1)} %copy-done.1, f32[1536]{0:T(1024)S(1)} %copy-done.9, f32[1536]{0:T(1024)S(1)} %copy-done.10), kind=kLoop, calls=%fused_computation.1 | loop fusion | flops 5505024 | bytes 7876608 | tf_op jit(solution)/shard_map/convert_element_type | solution.py:393
  (90 shorter events, 16.6 us)
Async XLA Ops:
  7.5 52.1 %all-to-all-start = ((bf16[16,48,1664]{2,1,0:T(8,128)(2,1)}), bf16[16,48,1664]{2,1,0:T(8,128)(2,1)S(1)}, u32[]{:S(2)}, u32[]{:S(2)}) async-start(bf16[16,48,1664]{2,1,0:T(8,128)(2,1)} %bitcast.46), calls=%async_computation | async-start | bytes 5111808 | tf_op jit(solution)/shard_map/all_to_all | solution.py:324
  14.4 5.4 %collective-permute-start.6 = (bf16[384,1536]{1,0:T(8,128)(2,1)}, bf16[384,1536]{1,0:T(8,128)(2,1)}, u32[]{:S(2)}, u32[]{:S(2)}) collective-permute-start(bf16[384,1536]{1,0:T(8,128)(2,1)} %refs_2_.3), channel_id=1, source_target_pairs={{0,1},{1,0},{32,33},{33,32},{64,65},{65,64},{96,97},{97,96},{4,5},... | collective-permute-start | bytes 3538952 | tf_op jit(solution)/shard_map/ppermute | solution.py:39
  14.6 5.3 %collective-permute-start.7 = (bf16[384,1536]{1,0:T(8,128)(2,1)}, bf16[384,1536]{1,0:T(8,128)(2,1)}, u32[]{:S(2)}, u32[]{:S(2)}) collective-permute-start(bf16[384,1536]{1,0:T(8,128)(2,1)} %refs_3_.3), channel_id=1, source_target_pairs={{0,1},{1,0},{32,33},{33,32},{64,65},{65,64},{96,97},{97,96},{4,5},... | collective-permute-start | bytes 3538952 | tf_op jit(solution)/shard_map/ppermute | solution.py:39
  17.2 42.9 %copy-start.13 = (bf16[1536]{0:T(1024)(128)(2,1)S(1)}, bf16[1536]{0:T(1024)(128)(2,1)}, u32[]{:S(2)}) copy-start(bf16[1536]{0:T(1024)(128)(2,1)} %param.14) | copy-start | bytes 9220
  17.2 40.2 %collective-permute-start.4 = (bf16[384,1536]{1,0:T(8,128)(2,1)}, bf16[384,1536]{1,0:T(8,128)(2,1)}, u32[]{:S(2)}, u32[]{:S(2)}) collective-permute-start(bf16[384,1536]{1,0:T(8,128)(2,1)} %stack.2), channel_id=1, source_target_pairs={{0,4},{1,13},{32,36},{33,45},{64,68},{65,77},{96,100},{97,109},{4,... | collective-permute-start | bytes 3538952 | tf_op jit(solution)/shard_map/ppermute | solution.py:39
  22.1 55.9 %collective-permute-start.8 = (bf16[384,1536]{1,0:T(8,128)(2,1)}, bf16[384,1536]{1,0:T(8,128)(2,1)}, u32[]{:S(2)}, u32[]{:S(2)}) collective-permute-start(bf16[384,1536]{1,0:T(8,128)(2,1)} %stack.3), channel_id=1, source_target_pairs={{0,4},{1,13},{32,36},{33,45},{64,68},{65,77},{96,100},{97,109},{4,... | collective-permute-start | bytes 3538952 | tf_op jit(solution)/shard_map/ppermute | solution.py:39
  57.4 66.3 %collective-permute-start.16 = (bf16[384,1536]{1,0:T(8,128)(2,1)}, bf16[384,1536]{1,0:T(8,128)(2,1)}, u32[]{:S(2)}, u32[]{:S(2)}) collective-permute-start(bf16[384,1536]{1,0:T(8,128)(2,1)} %collective-permute-done.4.refs_6_), channel_id=1, source_target_pairs={{0,1},{1,0},{32,33},{33,32},{64,65},{65,64},{96,97},{97,96},{4,5},... | collective-permute-start | bytes 3538952 | tf_op jit(solution)/shard_map/ppermute | solution.py:39
  58.9 26.6 %collective-permute-start.12 = (bf16[384,1536]{1,0:T(8,128)(2,1)}, bf16[384,1536]{1,0:T(8,128)(2,1)}, u32[]{:S(2)}, u32[]{:S(2)}) collective-permute-start(bf16[384,1536]{1,0:T(8,128)(2,1)} %collective-permute-done.4.refs_6_), channel_id=1, source_target_pairs={{0,4},{1,13},{32,36},{33,45},{64,68},{65,77},{96,100},{97,109},{4,... | collective-permute-start | bytes 3538952 | tf_op jit(solution)/shard_map/ppermute | solution.py:39
  61.5 9.1 %collective-permute-start.1 = (bf16[3,16,1536]{2,1,0:T(8,128)(2,1)S(1)}, bf16[3,16,1536]{2,1,0:T(8,128)(2,1)S(1)}, u32[]{:S(2)}, u32[]{:S(2)}) collective-permute-start(bf16[3,16,1536]{2,1,0:T(8,128)(2,1)S(1)} %bitcast.51), channel_id=1, source_target_pairs={{16,0},{32,16},{48,32},{64,48},{80,64},{96,80},{112,96},{17,1},{33... | collective-permute-start | bytes 442376 | tf_op jit(solution)/shard_map/ppermute | solution.py:69
  62.8 8.7 %collective-permute-start = (bf16[3,16,1536]{2,1,0:T(8,128)(2,1)S(1)}, bf16[3,16,1536]{2,1,0:T(8,128)(2,1)S(1)}, u32[]{:S(2)}, u32[]{:S(2)}) collective-permute-start(bf16[3,16,1536]{2,1,0:T(8,128)(2,1)S(1)} %bitcast.50), channel_id=1, source_target_pairs={{0,16},{16,32},{32,48},{48,64},{64,80},{80,96},{96,112},{1,17},{17... | collective-permute-start | bytes 442376 | tf_op jit(solution)/shard_map/ppermute | solution.py:68
  68.6 25.2 %copy-start.7 = (f32[1536]{0:T(1024)S(1)}, f32[1536]{0:T(1024)}, u32[]{:S(2)}) copy-start(f32[1536]{0:T(1024)} %param.17) | copy-start | bytes 18436
  68.7 25.8 %copy-start.8 = (f32[1536]{0:T(1024)S(1)}, f32[1536]{0:T(1024)}, u32[]{:S(2)}) copy-start(f32[1536]{0:T(1024)} %param.18) | copy-start | bytes 18436
  71.9 13.7 %collective-permute-start.3 = (bf16[38,3,1536]{2,1,0:T(4,128)(2,1)S(1)}, bf16[38,3,1536]{2,1,0:T(4,128)(2,1)S(1)}, u32[]{:S(2)}, u32[]{:S(2)}) collective-permute-start(bf16[38,3,1536]{2,1,0:T(4,128)(2,1)S(1)} %pad_maximum_fusion.1), channel_id=1, source_target_pairs={{1,0},{2,1},{3,2},{4,3},{5,4},{6,5},{7,6},{8,7},{9,8},{10,9},{11,1... | collective-permute-start | bytes 1050632 | tf_op jit(solution)/shard_map/ppermute | solution.py:379
  75.0 16.3 %collective-permute-start.2 = (bf16[38,3,1536]{2,1,0:T(4,128)(2,1)S(1)}, bf16[38,3,1536]{2,1,0:T(4,128)(2,1)S(1)}, u32[]{:S(2)}, u32[]{:S(2)}) collective-permute-start(bf16[38,3,1536]{2,1,0:T(4,128)(2,1)S(1)} %pad_maximum_fusion), channel_id=1, source_target_pairs={{0,1},{1,2},{2,3},{3,4},{4,5},{5,6},{6,7},{7,8},{8,9},{9,10},{10,1... | collective-permute-start | bytes 1050632 | tf_op jit(solution)/shard_map/ppermute | solution.py:378
  78.0 48.7 %collective-permute-start.5 = (bf16[384,1536]{1,0:T(8,128)(2,1)}, bf16[384,1536]{1,0:T(8,128)(2,1)}, u32[]{:S(2)}, u32[]{:S(2)}) collective-permute-start(bf16[384,1536]{1,0:T(8,128)(2,1)} %collective-permute-done.4.refs_6_), channel_id=1, source_target_pairs={{0,32},{1,97},{32,64},{33,1},{64,96},{65,33},{96,0},{97,65},{4,36}... | collective-permute-start | bytes 3538952 | tf_op jit(solution)/shard_map/ppermute | solution.py:39
  85.5 41.3 %collective-permute-start.17 = (bf16[384,1536]{1,0:T(8,128)(2,1)}, bf16[384,1536]{1,0:T(8,128)(2,1)}, u32[]{:S(2)}, u32[]{:S(2)}) collective-permute-start(bf16[384,1536]{1,0:T(8,128)(2,1)} %collective-permute-done.8.refs_7_), channel_id=1, source_target_pairs={{0,1},{1,0},{32,33},{33,32},{64,65},{65,64},{96,97},{97,96},{4,5},... | collective-permute-start | bytes 3538952 | tf_op jit(solution)/shard_map/ppermute | solution.py:39
  85.6 41.8 %collective-permute-start.9 = (bf16[384,1536]{1,0:T(8,128)(2,1)}, bf16[384,1536]{1,0:T(8,128)(2,1)}, u32[]{:S(2)}, u32[]{:S(2)}) collective-permute-start(bf16[384,1536]{1,0:T(8,128)(2,1)} %collective-permute-done.8.refs_7_), channel_id=1, source_target_pairs={{0,32},{1,97},{32,64},{33,1},{64,96},{65,33},{96,0},{97,65},{4,36}... | collective-permute-start | bytes 3538952 | tf_op jit(solution)/shard_map/ppermute | solution.py:39
  91.3 36.2 %collective-permute-start.14 = (bf16[384,1536]{1,0:T(8,128)(2,1)}, bf16[384,1536]{1,0:T(8,128)(2,1)}, u32[]{:S(2)}, u32[]{:S(2)}) collective-permute-start(bf16[384,1536]{1,0:T(8,128)(2,1)} %collective-permute-done.12.refs_6_), channel_id=1, source_target_pairs={{0,32},{1,97},{32,64},{33,1},{64,96},{65,33},{96,0},{97,65},{4,36}... | collective-permute-start | bytes 3538952 | tf_op jit(solution)/shard_map/ppermute | solution.py:39
  123.7 20.9 %collective-permute-start.18 = (bf16[512,1536]{1,0:T(8,128)(2,1)}, bf16[512,1536]{1,0:T(8,128)(2,1)}, u32[]{:S(2)}, u32[]{:S(2)}) collective-permute-start(bf16[512,1536]{1,0:T(8,128)(2,1)} %conv.3.refs_0_), channel_id=1, source_target_pairs={{0,2},{1,19},{32,34},{33,51},{64,66},{65,83},{96,98},{97,115},{4,6... | collective-permute-start | bytes 4718600 | tf_op jit(solution)/shard_map/ppermute | solution.py:39
  126.8 29.9 %collective-permute-start.13 = (bf16[384,1536]{1,0:T(8,128)(2,1)}, bf16[384,1536]{1,0:T(8,128)(2,1)S(1)}, u32[]{:S(2)}, u32[]{:S(2)}) collective-permute-start(bf16[384,1536]{1,0:T(8,128)(2,1)} %collective-permute-done.12.refs_6_), channel_id=1, source_target_pairs={{0,1},{1,0},{32,33},{33,32},{64,65},{65,64},{96,97},{97,96},{4,5},... | collective-permute-start | bytes 3538952 | tf_op jit(solution)/shard_map/ppermute | solution.py:39
  126.9 29.8 %collective-permute-start.10 = (bf16[384,1536]{1,0:T(8,128)(2,1)}, bf16[384,1536]{1,0:T(8,128)(2,1)S(1)}, u32[]{:S(2)}, u32[]{:S(2)}) collective-permute-start(bf16[384,1536]{1,0:T(8,128)(2,1)} %collective-permute-done.5.refs_2_), channel_id=1, source_target_pairs={{0,1},{1,0},{32,33},{33,32},{64,65},{65,64},{96,97},{97,96},{4,5},... | collective-permute-start | bytes 3538952 | tf_op jit(solution)/shard_map/ppermute | solution.py:39
  127.4 29.4 %collective-permute-start.11 = (bf16[384,1536]{1,0:T(8,128)(2,1)}, bf16[384,1536]{1,0:T(8,128)(2,1)}, u32[]{:S(2)}, u32[]{:S(2)}) collective-permute-start(bf16[384,1536]{1,0:T(8,128)(2,1)} %collective-permute-done.9.refs_3_), channel_id=1, source_target_pairs={{0,1},{1,0},{32,33},{33,32},{64,65},{65,64},{96,97},{97,96},{4,5},... | collective-permute-start | bytes 3538952 | tf_op jit(solution)/shard_map/ppermute | solution.py:39
  127.5 29.3 %collective-permute-start.15 = (bf16[384,1536]{1,0:T(8,128)(2,1)}, bf16[384,1536]{1,0:T(8,128)(2,1)}, u32[]{:S(2)}, u32[]{:S(2)}) collective-permute-start(bf16[384,1536]{1,0:T(8,128)(2,1)} %collective-permute-done.14.refs_8_), channel_id=1, source_target_pairs={{0,1},{1,0},{32,33},{33,32},{64,65},{65,64},{96,97},{97,96},{4,5},... | collective-permute-start | bytes 3538952 | tf_op jit(solution)/shard_map/ppermute | solution.py:39
  170.8 26.9 %collective-permute-start.19 = (bf16[512,1536]{1,0:T(8,128)(2,1)}, bf16[512,1536]{1,0:T(8,128)(2,1)}, u32[]{:S(2)}, u32[]{:S(2)}) collective-permute-start(bf16[512,1536]{1,0:T(8,128)(2,1)} %mlp.7), channel_id=1, source_target_pairs={{0,18},{1,3},{32,50},{33,35},{64,82},{65,67},{96,114},{97,99},{4,2... | collective-permute-start | bytes 4718600 | tf_op jit(solution)/shard_map/ppermute | solution.py:39
  (11 other events, 131.4 us)
where the time goes:
time: 203 us; the launch traced here: 202 us
  Pallas kernels  88.3 us (43%)
  waiting for transfers between devices  51 us (25%)
  starting transfers between devices  45.5 us (22%)
  other arithmetic  8.3 us (4%)
  local copies, waits for them, and re-layouts  7.07 us (3%)
    pallas_call x4, Pallas kernels, mlp(): pl.pallas_call(functools.partial(mlp_kernel, plan, len(pieces), int(adds)...  50.2 us
    ppermute x16, waiting for transfers between devices, send(): return lax.ppermute(value, ('row', 'col'), routes(move))  48.3 us
    pallas_call x2, Pallas kernels, conv_call(): pl.pallas_call(functools.partial(conv_kernel, first, count, ends is not N...  28.6 us
    ppermute x16, starting transfers between devices, send(): return lax.ppermute(value, ('row', 'col'), routes(move))  25.9 us
    all_to_all x1, starting transfers between devices, local(): lax.all_to_all(join(patches, extra), 'col', split_axis=0, concat_axis=0,...  6.9 us
    ppermute x1, starting transfers between devices, halo(): lax.ppermute(tail, axis, [(i, i + 1) for i in range(ends)])  5.5 us
    pallas_call x1, Pallas kernels, join(): pl.pallas_call(join_kernel, out_shape=jax.ShapeDtypeStruct((rows, a + b),...  4.98 us
    pallas_call x2, Pallas kernels, stack(): pl.pallas_call(stack_kernel, out_shape=jax.ShapeDtypeStruct((len(sources)...  4.53 us
  transfers between devices with their start and end apart: 21, of which 4 were waited for; matrix products, arithmetic and copies ran while one was open for 4% of the time, Pallas kernels for 35%

commit v1 on v0

v1 whole, which is shorter than its diff:
```python
import functools

import jax
import jax.numpy as jnp
from jax import lax
from jax.experimental import pallas as pl
from jax.experimental.pallas import tpu as pltpu
from jax.sharding import PartitionSpec as P


TH = 32
TW = 16
SHARD = 384
HALF = SHARD // 2
LANES = 128
BAND = TH // 2
PAIRS = BAND // 2
UNITS = 256

VMEM = pltpu.VMEM


def device_index(x, y, z, core):
    x, y, z = x % 4, y % 4, z % 4
    return (z * 2 + x // 2) * 16 + y * 4 + (x % 2) * 2 + core


def routes(move):
    return [
        (device_index(x, y, z, core), device_index(*move(x, y, z, core)))
        for x in range(4)
        for y in range(4)
        for z in range(4)
        for core in range(2)
    ]


def send(value, move):
    return lax.ppermute(value, ("row", "col"), routes(move))


def to_partner(x, y, z, core):
    return x, y, z, 1 - core


def along_y(x, y, z, core):
    return x, y + 1 - 2 * core, z, core


def along_z(x, y, z, core):
    return x, y, z + 1 - 2 * core, core


def along_x(x, y, z, core):
    return x + 1 - 2 * core, y, z, core


def back_x(x, y, z, core):
    return x - 1 + 2 * core, y, z, core


def halo(cells, axis, dim, width):
    count = lax.axis_size(axis)
    ends = count - 1
    head = lax.slice_in_dim(cells, 0, width, axis=dim)
    tail = lax.slice_in_dim(cells, cells.shape[dim] - width, cells.shape[dim], axis=dim)
    return (
        lax.ppermute(tail, axis, [(i, i + 1) for i in range(ends)]),
        lax.ppermute(head, axis, [(i + 1, i) for i in range(ends)]),
    )


def whole(space=VMEM):
    return pl.BlockSpec(memory_space=space)


def stack_kernel(half_ref, *refs):
    *sources, out_ref, sems = refs
    start = pl.multiple_of(half_ref[0] * HALF, HALF)
    copies = [
        pltpu.make_async_copy(source.at[pl.ds(start, HALF)], out_ref.at[pl.ds(k * HALF, HALF)], sems.at[k])
        for k, source in enumerate(sources)
    ]
    for copy in copies:
        copy.start()
    for copy in copies:
        copy.wait()


def stack(half, *sources):
    channels = sources[0].shape[1]
    return pl.pallas_call(
        stack_kernel,
        out_shape=jax.ShapeDtypeStruct((len(sources) * HALF, channels), jnp.bfloat16),
        in_specs=[whole(pltpu.SMEM)] + [whole(pl.ANY)] * len(sources),
        out_specs=whole(),
        scratch_shapes=[pltpu.SemaphoreType.DMA((len(sources),))],
        cost_estimate=pl.CostEstimate(flops=0, bytes_accessed=4 * len(sources) * HALF * channels, transcendentals=0),
        name="stack",
    )(half, *sources)


def conv_kernel(lower, grid_ref, edge_ref, left_ref, right_ref, weight_ref, vector_ref, out_ref, even, odd, both, conv):
    channels = grid_ref.shape[2]
    tiles = channels // LANES
    count = PAIRS + 3

    def tile(t, carry):
        at = pl.ds(pl.multiple_of(t * LANES, LANES), LANES)

        def row(k):
            if lower:
                inside = k < BAND + 3
                middle = grid_ref[TH - BAND - 3 + k, :, at] if inside else edge_ref[k - BAND - 3, :, at]
                side = TH - BAND + k
            else:
                middle = edge_ref[k, :, at] if k < 3 else grid_ref[k - 3, :, at]
                side = k
            parts = (left_ref[side, :, at], middle, right_ref[side, :, at])
            return [part.astype(jnp.float32) for part in parts]

        spans = (slice(5, 8), slice(8, 24), slice(24, 27))
        for k in range(count):
            for span, e, o in zip(spans, row(2 * k), row(2 * k + 1)):
                even[k, span, :] = e
                odd[k, span, :] = o
                both[k, span, :] = e + o
        zero = jnp.zeros((TW, LANES), jnp.float32)
        p, q, s = [zero] * PAIRS, [zero] * (PAIRS + 1), [zero] * PAIRS
        for along in range(7):
            h = [weight_ref[across, along : along + 1, at] for across in range(7)]
            mixed = [h[0]] + [h[2 * j] + h[2 * j - 1] for j in range(1, 4)]
            h, mixed = [[jnp.broadcast_to(v, (TW, LANES)) for v in group] for group in (h, mixed)]
            cols = slice(5 + along, 5 + along + TW)
            for k in range(count):
                e, o, b = even[k, cols, :], odd[k, cols, :], both[k, cols, :]
                for j in range(4):
                    if 0 <= k - j < PAIRS:
                        p[k - j] = p[k - j] + e * h[2 * j]
                        s[k - j] = s[k - j] + b * mixed[j]
                for j in range(3):
                    if 0 <= k - j <= PAIRS:
                        q[k - j] = q[k - j] + o * h[2 * j + 1]
        base = jnp.broadcast_to(vector_ref[0:1, at], (TW, LANES))
        for k in range(PAIRS):
            conv[t, 2 * k * TW : (2 * k + 1) * TW, :] = p[k] + q[k] + base
            conv[t, (2 * k + 1) * TW : (2 * k + 2) * TW, :] = s[k] - p[k] - q[k + 1] + base
        return carry

    lax.fori_loop(0, tiles, tile, 0)

    def norm(b, carry):
        rows = pl.ds(pl.multiple_of(b * 16, 16), 16)
        values = [conv[t, rows, :] for t in range(tiles)]
        mean = jnp.sum(sum(values), axis=-1, keepdims=True) * (1.0 / channels)
        centred = [v - mean for v in values]
        var = jnp.sum(sum(v * v for v in centred), axis=-1, keepdims=True) * (1.0 / channels)
        inverse = lax.rsqrt(var + 1e-06)
        for t in range(tiles):
            at = slice(t * LANES, (t + 1) * LANES)
            out_ref[rows, at] = (centred[t] * inverse * vector_ref[1:2, at] + vector_ref[2:3, at]).astype(
                jnp.bfloat16
            )
        return carry

    lax.fori_loop(0, BAND * TW // 16, norm, 0, unroll=2)


def conv_norm(lower, grid, edge, left, right, weight, vectors):
    channels = grid.shape[2]
    stage = VMEM((PAIRS + 3, 32, LANES), jnp.float32)
    return pl.pallas_call(
        functools.partial(conv_kernel, lower),
        out_shape=jax.ShapeDtypeStruct((BAND * TW, channels), jnp.bfloat16),
        in_specs=[whole()] * 6,
        out_specs=whole(),
        scratch_shapes=[stage, stage, stage, VMEM((channels // LANES, BAND * TW, LANES), jnp.float32)],
        cost_estimate=pl.CostEstimate(
            flops=100 * BAND * TW * channels, bytes_accessed=8 * BAND * TW * channels, transcendentals=0
        ),
        name="conv",
    )(grid, edge, left, right, weight, vectors)


PHI = (
    0.7978849411010742, 0.03633308410644531, -3.259496588725597e-05, -5.5306198191829026e-05,
    3.964745246776147e-06, -1.3226342332472996e-07, 1.7561730958348676e-09,
)


def gelu(pre):
    s = pre * pre
    p = PHI[-1]
    for c in PHI[-2::-1]:
        p = p * s + c
    half = 0.5 * pre
    return half + half * jnp.tanh(pre * p)


def mlp_kernel(plan, bands, count, adds, *refs):
    rows_refs, bias_ref = refs[:bands], refs[bands]
    pieces = refs[bands + 1 : bands + 1 + count]
    acc_ref = refs[bands + 1 + count] if adds else None
    out_ref, rows, w_in, w_out, hid, part, sems, row_sems = refs[bands + 1 + count + adds :]
    blocks = w_in.shape[0] // UNITS
    columns = w_out.shape[1] // UNITS
    ins, outs, at = [], [], 0
    for k, (a, row_a, b, row_b, size) in enumerate(plan):
        ins.append(pltpu.make_async_copy(pieces[a].at[pl.ds(row_a, size)], w_in.at[pl.ds(at, size)], sems.at[k, 0]))
        outs.append(pltpu.make_async_copy(pieces[b].at[pl.ds(row_b, size)], w_out.at[pl.ds(at, size)], sems.at[k, 1]))
        at += size
    step = rows.shape[0] // bands
    moves = [
        pltpu.make_async_copy(ref, rows.at[pl.ds(k * step, step)], row_sems.at[k]) for k, ref in enumerate(rows_refs)
    ]
    early = next(k for k in range(len(plan) + 1) if sum(p[4] for p in plan[:k]) >= 3 * UNITS)
    for copy in moves + ins + outs:
        copy.start()
    for copy in moves + ins[:early]:
        copy.wait()

    def first(h):
        return lax.dot_general(
            rows[...], w_in[h * UNITS : (h + 1) * UNITS, :], (((1,), (1,)), ((), ())),
            preferred_element_type=jnp.float32,
        )

    def middle(h, pre):
        at = slice(h * UNITS, (h + 1) * UNITS)
        hid[:, at] = gelu(pre + bias_ref[0:1, at]).astype(jnp.bfloat16)

    split = blocks // 2 * UNITS

    def second(n, last):
        at = slice(n * UNITS, (n + 1) * UNITS)
        span = slice(split, None) if last else slice(0, split)
        total = jnp.dot(hid[:, span], w_out[span, at], preferred_element_type=jnp.float32)
        if last:
            out_ref[:, at] = (part[:, at] + total).astype(out_ref.dtype)
        else:
            part[:, at] = total + acc_ref[:, at] if adds else total

    waiting, sent = None, 0
    for h in range(blocks):
        if h == blocks // 2:
            for copy in ins[early:] + outs:
                copy.wait()
        pre = first(h)
        if waiting is not None:
            middle(*waiting)
        waiting = (h, pre)
        if h > blocks // 2:
            for n in range(sent, sent + 2):
                second(n, False)
            sent += 2
    middle(*waiting)
    for n in range(sent, columns):
        second(n, False)
    for n in range(columns):
        second(n, True)


def mlp(rows, bias, pieces, plan, acc=None, out_dtype=jnp.float32):
    m, channels = sum(part.shape[0] for part in rows), rows[0].shape[1]
    hidden = sum(p[4] for p in plan)
    adds = acc is not None
    return pl.pallas_call(
        functools.partial(mlp_kernel, plan, len(rows), len(pieces), int(adds)),
        out_shape=jax.ShapeDtypeStruct((m, channels), out_dtype),
        in_specs=[whole(pl.ANY)] * len(rows) + [whole()] + [whole(pl.ANY)] * len(pieces) + [whole()] * adds,
        out_specs=whole(),
        scratch_shapes=[
            VMEM((m, channels), jnp.bfloat16),
            VMEM((hidden, channels), jnp.bfloat16),
            VMEM((hidden, channels), jnp.bfloat16),
            VMEM((m, hidden), jnp.bfloat16),
            VMEM((m, channels), jnp.float32),
            pltpu.SemaphoreType.DMA((len(plan), 2)),
            pltpu.SemaphoreType.DMA((len(rows),)),
        ],
        cost_estimate=pl.CostEstimate(
            flops=4 * m * hidden * channels, bytes_accessed=4 * hidden * channels, transcendentals=m * hidden
        ),
        name="mlp",
    )(*rows, bias.reshape(1, hidden), *pieces, *([acc] if adds else []))


def local(
    patches,
    dest,
    background,
    conv_weight,
    conv_bias,
    norm_gain,
    norm_bias,
    w_in,
    b_in,
    w_out,
    b_out,
    layer_scale,
):
    cells = TH * TW
    channels = patches.shape[1]
    row, col = lax.axis_index("row"), lax.axis_index("col")
    my_y, my_lo, my_core, my_h = col // 4, (col // 2) % 2, col % 2, (row // 2) % 2

    moved = lax.all_to_all(patches, "col", split_axis=0, concat_axis=0, tiled=True)
    slots = dest.reshape(16, 48)
    notes = jnp.concatenate(
        [slots >> 4, slots & 15, jnp.zeros((16, 32), jnp.int32)], axis=1
    ).astype(jnp.bfloat16)
    notes = jnp.concatenate([notes, jnp.broadcast_to(b_in, (16, SHARD))], axis=1)
    notes = lax.all_to_all(notes, "col", split_axis=0, concat_axis=0, tiled=True)

    w_in_p, w_out_p = send(w_in, to_partner), send(w_out, to_partner)
    half = my_h.astype(jnp.int32).reshape(1)
    near_a = send(stack(half, w_in, w_out), along_y)
    near_b = send(stack(half, w_in_p, w_out_p), along_y)
    near_a_z = send(near_a, along_z)
    far = send(near_a, along_y)
    near_a_p = send(near_a, to_partner)
    near_b_z = send(near_b, along_z)
    near_b_p = send(near_b, to_partner)
    far_z = send(far, along_z)
    far_p = send(far, to_partner)
    near_a_zp = send(near_a_z, to_partner)
    near_b_zp = send(near_b_z, to_partner)
    far_zp = send(far_z, to_partner)

    bias = notes[:, 128:].reshape(4, 2, 2, 2, HALF)
    bias = lax.dynamic_index_in_dim(bias, my_lo, axis=1, keepdims=False)
    bias = jnp.where(my_core == 1, bias[:, ::-1], bias)
    turned = jnp.where(my_h == 1, bias[:, :, ::-1], bias)
    ahead = 2 * my_core - 1

    def at(array, step):
        return lax.dynamic_index_in_dim(array, (my_y + step + 4) % 4, axis=0, keepdims=False)

    b_one, b_two, b_far = at(turned, ahead), at(turned, -ahead), at(turned, 2)
    b0 = at(bias, 0).reshape(-1)
    b1 = jnp.concatenate([b_one[0, 0], b_one[1, 0], b_two[1, 0], b_two[0, 0]])
    b2 = jnp.concatenate([b_one[0, 1], b_one[1, 1], b_two[1, 1], b_two[0, 1]])
    b3 = jnp.concatenate([b_far[0, 0], b_far[1, 0], b_far[0, 1], b_far[1, 1]])
    early = (w_in, w_out, w_in_p, w_out_p, near_a, near_b, near_a_p, near_b_p)
    early_plan = ((0, 0, 1, 0, SHARD), (2, 0, 3, 0, SHARD)) + tuple((a, 0, a, HALF, HALF) for a in range(4, 8))
    early_bias = jnp.concatenate([b0, b1]).astype(jnp.float32)
    late = (near_a_z, near_b_z, near_a_zp, near_b_zp, far, far_p, far_z, far_zp)
    late_plan = tuple((a, 0, a, HALF, HALF) for a in range(8))
    late_bias = jnp.concatenate([b2, b3]).astype(jnp.float32)

    where = (notes[:, :48].astype(jnp.int32) << 4) + notes[:, 48:96].astype(jnp.int32)
    where = where.reshape(-1)
    vectors = jnp.stack([conv_bias, norm_gain, norm_bias])
    moved, where, vectors, early_bias, late_bias = lax.optimization_barrier(
        (moved, where, vectors, early_bias, late_bias)
    )
    onehot = where[None, :] == jnp.arange(cells, dtype=jnp.int32)[:, None]
    placed = jnp.dot(
        onehot.astype(jnp.bfloat16), moved, preferred_element_type=jnp.float32
    )
    present = jnp.any(onehot, axis=1)
    grid = jnp.where(present[:, None], placed, background.astype(jnp.float32)[None, :]).astype(
        jnp.bfloat16
    )
    block = grid.reshape(TH, TW, channels)
    top, bottom = halo(block, "row", 0, 3)
    tall = [
        jnp.concatenate([part[:, cut] for part in (top, block, bottom)], axis=0)
        for cut in (slice(TW - 3, TW), slice(0, 3))
    ]
    ends = lax.axis_size("col") - 1
    left = lax.ppermute(tall[0], "col", [(i, i + 1) for i in range(ends)])
    right = lax.ppermute(tall[1], "col", [(i + 1, i) for i in range(ends)])
    flat_a = conv_norm(False, block, top, left, right, conv_weight, vectors)
    flat_b = conv_norm(True, block, bottom, left, right, conv_weight, vectors)

    flat = (flat_a, flat_b)
    other = (send(flat_a, along_x), send(flat_b, along_x))
    mine = mlp(flat, early_bias, early, early_plan)
    theirs = mlp(other, early_bias, early, early_plan)
    theirs = mlp(other, late_bias, late, late_plan, acc=theirs, out_dtype=jnp.bfloat16)
    returned = send(theirs, back_x)
    mine = mlp(flat, late_bias, late, late_plan, acc=mine)
    mixed = mine + returned.astype(jnp.float32)
    result = grid.astype(jnp.float32) + layer_scale * (mixed + b_out)
    return result.astype(jnp.bfloat16).reshape(TH, TW, channels)


def solution(mesh):
    placed = (
        P(("row", "col"), None),
        P(("row", "col")),
        P(),
        P(),
        P(),
        P(),
        P(),
        P("col", None),
        P("col"),
        P("col", None),
        P(),
        P(),
    )

    def step(*args):
        return local(*args)

    step = jax.shard_map(
        step, mesh=mesh, in_specs=placed, out_specs=P("row", "col", None), check_vma=False
    )
    return step
```

time: 203 us -> 208 us (1.025)
  local copies, waits for them, and re-layouts: 7.07 us -> 30 us
  waiting for transfers between devices: 51 us -> 28.7 us
  blocking collectives: 0 us -> 12.5 us
  starting transfers between devices: 45.5 us -> 36.7 us
  Pallas kernels: 88.3 us -> 83.6 us
  other arithmetic: 8.3 us -> 12 us
    ppermute x16 -> x17, waiting for transfers between devices: 48.3 us -> 11.4 us  [send(): return lax.ppermute(value, ('row', 'col'), routes(move))]
    all_to_all x0 -> x1, blocking collectives: none -> 12.5 us  [local(): lax.all_to_all(notes, 'col', split_axis=0, concat_axis=0, tiled=True)]
    concatenate x2 -> x1, local copies, waits for them, and re-layouts: 0.1 us -> 5.81 us  [local(): late_bias = jnp.concatenate([b2, b3]).astype(jnp.float32)]
    ppermute x1, waiting for transfers between devices: 0.01 us -> 5.49 us  [local(): left = lax.ppermute(tall[0], 'col', [(i, i + 1) for i in range(ends)])]
    ppermute x1, waiting for transfers between devices: 1.9 us -> 7.01 us  [halo(): lax.ppermute(head, axis, [(i + 1, i) for i in range(ends)])]
    pallas_call x7 -> x6, Pallas kernels: 83.8 us -> 78.9 us  [the longest x4 60.4 us: mlp(): pl.pallas_call(functools.partial(mlp_kernel, plan, len(rows), len(pieces)...]
    another operation x0 -> x3, local copies, waits for them, and re-layouts: none -> 3.87 us  [local(): vectors = jnp.stack([conv_bias, norm_gain, norm_bias])]
    concatenate x4 -> x1, local copies, waits for them, and re-layouts: 0.2 us -> 3.99 us  [local(): early_bias = jnp.concatenate([b0, b1]).astype(jnp.float32)]
  transfers between devices with their start and end apart: 21 -> 22, of which waited for: 4 -> 6; matrix products, arithmetic and copies ran while one was open for 4% -> 16% of each run, Pallas kernels for 35% -> 33%
where the time goes in v1:
time: 208 us; the launch traced here: 205 us
  Pallas kernels  83.6 us (40%)
  starting transfers between devices  36.7 us (18%)
  local copies, waits for them, and re-layouts  30 us (14%)
  waiting for transfers between devices  28.7 us (14%)
  blocking collectives  12.5 us (6%)
  other arithmetic  12 us (6%)
    pallas_call x4, Pallas kernels, mlp(): pl.pallas_call(functools.partial(mlp_kernel, plan, len(rows), len(pieces)...  60.4 us
    ppermute x17, starting transfers between devices, send(): return lax.ppermute(value, ('row', 'col'), routes(move))  23.2 us
    pallas_call x2, Pallas kernels, conv_norm(): pl.pallas_call(functools.partial(conv_kernel, lower), out_shape=jax.Shape...  18.5 us
    all_to_all x1, blocking collectives, local(): lax.all_to_all(notes, 'col', split_axis=0, concat_axis=0, tiled=True)  12.5 us
    ppermute x17, waiting for transfers between devices, send(): return lax.ppermute(value, ('row', 'col'), routes(move))  11.4 us
    ppermute x1, waiting for transfers between devices, halo(): lax.ppermute(head, axis, [(i + 1, i) for i in range(ends)])  7.01 us
    concatenate x1, local copies, waits for them, and re-layouts, local(): late_bias = jnp.concatenate([b2, b3]).astype(jnp.float32)  5.81 us
    ppermute x1, waiting for transfers between devices, local(): left = lax.ppermute(tall[0], 'col', [(i, i + 1) for i in range(ends)])  5.49 us
  transfers between devices with their start and end apart: 22, of which 6 were waited for; matrix products, arithmetic and copies ran while one was open for 16% of the time, Pallas kernels for 33%

profile of v1, /device:TPU:1, one launch (start us, length us, event | category | flops | bytes accessed | tf_op | source)
XLA Modules:
  0.0 205.3 jit_solution(8303827461869310301)
XLA Ops:
  2.9 12.5 %all_to_all.24 = bf16[16,2,256]{2,1,0:T(2,128)(2,1)S(1)} all-to-all(bf16[16,2,256]{2,1,0:T(2,128)(2,1)S(1)} %reshape.66), channel_id=1, replica_groups=mesh['row'=8,'col'=16] {'col'}, dimensions={0} | all-to-all | bytes 32768 | tf_op jit(solution)/shard_map/all_to_all | solution.py:313
  15.4 4.0 %all-to-all-start = ((bf16[16,48,1536]{2,1,0:T(8,128)(2,1)}), bf16[16,48,1536]{2,1,0:T(8,128)(2,1)S(1)}, u32[]{:S(2)}, u32[]{:S(2)}) async-start(bf16[16,48,1536]{2,1,0:T(8,128)(2,1)} %bitcast.24), calls=%async_computation | async-start | bytes 4718592 | tf_op jit(solution)/shard_map/all_to_all | solution.py:307
  20.0 2.3 %stack.18 = bf16[384,1536]{1,0:T(8,128)(2,1)} custom-call(s32[1]{0:T(128)} %bitcast.10.half_ref, bf16[384,1536]{1,0:T(8,128)(2,1)} %refs_3_.3, bf16[384,1536]{1,0:T(8,128)(2,1)} %refs_4_.3), custom_call_target="tpu_custom_call" | custom-call | bytes 2359296 | tf_op jit(solution)/shard_map/stack/pallas_call | solution.py:92
  22.3 2.7 %collective-permute-start.4 = (bf16[384,1536]{1,0:T(8,128)(2,1)}, bf16[384,1536]{1,0:T(8,128)(2,1)}, u32[]{:S(2)}, u32[]{:S(2)}) collective-permute-start(bf16[384,1536]{1,0:T(8,128)(2,1)} %stack.18), channel_id=1, source_target_pairs={{0,4},{1,13},{32,36},{33,45},{64,68},{65,77},{96,100},{97,109},{4,... | collective-permute-start | bytes 3538952 | tf_op jit(solution)/shard_map/ppermute | solution.py:39
  38.9 5.8 %concatenate.20 = bf16[1536]{0:T(1024)(128)(2,1)} concatenate(bf16[192]{0:T(256)(128)(2,1)} %get-tuple-element.24, bf16[192]{0:T(256)(128)(2,1)} %get-tuple-element.23, bf16[192]{0:T(256)(128)(2,1)} %get-tuple-element.42, bf16[192]{0:T(256)(128)(2,1)} %get-tuple-element.43, bf16[192]{0:T(256)(128)(2,1)} %get-tuple-element.18, bf16[192]{0:T(256)(128)(2,1)} %get-tuple-element.17, ...), dimensions={0} | concatenate | bytes 6144 | tf_op jit(solution)/shard_map/concatenate | solution.py:349
  48.6 4.0 %concatenate.19 = bf16[1536]{0:T(1024)(128)(2,1)} concatenate(bf16[768]{0:T(1024)(128)(2,1)} %reshape.47, bf16[192]{0:T(256)(128)(2,1)} %get-tuple-element.26, bf16[192]{0:T(256)(128)(2,1)} %get-tuple-element.25, bf16[192]{0:T(256)(128)(2,1)} %get-tuple-element.40, bf16[192]{0:T(256)(128)(2,1)} %get-tuple-element.41), dimensions={0} | concatenate | bytes 6144 | tf_op jit(solution)/shard_map/concatenate | solution.py:346
  55.3 2.4 %stack.19 = bf16[384,1536]{1,0:T(8,128)(2,1)} custom-call(s32[1]{0:T(128)} %bitcast.10.half_ref, bf16[384,1536]{1,0:T(8,128)(2,1)} %collective-permute-done.6.refs_0_.refs_5_, bf16[384,1536]{1,0:T(8,128)(2,1)} %collective-permute-done.7.refs_1_.refs_6_), custom_call_target="tpu_custom_call" | custom-call | bytes 2359296 | tf_op jit(solution)/shard_map/stack/pallas_call | solution.py:92
  58.3 2.1 %collective-permute-done.4.refs_7_ = bf16[384,1536]{1,0:T(8,128)(2,1)} collective-permute-done((bf16[384,1536]{1,0:T(8,128)(2,1)}, bf16[384,1536]{1,0:T(8,128)(2,1)}, u32[]{:S(2)}, u32[]{:S(2)}) %collective-permute-start.4) | collective-permute-done | bytes 1179680 | tf_op jit(solution)/shard_map/ppermute | solution.py:39
  62.5 3.8 %collective-permute-start.5 = (bf16[384,1536]{1,0:T(8,128)(2,1)}, bf16[384,1536]{1,0:T(8,128)(2,1)}, u32[]{:S(2)}, u32[]{:S(2)}) collective-permute-start(bf16[384,1536]{1,0:T(8,128)(2,1)} %collective-permute-done.4.refs_7_), channel_id=1, source_target_pairs={{0,32},{1,97},{32,64},{33,1},{64,96},{65,33},{96,0},{97,65},{4,36}... | collective-permute-start | bytes 3538952 | tf_op jit(solution)/shard_map/ppermute | solution.py:39
  68.0 4.4 %collective-permute-start = (bf16[3,16,1536]{2,1,0:T(8,128)(2,1)S(1)}, bf16[3,16,1536]{2,1,0:T(8,128)(2,1)S(1)}, u32[]{:S(2)}, u32[]{:S(2)}) collective-permute-start(bf16[3,16,1536]{2,1,0:T(8,128)(2,1)S(1)} %bitcast.27), channel_id=1, source_target_pairs={{0,16},{16,32},{32,48},{48,64},{64,80},{80,96},{96,112},{1,17},{17... | collective-permute-start | bytes 442376 | tf_op jit(solution)/shard_map/ppermute | solution.py:68
  75.8 7.0 %collective-permute-done.1.edge_ref = bf16[3,16,1536]{2,1,0:T(8,128)(2,1)S(1)} collective-permute-done((bf16[3,16,1536]{2,1,0:T(8,128)(2,1)S(1)}, bf16[3,16,1536]{2,1,0:T(8,128)(2,1)S(1)}, u32[]{:S(2)}, u32[]{:S(2)}) %collective-permute-start.1) | collective-permute-done | bytes 147488 | tf_op jit(solution)/shard_map/ppermute | solution.py:69
  83.2 1.9 collective-permute-start.3
  85.1 4.8 %collective-permute-start.9 = (bf16[384,1536]{1,0:T(8,128)(2,1)}, bf16[384,1536]{1,0:T(8,128)(2,1)S(1)}, u32[]{:S(2)}, u32[]{:S(2)}) collective-permute-start(bf16[384,1536]{1,0:T(8,128)(2,1)} %collective-permute-done.8.refs_8_), channel_id=1, source_target_pairs={{0,32},{1,97},{32,64},{33,1},{64,96},{65,33},{96,0},{97,65},{4,36}... | collective-permute-start | bytes 3538952 | tf_op jit(solution)/shard_map/ppermute | solution.py:39
  90.4 3.0 %collective-permute-done.3.right_ref = bf16[38,3,1536]{2,1,0:T(4,128)(2,1)S(1)} collective-permute-done((bf16[38,3,1536]{2,1,0:T(4,128)(2,1)S(1)}, bf16[38,3,1536]{2,1,0:T(4,128)(2,1)S(1)}, u32[]{:S(2)}, u32[]{:S(2)}) %collective-permute-start.3) | collective-permute-done | bytes 350240 | tf_op jit(solution)/shard_map/ppermute | solution.py:373
  95.3 5.5 %collective-permute-done.2.left_ref = bf16[38,3,1536]{2,1,0:T(4,128)(2,1)S(1)} collective-permute-done((bf16[38,3,1536]{2,1,0:T(4,128)(2,1)S(1)}, bf16[38,3,1536]{2,1,0:T(4,128)(2,1)S(1)}, u32[]{:S(2)}, u32[]{:S(2)}) %collective-permute-start.2) | collective-permute-done | bytes 350240 | tf_op jit(solution)/shard_map/ppermute | solution.py:372
  101.6 9.3 %conv.3.refs_1_ = bf16[256,1536]{1,0:T(8,128)(2,1)} custom-call(bf16[32,16,1536]{2,1,0:T(8,128)(2,1)} %bitcast.22, bf16[3,16,1536]{2,1,0:T(8,128)(2,1)} %copy-done.6, bf16[38,3,1536]{2,1,0:T(4,128)(2,1)} %copy-done.3, bf16[38,3,1536]{2,1,0:T(4,128)(2,1)} %copy-done.2, f32[7,7,1536]{2,1,0:T(8,128)} %weight_ref.3, f32[3,1536]{1,0:T(4,128)} %pad_maximum_fusion.2.vector_ref), custom_call_target="tpu_custom_call" | custom-call | flops 39321600 | bytes 3145728 | tf_op jit(solution)/shard_map/conv/pallas_call | solution.py:172
  110.8 5.5 %collective-permute-start.19 = (bf16[256,1536]{1,0:T(8,128)(2,1)}, bf16[256,1536]{1,0:T(8,128)(2,1)}, u32[]{:S(2)}, u32[]{:S(2)}) collective-permute-start(bf16[256,1536]{1,0:T(8,128)(2,1)} %conv.3.refs_1_), channel_id=1, source_target_pairs={{0,2},{1,19},{32,34},{33,51},{64,66},{65,83},{96,98},{97,115},{4,6... | collective-permute-start | bytes 2359304 | tf_op jit(solution)/shard_map/ppermute | solution.py:39
  116.4 9.3 %conv.2.refs_0_ = bf16[256,1536]{1,0:T(8,128)(2,1)} custom-call(bf16[32,16,1536]{2,1,0:T(8,128)(2,1)} %bitcast.23, bf16[3,16,1536]{2,1,0:T(8,128)(2,1)} %copy-done.5, bf16[38,3,1536]{2,1,0:T(4,128)(2,1)} %copy-done.3, bf16[38,3,1536]{2,1,0:T(4,128)(2,1)} %copy-done.2, f32[7,7,1536]{2,1,0:T(8,128)} %weight_ref.3, f32[3,1536]{1,0:T(4,128)} %pad_maximum_fusion.2.vector_ref), custom_call_target="tpu_custom_call" | custom-call | flops 39321600 | bytes 3145728 | tf_op jit(solution)/shard_map/conv/pallas_call | solution.py:172
  127.4 9.3 %collective-permute-done.18.refs_0_ = bf16[256,1536]{1,0:T(8,128)(2,1)S(1)} collective-permute-done((bf16[256,1536]{1,0:T(8,128)(2,1)}, bf16[256,1536]{1,0:T(8,128)(2,1)S(1)}, u32[]{:S(2)}, u32[]{:S(2)}) %collective-permute-start.18) | collective-permute-done | bytes 786464 | tf_op jit(solution)/shard_map/ppermute | solution.py:39
  139.3 14.6 %mlp.6.refs_11_ = f32[512,1536]{1,0:T(8,128)} custom-call(bf16[256,1536]{1,0:T(8,128)(2,1)} %copy-done.14, bf16[256,1536]{1,0:T(8,128)(2,1)} %collective-permute-done.19.refs_1_, f32[1,1536]{1,0:T(1,128)} %reshape.51.refs_2_, bf16[384,1536]{1,0:T(8,128)(2,1)} %refs_3_.3, bf16[384,1536]{1,0:T(8,128)(2,1)} %refs_4_.3, ...), custom_call_target="tpu_custom_call" | custom-call | flops 4831838208 | bytes 9437184 | tf_op jit(solution)/shard_map/mlp/pallas_call | solution.py:267
  154.9 15.3 %mlp.7 = bf16[512,1536]{1,0:T(8,128)(2,1)} custom-call(bf16[256,1536]{1,0:T(8,128)(2,1)} %copy-done.14, bf16[256,1536]{1,0:T(8,128)(2,1)} %collective-permute-done.19.refs_1_, f32[1,1536]{1,0:T(1,128)} %reshape.49.refs_2_, bf16[384,1536]{1,0:T(8,128)(2,1)} %collective-permute-done.5.refs_3_, bf16[384,1536]{1,0:T(8,128)(2,1)} %copy-done.12, ...), custom_call_target="tpu_custom_call" | custom-call | flops 4831838208 | bytes 9437184 | tf_op jit(solution)/shard_map/mlp/pallas_call | solution.py:267
  170.9 14.6 %mlp.4.refs_11_ = f32[512,1536]{1,0:T(8,128)} custom-call(bf16[256,1536]{1,0:T(8,128)(2,1)} %conv.2.refs_0_, bf16[256,1536]{1,0:T(8,128)(2,1)} %conv.3.refs_1_, f32[1,1536]{1,0:T(1,128)} %reshape.51.refs_2_, bf16[384,1536]{1,0:T(8,128)(2,1)} %refs_3_.3, bf16[384,1536]{1,0:T(8,128)(2,1)} %refs_4_.3, bf16[384,1536]{1,0:T(8,128)(2,1)} %collective-permute-done.6.refs_0_.refs_5_, ...), custom_call_target="tpu_custom_call" | custom-call | flops 4831838208 | bytes 9437184 | tf_op jit(solution)/shard_map/mlp/pallas_call | solution.py:267
  185.5 16.0 %mlp.5 = f32[512,1536]{1,0:T(8,128)} custom-call(bf16[256,1536]{1,0:T(8,128)(2,1)} %conv.2.refs_0_, bf16[256,1536]{1,0:T(8,128)(2,1)} %conv.3.refs_1_, f32[1,1536]{1,0:T(1,128)} %reshape.49.refs_2_, bf16[384,1536]{1,0:T(8,128)(2,1)} %collective-permute-done.5.refs_3_, bf16[384,1536]{1,0:T(8,128)(2,1)} %copy-done.12, ...), custom_call_target="tpu_custom_call" | custom-call | flops 4831838208 | bytes 9437184 | tf_op jit(solution)/shard_map/mlp/pallas_call | solution.py:267
  201.5 3.8 %add_convert_fusion = bf16[512,1536]{1,0:T(8,128)(2,1)} fusion(f32[512,1536]{1,0:T(8,128)} %mlp.5, bf16[512,1536]{1,0:T(8,128)(2,1)S(1)} %collective-permute-done.20, bf16[512,1536]{1,0:T(8,128)(2,1)S(1)} %copy-done.1, f32[1536]{0:T(1024)S(1)} %copy-done.10, f32[1536]{0:T(1024)S(1)} %copy-done.11), kind=kLoop, calls=%fused_computation.1 | loop fusion | flops 5505024 | bytes 7876608 | tf_op jit(solution)/shard_map/convert_element_type | solution.py:386
  (105 shorter events, 41.3 us)
Async XLA Ops:
  15.4 50.9 %all-to-all-start = ((bf16[16,48,1536]{2,1,0:T(8,128)(2,1)}), bf16[16,48,1536]{2,1,0:T(8,128)(2,1)S(1)}, u32[]{:S(2)}, u32[]{:S(2)}) async-start(bf16[16,48,1536]{2,1,0:T(8,128)(2,1)} %bitcast.24), calls=%async_computation | async-start | bytes 4718592 | tf_op jit(solution)/shard_map/all_to_all | solution.py:307
  19.4 35.8 %collective-permute-start.6 = (bf16[384,1536]{1,0:T(8,128)(2,1)S(1)}, bf16[384,1536]{1,0:T(8,128)(2,1)}, u32[]{:S(2)}, u32[]{:S(2)}) collective-permute-start(bf16[384,1536]{1,0:T(8,128)(2,1)S(1)} %copy-done.4), channel_id=1, source_target_pairs={{0,1},{1,0},{32,33},{33,32},{64,65},{65,64},{96,97},{97,96},{4,5},... | collective-permute-start | bytes 3538952 | tf_op jit(solution)/shard_map/ppermute | solution.py:39
  19.8 35.5 %collective-permute-start.7 = (bf16[384,1536]{1,0:T(8,128)(2,1)}, bf16[384,1536]{1,0:T(8,128)(2,1)}, u32[]{:S(2)}, u32[]{:S(2)}) collective-permute-start(bf16[384,1536]{1,0:T(8,128)(2,1)} %refs_4_.3), channel_id=1, source_target_pairs={{0,1},{1,0},{32,33},{33,32},{64,65},{65,64},{96,97},{97,96},{4,5},... | collective-permute-start | bytes 3538952 | tf_op jit(solution)/shard_map/ppermute | solution.py:39
  22.3 38.0 %collective-permute-start.4 = (bf16[384,1536]{1,0:T(8,128)(2,1)}, bf16[384,1536]{1,0:T(8,128)(2,1)}, u32[]{:S(2)}, u32[]{:S(2)}) collective-permute-start(bf16[384,1536]{1,0:T(8,128)(2,1)} %stack.18), channel_id=1, source_target_pairs={{0,4},{1,13},{32,36},{33,45},{64,68},{65,77},{96,100},{97,109},{4,... | collective-permute-start | bytes 3538952 | tf_op jit(solution)/shard_map/ppermute | solution.py:39
  57.7 27.5 %collective-permute-start.8 = (bf16[384,1536]{1,0:T(8,128)(2,1)}, bf16[384,1536]{1,0:T(8,128)(2,1)}, u32[]{:S(2)}, u32[]{:S(2)}) collective-permute-start(bf16[384,1536]{1,0:T(8,128)(2,1)} %stack.19), channel_id=1, source_target_pairs={{0,4},{1,13},{32,36},{33,45},{64,68},{65,77},{96,100},{97,109},{4,... | collective-permute-start | bytes 3538952 | tf_op jit(solution)/shard_map/ppermute | solution.py:39
  60.4 65.3 %collective-permute-start.16 = (bf16[384,1536]{1,0:T(8,128)(2,1)}, bf16[384,1536]{1,0:T(8,128)(2,1)}, u32[]{:S(2)}, u32[]{:S(2)}) collective-permute-start(bf16[384,1536]{1,0:T(8,128)(2,1)} %collective-permute-done.4.refs_7_), channel_id=1, source_target_pairs={{0,1},{1,0},{32,33},{33,32},{64,65},{65,64},{96,97},{97,96},{4,5},... | collective-permute-start | bytes 3538952 | tf_op jit(solution)/shard_map/ppermute | solution.py:39
  62.0 28.0 %collective-permute-start.12 = (bf16[384,1536]{1,0:T(8,128)(2,1)}, bf16[384,1536]{1,0:T(8,128)(2,1)}, u32[]{:S(2)}, u32[]{:S(2)}) collective-permute-start(bf16[384,1536]{1,0:T(8,128)(2,1)} %collective-permute-done.4.refs_7_), channel_id=1, source_target_pairs={{0,4},{1,13},{32,36},{33,45},{64,68},{65,77},{96,100},{97,109},{4,... | collective-permute-start | bytes 3538952 | tf_op jit(solution)/shard_map/ppermute | solution.py:39
  62.5 63.1 %collective-permute-start.5 = (bf16[384,1536]{1,0:T(8,128)(2,1)}, bf16[384,1536]{1,0:T(8,128)(2,1)}, u32[]{:S(2)}, u32[]{:S(2)}) collective-permute-start(bf16[384,1536]{1,0:T(8,128)(2,1)} %collective-permute-done.4.refs_7_), channel_id=1, source_target_pairs={{0,32},{1,97},{32,64},{33,1},{64,96},{65,33},{96,0},{97,65},{4,36}... | collective-permute-start | bytes 3538952 | tf_op jit(solution)/shard_map/ppermute | solution.py:39
  68.0 6.4 %collective-permute-start = (bf16[3,16,1536]{2,1,0:T(8,128)(2,1)S(1)}, bf16[3,16,1536]{2,1,0:T(8,128)(2,1)S(1)}, u32[]{:S(2)}, u32[]{:S(2)}) collective-permute-start(bf16[3,16,1536]{2,1,0:T(8,128)(2,1)S(1)} %bitcast.27), channel_id=1, source_target_pairs={{0,16},{16,32},{32,48},{48,64},{64,80},{80,96},{96,112},{1,17},{17... | collective-permute-start | bytes 442376 | tf_op jit(solution)/shard_map/ppermute | solution.py:68
  74.5 36.4 %copy-start.5 = (bf16[3,16,1536]{2,1,0:T(8,128)(2,1)}, bf16[3,16,1536]{2,1,0:T(8,128)(2,1)S(1)}, u32[]{:S(2)}) copy-start(bf16[3,16,1536]{2,1,0:T(8,128)(2,1)S(1)} %collective-permute-done.edge_ref) | copy-start | bytes 442372
  74.5 8.3 %collective-permute-start.1 = (bf16[3,16,1536]{2,1,0:T(8,128)(2,1)S(1)}, bf16[3,16,1536]{2,1,0:T(8,128)(2,1)S(1)}, u32[]{:S(2)}, u32[]{:S(2)}) collective-permute-start(bf16[3,16,1536]{2,1,0:T(8,128)(2,1)S(1)} %bitcast.26), channel_id=1, source_target_pairs={{16,0},{32,16},{48,32},{64,48},{80,64},{96,80},{112,96},{17,1},{33... | collective-permute-start | bytes 442376 | tf_op jit(solution)/shard_map/ppermute | solution.py:69
  83.2 10.2 %collective-permute-start.3 = (bf16[38,3,1536]{2,1,0:T(4,128)(2,1)S(1)}, bf16[38,3,1536]{2,1,0:T(4,128)(2,1)S(1)}, u32[]{:S(2)}, u32[]{:S(2)}) collective-permute-start(bf16[38,3,1536]{2,1,0:T(4,128)(2,1)S(1)} %pad_maximum_fusion.1), channel_id=1, source_target_pairs={{1,0},{2,1},{3,2},{4,3},{5,4},{6,5},{7,6},{8,7},{9,8},{10,9},{11,1... | collective-permute-start | bytes 1050632 | tf_op jit(solution)/shard_map/ppermute | solution.py:373
  85.1 51.6 %collective-permute-start.9 = (bf16[384,1536]{1,0:T(8,128)(2,1)}, bf16[384,1536]{1,0:T(8,128)(2,1)S(1)}, u32[]{:S(2)}, u32[]{:S(2)}) collective-permute-start(bf16[384,1536]{1,0:T(8,128)(2,1)} %collective-permute-done.8.refs_8_), channel_id=1, source_target_pairs={{0,32},{1,97},{32,64},{33,1},{64,96},{65,33},{96,0},{97,65},{4,36}... | collective-permute-start | bytes 3538952 | tf_op jit(solution)/shard_map/ppermute | solution.py:39
  89.9 47.6 %collective-permute-start.14 = (bf16[384,1536]{1,0:T(8,128)(2,1)}, bf16[384,1536]{1,0:T(8,128)(2,1)}, u32[]{:S(2)}, u32[]{:S(2)}) collective-permute-start(bf16[384,1536]{1,0:T(8,128)(2,1)} %collective-permute-done.12.refs_7_), channel_id=1, source_target_pairs={{0,32},{1,97},{32,64},{33,1},{64,96},{65,33},{96,0},{97,65},{4,36}... | collective-permute-start | bytes 3538952 | tf_op jit(solution)/shard_map/ppermute | solution.py:39
  93.4 7.4 %collective-permute-start.2 = (bf16[38,3,1536]{2,1,0:T(4,128)(2,1)S(1)}, bf16[38,3,1536]{2,1,0:T(4,128)(2,1)S(1)}, u32[]{:S(2)}, u32[]{:S(2)}) collective-permute-start(bf16[38,3,1536]{2,1,0:T(4,128)(2,1)S(1)} %pad_maximum_fusion), channel_id=1, source_target_pairs={{0,1},{1,2},{2,3},{3,4},{4,5},{5,6},{6,7},{7,8},{8,9},{9,10},{10,1... | collective-permute-start | bytes 1050632 | tf_op jit(solution)/shard_map/ppermute | solution.py:372
  110.8 27.8 %copy-start.8 = (f32[1536]{0:T(1024)S(1)}, f32[1536]{0:T(1024)}, u32[]{:S(2)}) copy-start(f32[1536]{0:T(1024)} %convert_element_type.32) | copy-start | bytes 18436
  110.8 14.9 %collective-permute-start.19 = (bf16[256,1536]{1,0:T(8,128)(2,1)}, bf16[256,1536]{1,0:T(8,128)(2,1)}, u32[]{:S(2)}, u32[]{:S(2)}) collective-permute-start(bf16[256,1536]{1,0:T(8,128)(2,1)} %conv.3.refs_1_), channel_id=1, source_target_pairs={{0,2},{1,19},{32,34},{33,51},{64,66},{65,83},{96,98},{97,115},{4,6... | collective-permute-start | bytes 2359304 | tf_op jit(solution)/shard_map/ppermute | solution.py:39
  125.6 11.1 %collective-permute-start.18 = (bf16[256,1536]{1,0:T(8,128)(2,1)}, bf16[256,1536]{1,0:T(8,128)(2,1)S(1)}, u32[]{:S(2)}, u32[]{:S(2)}) collective-permute-start(bf16[256,1536]{1,0:T(8,128)(2,1)} %conv.2.refs_0_), channel_id=1, source_target_pairs={{0,2},{1,19},{32,34},{33,51},{64,66},{65,83},{96,98},{97,115},{4,6... | collective-permute-start | bytes 2359304 | tf_op jit(solution)/shard_map/ppermute | solution.py:39
  125.6 13.6 %collective-permute-start.17 = (bf16[384,1536]{1,0:T(8,128)(2,1)}, bf16[384,1536]{1,0:T(8,128)(2,1)}, u32[]{:S(2)}, u32[]{:S(2)}) collective-permute-start(bf16[384,1536]{1,0:T(8,128)(2,1)} %collective-permute-done.8.refs_8_), channel_id=1, source_target_pairs={{0,1},{1,0},{32,33},{33,32},{64,65},{65,64},{96,97},{97,96},{4,5},... | collective-permute-start | bytes 3538952 | tf_op jit(solution)/shard_map/ppermute | solution.py:39
  125.7 28.1 %collective-permute-start.13 = (bf16[384,1536]{1,0:T(8,128)(2,1)}, bf16[384,1536]{1,0:T(8,128)(2,1)S(1)}, u32[]{:S(2)}, u32[]{:S(2)}) collective-permute-start(bf16[384,1536]{1,0:T(8,128)(2,1)} %collective-permute-done.12.refs_7_), channel_id=1, source_target_pairs={{0,1},{1,0},{32,33},{33,32},{64,65},{65,64},{96,97},{97,96},{4,5},... | collective-permute-start | bytes 3538952 | tf_op jit(solution)/shard_map/ppermute | solution.py:39
  136.7 17.2 %collective-permute-start.10 = (bf16[384,1536]{1,0:T(8,128)(2,1)}, bf16[384,1536]{1,0:T(8,128)(2,1)}, u32[]{:S(2)}, u32[]{:S(2)}) collective-permute-start(bf16[384,1536]{1,0:T(8,128)(2,1)} %collective-permute-done.5.refs_3_), channel_id=1, source_target_pairs={{0,1},{1,0},{32,33},{33,32},{64,65},{65,64},{96,97},{97,96},{4,5},... | collective-permute-start | bytes 3538952 | tf_op jit(solution)/shard_map/ppermute | solution.py:39
  137.6 16.3 %collective-permute-start.11 = (bf16[384,1536]{1,0:T(8,128)(2,1)S(1)}, bf16[384,1536]{1,0:T(8,128)(2,1)}, u32[]{:S(2)}, u32[]{:S(2)}) collective-permute-start(bf16[384,1536]{1,0:T(8,128)(2,1)S(1)} %collective-permute-done.9.refs_4_), channel_id=1, source_target_pairs={{0,1},{1,0},{32,33},{33,32},{64,65},{65,64},{96,97},{97,96},{4,5},... | collective-permute-start | bytes 3538952 | tf_op jit(solution)/shard_map/ppermute | solution.py:39
  137.6 16.3 %collective-permute-start.15 = (bf16[384,1536]{1,0:T(8,128)(2,1)}, bf16[384,1536]{1,0:T(8,128)(2,1)}, u32[]{:S(2)}, u32[]{:S(2)}) collective-permute-start(bf16[384,1536]{1,0:T(8,128)(2,1)} %collective-permute-done.14.refs_9_), channel_id=1, source_target_pairs={{0,1},{1,0},{32,33},{33,32},{64,65},{65,64},{96,97},{97,96},{4,5},... | collective-permute-start | bytes 3538952 | tf_op jit(solution)/shard_map/ppermute | solution.py:39
  170.2 31.3 %collective-permute-start.20 = (bf16[512,1536]{1,0:T(8,128)(2,1)}, bf16[512,1536]{1,0:T(8,128)(2,1)S(1)}, u32[]{:S(2)}, u32[]{:S(2)}) collective-permute-start(bf16[512,1536]{1,0:T(8,128)(2,1)} %mlp.7), channel_id=1, source_target_pairs={{0,18},{1,3},{32,50},{33,35},{64,82},{65,67},{96,114},{97,99},{4,2... | collective-permute-start | bytes 4718600 | tf_op jit(solution)/shard_map/ppermute | solution.py:39
  (14 other events, 150.8 us)

commit v2 on v1

--- a/solution.py
+++ b/solution.py
@@ -72,6 +72,31 @@
 
 def whole(space=VMEM):
     return pl.BlockSpec(memory_space=space)
+
+
+def join_kernel(patches_ref, head_ref, out_ref, sem):
+    channels = patches_ref.shape[1]
+    copy = pltpu.make_async_copy(patches_ref, out_ref.at[:, pl.ds(0, channels)], sem)
+    copy.start()
+    groups, lines, _ = head_ref.shape
+    size = out_ref.shape[0] // groups
+    out_ref[:, channels:] = jnp.zeros((out_ref.shape[0], LANES), out_ref.dtype)
+    for g in range(groups):
+        out_ref[g * size : g * size + lines, channels:] = head_ref[g]
+    copy.wait()
+
+
+def join(patches, head):
+    rows, channels = patches.shape
+    return pl.pallas_call(
+        join_kernel,
+        out_shape=jax.ShapeDtypeStruct((rows, channels + LANES), patches.dtype),
+        in_specs=[whole(pl.ANY), whole()],
+        out_specs=whole(),
+        scratch_shapes=[pltpu.SemaphoreType.DMA],
+        cost_estimate=pl.CostEstimate(flops=0, bytes_accessed=4 * rows * channels, transcendentals=0),
+        name="join",
+    )(patches, head)
 
 
 def stack_kernel(half_ref, *refs):
@@ -98,6 +123,52 @@
         cost_estimate=pl.CostEstimate(flops=0, bytes_accessed=4 * len(sources) * HALF * channels, transcendentals=0),
         name="stack",
     )(half, *sources)
+
+
+def notes_kernel(place_ref, moved_ref, slots_ref, bias_ref, notes):
+    groups, lines, _ = notes.shape
+    notes[...] = moved_ref[:, :lines, moved_ref.shape[2] - LANES :]
+    y, lo, core, odd = place_ref[0], place_ref[1], place_ref[2], place_ref[3]
+    width = slots_ref.shape[1]
+    for g in range(groups):
+        parts = notes[g, 0:2, :width].astype(jnp.float32)
+        slots_ref[g : g + 1, :] = (parts[0:1] * 16.0 + parts[1:2]).astype(jnp.int32)
+
+    def half(step, other, turn):
+        shard = lax.rem(y + step + 4, 4) * 4 + lo * 2 + (1 - core if other else core)
+        lines = notes[shard, :, : HALF // 2].astype(jnp.float32)
+        one, two = [lines[2:3], lines[3:4]], [lines[4:5], lines[5:6]]
+        if turn is None:
+            return one + two
+        pick = jnp.full(one[0].shape, odd, jnp.int32) == (1 - turn)
+        return [jnp.where(pick, q, p) for p, q in zip(one, two)]
+
+    ahead = 2 * core - 1
+    early, late = half(0, False, None) + half(0, True, None), []
+    for turn, group in ((0, early), (1, late)):
+        for step, other in ((ahead, False), (ahead, True), (-ahead, True), (-ahead, False)):
+            group += half(step, other, turn)
+    for turn, other in ((0, False), (0, True), (1, False), (1, True)):
+        late += half(2, other, turn)
+    for k, group in enumerate((early, late)):
+        for j in range(0, len(group), 4):
+            at = slice(j * HALF // 2, (j + 4) * HALF // 2)
+            bias_ref[k : k + 1, at] = jnp.concatenate(group[j : j + 4], axis=1)
+
+
+def read_notes(place, moved):
+    groups, width = moved.shape[:2]
+    return pl.pallas_call(
+        notes_kernel,
+        out_shape=[
+            jax.ShapeDtypeStruct((groups, width), jnp.int32),
+            jax.ShapeDtypeStruct((2, 8 * HALF), jnp.float32),
+        ],
+        in_specs=[whole(pltpu.SMEM), whole()],
+        out_specs=[whole(), whole()],
+        scratch_shapes=[VMEM((groups, 8, LANES), jnp.bfloat16)],
+        name="notes",
+    )(place, moved)
 
 
 def conv_kernel(lower, grid_ref, edge_ref, left_ref, right_ref, weight_ref, vector_ref, out_ref, even, odd, both, conv):
@@ -197,11 +268,11 @@
     return half + half * jnp.tanh(pre * p)
 
 
-def mlp_kernel(plan, bands, count, adds, *refs):
+def mlp_kernel(plan, line, bands, count, adds, *refs):
     rows_refs, bias_ref = refs[:bands], refs[bands]
     pieces = refs[bands + 1 : bands + 1 + count]
     acc_ref = refs[bands + 1 + count] if adds else None
-    out_ref, rows, w_in, w_out, hid, part, sems, row_sems = refs[bands + 1 + count + adds :]
+    out_ref, rows, w_in, w_out, hid, sems, row_sems = refs[bands + 1 + count + adds :]
     blocks = w_in.shape[0] // UNITS
     columns = w_out.shape[1] // UNITS
     ins, outs, at = [], [], 0
@@ -227,20 +298,9 @@
 
     def middle(h, pre):
         at = slice(h * UNITS, (h + 1) * UNITS)
-        hid[:, at] = gelu(pre + bias_ref[0:1, at]).astype(jnp.bfloat16)
-
-    split = blocks // 2 * UNITS
-
-    def second(n, last):
-        at = slice(n * UNITS, (n + 1) * UNITS)
-        span = slice(split, None) if last else slice(0, split)
-        total = jnp.dot(hid[:, span], w_out[span, at], preferred_element_type=jnp.float32)
-        if last:
-            out_ref[:, at] = (part[:, at] + total).astype(out_ref.dtype)
-        else:
-            part[:, at] = total + acc_ref[:, at] if adds else total
-
-    waiting, sent = None, 0
+        hid[:, at] = gelu(pre + bias_ref[line : line + 1, at]).astype(jnp.bfloat16)
+
+    waiting = None
     for h in range(blocks):
         if h == blocks // 2:
             for copy in ins[early:] + outs:
@@ -249,23 +309,21 @@
         if waiting is not None:
             middle(*waiting)
         waiting = (h, pre)
-        if h > blocks // 2:
-            for n in range(sent, sent + 2):
-                second(n, False)
-            sent += 2
     middle(*waiting)
-    for n in range(sent, columns):
-        second(n, False)
     for n in range(columns):
-        second(n, True)
-
-
-def mlp(rows, bias, pieces, plan, acc=None, out_dtype=jnp.float32):
+        at = slice(n * UNITS, (n + 1) * UNITS)
+        total = jnp.dot(hid[...], w_out[:, at], preferred_element_type=jnp.float32)
+        if adds:
+            total = total + acc_ref[:, at]
+        out_ref[:, at] = total.astype(out_ref.dtype)
+
+
+def mlp(rows, bias, line, pieces, plan, acc=None, out_dtype=jnp.float32):
     m, channels = sum(part.shape[0] for part in rows), rows[0].shape[1]
     hidden = sum(p[4] for p in plan)
     adds = acc is not None
     return pl.pallas_call(
-        functools.partial(mlp_kernel, plan, len(rows), len(pieces), int(adds)),
+        functools.partial(mlp_kernel, plan, line, len(rows), len(pieces), int(adds)),
         out_shape=jax.ShapeDtypeStruct((m, channels), out_dtype),
         in_specs=[whole(pl.ANY)] * len(rows) + [whole()] + [whole(pl.ANY)] * len(pieces) + [whole()] * adds,
         out_specs=whole(),
@@ -274,7 +332,6 @@
             VMEM((hidden, channels), jnp.bfloat16),
             VMEM((hidden, channels), jnp.bfloat16),
             VMEM((m, hidden), jnp.bfloat16),
-            VMEM((m, channels), jnp.float32),
             pltpu.SemaphoreType.DMA((len(plan), 2)),
             pltpu.SemaphoreType.DMA((len(rows),)),
         ],
@@ -282,7 +339,7 @@
             flops=4 * m * hidden * channels, bytes_accessed=4 * hidden * channels, transcendentals=m * hidden
         ),
         name="mlp",
-    )(*rows, bias.reshape(1, hidden), *pieces, *([acc] if adds else []))
+    )(*rows, bias, *pieces, *([acc] if adds else []))
 
 
 def local(
@@ -304,17 +361,17 @@
     row, col = lax.axis_index("row"), lax.axis_index("col")
     my_y, my_lo, my_core, my_h = col // 4, (col // 2) % 2, col % 2, (row // 2) % 2
 
-    moved = lax.all_to_all(patches, "col", split_axis=0, concat_axis=0, tiled=True)
-    slots = dest.reshape(16, 48)
-    notes = jnp.concatenate(
-        [slots >> 4, slots & 15, jnp.zeros((16, 32), jnp.int32)], axis=1
-    ).astype(jnp.bfloat16)
-    notes = jnp.concatenate([notes, jnp.broadcast_to(b_in, (16, SHARD))], axis=1)
-    notes = lax.all_to_all(notes, "col", split_axis=0, concat_axis=0, tiled=True)
-
-    w_in_p, w_out_p = send(w_in, to_partner), send(w_out, to_partner)
+    slots = dest.reshape(16, 1, 48)
+    parts = jnp.concatenate([slots >> 4, slots & 15], axis=1).astype(jnp.bfloat16)
+    ours = jnp.broadcast_to(b_in.reshape(1, 4, HALF // 2), (16, 4, HALF // 2))
+    head = jnp.concatenate(
+        [jnp.pad(parts, ((0, 0), (0, 0), (0, 80))), jnp.pad(ours, ((0, 0), (0, 2), (0, 32)))], axis=1
+    )
+    moved = lax.all_to_all(join(patches, head), "col", split_axis=0, concat_axis=0, tiled=True)
+
     half = my_h.astype(jnp.int32).reshape(1)
     near_a = send(stack(half, w_in, w_out), along_y)
+    w_in_p, w_out_p = send(w_in, to_partner), send(w_out, to_partner)
     near_b = send(stack(half, w_in_p, w_out_p), along_y)
     near_a_z = send(near_a, along_z)
     far = send(near_a, along_y)
@@ -327,36 +384,19 @@
     near_b_zp = send(near_b_z, to_partner)
     far_zp = send(far_z, to_partner)
 
-    bias = notes[:, 128:].reshape(4, 2, 2, 2, HALF)
-    bias = lax.dynamic_index_in_dim(bias, my_lo, axis=1, keepdims=False)
-    bias = jnp.where(my_core == 1, bias[:, ::-1], bias)
-    turned = jnp.where(my_h == 1, bias[:, :, ::-1], bias)
-    ahead = 2 * my_core - 1
-
-    def at(array, step):
-        return lax.dynamic_index_in_dim(array, (my_y + step + 4) % 4, axis=0, keepdims=False)
-
-    b_one, b_two, b_far = at(turned, ahead), at(turned, -ahead), at(turned, 2)
-    b0 = at(bias, 0).reshape(-1)
-    b1 = jnp.concatenate([b_one[0, 0], b_one[1, 0], b_two[1, 0], b_two[0, 0]])
-    b2 = jnp.concatenate([b_one[0, 1], b_one[1, 1], b_two[1, 1], b_two[0, 1]])
-    b3 = jnp.concatenate([b_far[0, 0], b_far[1, 0], b_far[0, 1], b_far[1, 1]])
     early = (w_in, w_out, w_in_p, w_out_p, near_a, near_b, near_a_p, near_b_p)
     early_plan = ((0, 0, 1, 0, SHARD), (2, 0, 3, 0, SHARD)) + tuple((a, 0, a, HALF, HALF) for a in range(4, 8))
-    early_bias = jnp.concatenate([b0, b1]).astype(jnp.float32)
     late = (near_a_z, near_b_z, near_a_zp, near_b_zp, far, far_p, far_z, far_zp)
     late_plan = tuple((a, 0, a, HALF, HALF) for a in range(8))
-    late_bias = jnp.concatenate([b2, b3]).astype(jnp.float32)
-
-    where = (notes[:, :48].astype(jnp.int32) << 4) + notes[:, 48:96].astype(jnp.int32)
+
+    place = jnp.stack([my_y, my_lo, my_core, my_h]).astype(jnp.int32)
+    vectors = jnp.stack([conv_bias, norm_gain, norm_bias])
+    moved, vectors, place = lax.optimization_barrier((moved, vectors, place))
+    where, bias = read_notes(place, moved.reshape(16, 48, -1))
     where = where.reshape(-1)
-    vectors = jnp.stack([conv_bias, norm_gain, norm_bias])
-    moved, where, vectors, early_bias, late_bias = lax.optimization_barrier(
-        (moved, where, vectors, early_bias, late_bias)
-    )
     onehot = where[None, :] == jnp.arange(cells, dtype=jnp.int32)[:, None]
     placed = jnp.dot(
-        onehot.astype(jnp.bfloat16), moved, preferred_element_type=jnp.float32
+        onehot.astype(jnp.bfloat16), moved[:, :channels], preferred_element_type=jnp.float32
     )
     present = jnp.any(onehot, axis=1)
     grid = jnp.where(present[:, None], placed, background.astype(jnp.float32)[None, :]).astype(
@@ -376,11 +416,11 @@
 
     flat = (flat_a, flat_b)
     other = (send(flat_a, along_x), send(flat_b, along_x))
-    mine = mlp(flat, early_bias, early, early_plan)
-    theirs = mlp(other, early_bias, early, early_plan)
-    theirs = mlp(other, late_bias, late, late_plan, acc=theirs, out_dtype=jnp.bfloat16)
+    mine = mlp(flat, bias, 0, early, early_plan)
+    theirs = mlp(other, bias, 0, early, early_plan)
+    theirs = mlp(other, bias, 1, late, late_plan, acc=theirs, out_dtype=jnp.bfloat16)
     returned = send(theirs, back_x)
-    mine = mlp(flat, late_bias, late, late_plan, acc=mine)
+    mine = mlp(flat, bias, 1, late, late_plan, acc=mine)
     mixed = mine + returned.astype(jnp.float32)
     result = grid.astype(jnp.float32) + layer_scale * (mixed + b_out)
     return result.astype(jnp.bfloat16).reshape(TH, TW, channels)

time: 208 us -> 193 us (0.928)
  local copies, waits for them, and re-layouts: 30 us -> 5.39 us
  waiting for transfers between devices: 28.7 us -> 50.8 us
  blocking collectives: 12.5 us -> 0 us
  other arithmetic: 12 us -> 7.29 us
  starting transfers between devices: 36.7 us -> 40.1 us
    ppermute x17, waiting for transfers between devices: 11.4 us -> 42.4 us  [send(): return lax.ppermute(value, ('row', 'col'), routes(move))]
    all_to_all x1 -> x0, blocking collectives: 12.5 us -> none  [local(): lax.all_to_all(notes, 'col', split_axis=0, concat_axis=0, tiled=True)]
    concatenate x4 -> x0, local copies, waits for them, and re-layouts: 10.6 us -> none  [the longest x1 5.81 us: local(): late_bias = jnp.concatenate([b2, b3]).astype(jnp.float32)]
    ppermute x1, waiting for transfers between devices: 5.49 us -> 0.01 us  [local(): left = lax.ppermute(tall[0], 'col', [(i, i + 1) for i in range(ends)])]
    reshape x5 -> x0, local copies, waits for them, and re-layouts: 4.68 us -> none  [the longest x1 1.39 us: local(): bias = notes[:, 128:].reshape(4, 2, 2, 2, HALF)]
    another operation x3, local copies, waits for them, and re-layouts: 3.87 us -> 0.02 us  [local(): vectors = jnp.stack([conv_bias, norm_gain, norm_bias])]
    all_to_all x1, starting transfers between devices: 4.04 us -> 6.91 us  [local(): lax.all_to_all(join(patches, head), 'col', split_axis=0, concat_axis=0, t...]
    convert_element_type x2 -> x0, other arithmetic: 2.54 us -> none  [the longest x1 1.27 us: local(): early_bias = jnp.concatenate([b0, b1]).astype(jnp.float32)]
  transfers between devices with their start and end apart: 22 -> 22, of which waited for: 6 -> 6; matrix products, arithmetic and copies ran while one was open for 16% -> 3% of each run, Pallas kernels for 33% -> 35%
where the time goes in v2:
time: 193 us; the launch traced here: 191 us
  Pallas kernels  84.4 us (44%)
  waiting for transfers between devices  50.8 us (26%)
  starting transfers between devices  40.1 us (21%)
  other arithmetic  7.29 us (4%)
  local copies, waits for them, and re-layouts  5.39 us (3%)
  matrix products  3.05 us (2%)
    pallas_call x4, Pallas kernels, mlp(): pl.pallas_call(functools.partial(mlp_kernel, plan, line, len(rows), len(p...  54.9 us
    ppermute x17, waiting for transfers between devices, send(): return lax.ppermute(value, ('row', 'col'), routes(move))  42.4 us
    ppermute x17, starting transfers between devices, send(): return lax.ppermute(value, ('row', 'col'), routes(move))  21.9 us
    pallas_call x2, Pallas kernels, conv_norm(): pl.pallas_call(functools.partial(conv_kernel, lower), out_shape=jax.Shape...  18.5 us
    all_to_all x1, starting transfers between devices, local(): lax.all_to_all(join(patches, head), 'col', split_axis=0, concat_axis=0, t...  6.91 us
    ppermute x1, waiting for transfers between devices, halo(): lax.ppermute(head, axis, [(i + 1, i) for i in range(ends)])  5.62 us
    pallas_call x2, Pallas kernels, stack(): pl.pallas_call(stack_kernel, out_shape=jax.ShapeDtypeStruct((len(sources)...  4.61 us
    ppermute x1, starting transfers between devices, halo(): lax.ppermute(tail, axis, [(i, i + 1) for i in range(ends)])  4.36 us
  transfers between devices with their start and end apart: 22, of which 6 were waited for; matrix products, arithmetic and copies ran while one was open for 3% of the time, Pallas kernels for 35%

profile of v2, /device:TPU:1, one launch (start us, length us, event | category | flops | bytes accessed | tf_op | source)
XLA Modules:
  0.0 191.5 jit_solution(13833537128412960907)
XLA Ops:
  2.3 3.9 %join.1 = bf16[768,1664]{1,0:T(8,128)(2,1)} custom-call(bf16[768,1536]{1,0:T(8,128)(2,1)} %patches_ref.1, bf16[16,8,128]{2,1,0:T(8,128)(2,1)} %pad_maximum_fusion.2.head_ref), custom_call_target="tpu_custom_call" | custom-call | bytes 4718592 | tf_op jit(solution)/shard_map/join/pallas_call | solution.py:91
  6.2 6.9 %all-to-all-start = ((bf16[16,48,1664]{2,1,0:T(8,128)(2,1)}), bf16[16,48,1664]{2,1,0:T(8,128)(2,1)S(1)}, u32[]{:S(2)}, u32[]{:S(2)}) async-start(bf16[16,48,1664]{2,1,0:T(8,128)(2,1)} %bitcast.15), calls=%async_computation | async-start | bytes 5111808 | tf_op jit(solution)/shard_map/all_to_all | solution.py:370
  13.7 2.3 %stack.38 = bf16[384,1536]{1,0:T(8,128)(2,1)} custom-call(s32[1]{0:T(128)} %bitcast.5.half_ref, bf16[384,1536]{1,0:T(8,128)(2,1)} %refs_3_.3, bf16[384,1536]{1,0:T(8,128)(2,1)} %refs_4_.3), custom_call_target="tpu_custom_call" | custom-call | bytes 2359296 | tf_op jit(solution)/shard_map/stack/pallas_call | solution.py:117
  16.0 2.6 %collective-permute-start.4 = (bf16[384,1536]{1,0:T(8,128)(2,1)}, bf16[384,1536]{1,0:T(8,128)(2,1)}, u32[]{:S(2)}, u32[]{:S(2)}) collective-permute-start(bf16[384,1536]{1,0:T(8,128)(2,1)} %stack.38), channel_id=1, source_target_pairs={{0,4},{1,13},{32,36},{33,45},{64,68},{65,77},{96,100},{97,109},{4,... | collective-permute-start | bytes 3538952 | tf_op jit(solution)/shard_map/ppermute | solution.py:39
  20.0 2.3 %stack.39 = bf16[384,1536]{1,0:T(8,128)(2,1)} custom-call(s32[1]{0:T(128)} %bitcast.5.half_ref, bf16[384,1536]{1,0:T(8,128)(2,1)} %collective-permute-done.6.refs_0_.refs_5_, bf16[384,1536]{1,0:T(8,128)(2,1)} %collective-permute-done.7.refs_1_.refs_6_), custom_call_target="tpu_custom_call" | custom-call | bytes 2359296 | tf_op jit(solution)/shard_map/stack/pallas_call | solution.py:117
  23.1 33.0 %collective-permute-done.4.refs_7_ = bf16[384,1536]{1,0:T(8,128)(2,1)} collective-permute-done((bf16[384,1536]{1,0:T(8,128)(2,1)}, bf16[384,1536]{1,0:T(8,128)(2,1)}, u32[]{:S(2)}, u32[]{:S(2)}) %collective-permute-start.4) | collective-permute-done | bytes 1179680 | tf_op jit(solution)/shard_map/ppermute | solution.py:39
  59.8 2.4 %notes.1 = (s32[16,48]{1,0:T(8,128)}, f32[2,1536]{1,0:T(2,128)}) custom-call(s32[4]{0:T(128)} %pad_add_fusion.place_ref, bf16[16,48,1664]{2,1,0:T(8,128)(2,1)} %copy-done.2), custom_call_target="tpu_custom_call" | custom-call | tf_op jit(solution)/shard_map/notes/pallas_call | solution.py:161
  63.3 3.1 %fusion = bf16[512,1536]{1,0:T(8,128)(2,1)S(1)} fusion(bf16[768,1664]{1,0:T(8,128)(2,1)} %bitcast.14, bf16[1536]{0:T(1024)(128)(2,1)S(1)} %copy-done.15, pred[512]{0:T(512)(128)(4,1)S(1)} %fusion.2, s32[768]{0:T(1024)S(1)} %eq.19), kind=kOutput, calls=%fused_computation.2 | convolution fusion | flops 1209139200 | bytes 3938816 | tf_op jit(solution)/shard_map/dot_general | solution.py:398
  66.4 4.4 %collective-permute-start = (bf16[3,16,1536]{2,1,0:T(8,128)(2,1)S(1)}, bf16[3,16,1536]{2,1,0:T(8,128)(2,1)S(1)}, u32[]{:S(2)}, u32[]{:S(2)}) collective-permute-start(bf16[3,16,1536]{2,1,0:T(8,128)(2,1)S(1)} %bitcast.17), channel_id=1, source_target_pairs={{0,16},{16,32},{32,48},{48,64},{64,80},{80,96},{96,112},{1,17},{17... | collective-permute-start | bytes 442376 | tf_op jit(solution)/shard_map/ppermute | solution.py:68
  72.4 1.8 collective-permute-done.edge_ref
  74.2 5.6 %collective-permute-done.1.edge_ref = bf16[3,16,1536]{2,1,0:T(8,128)(2,1)S(1)} collective-permute-done((bf16[3,16,1536]{2,1,0:T(8,128)(2,1)S(1)}, bf16[3,16,1536]{2,1,0:T(8,128)(2,1)S(1)}, u32[]{:S(2)}, u32[]{:S(2)}) %collective-permute-start.1) | collective-permute-done | bytes 147488 | tf_op jit(solution)/shard_map/ppermute | solution.py:69
  80.2 2.8 %collective-permute-start.3 = (bf16[38,3,1536]{2,1,0:T(4,128)(2,1)S(1)}, bf16[38,3,1536]{2,1,0:T(4,128)(2,1)S(1)}, u32[]{:S(2)}, u32[]{:S(2)}) collective-permute-start(bf16[38,3,1536]{2,1,0:T(4,128)(2,1)S(1)} %pad_maximum_fusion.1), channel_id=1, source_target_pairs={{1,0},{2,1},{3,2},{4,3},{5,4},{6,5},{7,6},{8,7},{9,8},{10,9},{11,1... | collective-permute-start | bytes 1050632 | tf_op jit(solution)/shard_map/ppermute | solution.py:413
  83.4 2.9 %collective-permute-start.2 = (bf16[38,3,1536]{2,1,0:T(4,128)(2,1)S(1)}, bf16[38,3,1536]{2,1,0:T(4,128)(2,1)S(1)}, u32[]{:S(2)}, u32[]{:S(2)}) collective-permute-start(bf16[38,3,1536]{2,1,0:T(4,128)(2,1)S(1)} %pad_maximum_fusion), channel_id=1, source_target_pairs={{0,1},{1,2},{2,3},{3,4},{4,5},{5,6},{6,7},{7,8},{8,9},{9,10},{10,1... | collective-permute-start | bytes 1050632 | tf_op jit(solution)/shard_map/ppermute | solution.py:412
  86.3 3.7 %collective-permute-start.5 = (bf16[384,1536]{1,0:T(8,128)(2,1)}, bf16[384,1536]{1,0:T(8,128)(2,1)S(1)}, u32[]{:S(2)}, u32[]{:S(2)}) collective-permute-start(bf16[384,1536]{1,0:T(8,128)(2,1)} %collective-permute-done.4.refs_7_), channel_id=1, source_target_pairs={{0,32},{1,97},{32,64},{33,1},{64,96},{65,33},{96,0},{97,65},{4,36}... | collective-permute-start | bytes 3538952 | tf_op jit(solution)/shard_map/ppermute | solution.py:39
  91.0 4.6 %collective-permute-start.9 = (bf16[384,1536]{1,0:T(8,128)(2,1)}, bf16[384,1536]{1,0:T(8,128)(2,1)}, u32[]{:S(2)}, u32[]{:S(2)}) collective-permute-start(bf16[384,1536]{1,0:T(8,128)(2,1)} %collective-permute-done.8.refs_8_), channel_id=1, source_target_pairs={{0,32},{1,97},{32,64},{33,1},{64,96},{65,33},{96,0},{97,65},{4,36}... | collective-permute-start | bytes 3538952 | tf_op jit(solution)/shard_map/ppermute | solution.py:39
  96.3 9.3 %conv.3.refs_1_ = bf16[256,1536]{1,0:T(8,128)(2,1)} custom-call(bf16[32,16,1536]{2,1,0:T(8,128)(2,1)} %bitcast.12, bf16[3,16,1536]{2,1,0:T(8,128)(2,1)} %copy-done.6, bf16[38,3,1536]{2,1,0:T(4,128)(2,1)} %copy-done.4, bf16[38,3,1536]{2,1,0:T(4,128)(2,1)} %copy-done.3, f32[7,7,1536]{2,1,0:T(8,128)} %weight_ref.3, f32[3,1536]{1,0:T(4,128)} %pad_maximum_fusion.3.vector_ref), custom_call_target="tpu_custom_call" | custom-call | flops 39321600 | bytes 3145728 | tf_op jit(solution)/shard_map/conv/pallas_call | solution.py:243
  105.6 4.8 %collective-permute-start.19 = (bf16[256,1536]{1,0:T(8,128)(2,1)}, bf16[256,1536]{1,0:T(8,128)(2,1)S(1)}, u32[]{:S(2)}, u32[]{:S(2)}) collective-permute-start(bf16[256,1536]{1,0:T(8,128)(2,1)} %conv.3.refs_1_), channel_id=1, source_target_pairs={{0,2},{1,19},{32,34},{33,51},{64,66},{65,83},{96,98},{97,115},{4,6... | collective-permute-start | bytes 2359304 | tf_op jit(solution)/shard_map/ppermute | solution.py:39
  110.4 9.2 %conv.2.refs_0_ = bf16[256,1536]{1,0:T(8,128)(2,1)} custom-call(bf16[32,16,1536]{2,1,0:T(8,128)(2,1)} %bitcast.13, bf16[3,16,1536]{2,1,0:T(8,128)(2,1)} %copy-done.5, bf16[38,3,1536]{2,1,0:T(4,128)(2,1)} %copy-done.4, bf16[38,3,1536]{2,1,0:T(4,128)(2,1)} %copy-done.3, f32[7,7,1536]{2,1,0:T(8,128)} %weight_ref.3, f32[3,1536]{1,0:T(4,128)} %pad_maximum_fusion.3.vector_ref), custom_call_target="tpu_custom_call" | custom-call | flops 39321600 | bytes 3145728 | tf_op jit(solution)/shard_map/conv/pallas_call | solution.py:243
  120.3 8.4 %collective-permute-done.14.refs_9_ = bf16[384,1536]{1,0:T(8,128)(2,1)} collective-permute-done((bf16[384,1536]{1,0:T(8,128)(2,1)}, bf16[384,1536]{1,0:T(8,128)(2,1)}, u32[]{:S(2)}, u32[]{:S(2)}) %collective-permute-start.14) | collective-permute-done | bytes 1179680 | tf_op jit(solution)/shard_map/ppermute | solution.py:39
  130.8 13.2 %mlp.6.refs_11_ = f32[512,1536]{1,0:T(8,128)} custom-call(bf16[256,1536]{1,0:T(8,128)(2,1)} %collective-permute-done.18.refs_0_, bf16[256,1536]{1,0:T(8,128)(2,1)} %copy-done.14, f32[2,1536]{1,0:T(2,128)} %get-tuple-element.14.refs_2_, bf16[384,1536]{1,0:T(8,128)(2,1)} %refs_3_.3, bf16[384,1536]{1,0:T(8,128)(2,1)} %refs_4_.3, ...), custom_call_target="tpu_custom_call" | custom-call | flops 4831838208 | bytes 9437184 | tf_op jit(solution)/shard_map/mlp/pallas_call | solution.py:325
  145.1 14.0 %mlp.7 = bf16[512,1536]{1,0:T(8,128)(2,1)} custom-call(bf16[256,1536]{1,0:T(8,128)(2,1)} %collective-permute-done.18.refs_0_, bf16[256,1536]{1,0:T(8,128)(2,1)} %copy-done.14, f32[2,1536]{1,0:T(2,128)} %get-tuple-element.14.refs_2_, bf16[384,1536]{1,0:T(8,128)(2,1)} %copy-done.12, bf16[384,1536]{1,0:T(8,128)(2,1)} %collective-permute-done.9.refs_4_, ...), custom_call_target="tpu_custom_call" | custom-call | flops 4831838208 | bytes 9437184 | tf_op jit(solution)/shard_map/mlp/pallas_call | solution.py:325
  159.8 13.2 %mlp.4.refs_11_ = f32[512,1536]{1,0:T(8,128)} custom-call(bf16[256,1536]{1,0:T(8,128)(2,1)} %conv.2.refs_0_, bf16[256,1536]{1,0:T(8,128)(2,1)} %conv.3.refs_1_, f32[2,1536]{1,0:T(2,128)} %get-tuple-element.14.refs_2_, bf16[384,1536]{1,0:T(8,128)(2,1)} %refs_3_.3, bf16[384,1536]{1,0:T(8,128)(2,1)} %refs_4_.3, ...), custom_call_target="tpu_custom_call" | custom-call | flops 4831838208 | bytes 9437184 | tf_op jit(solution)/shard_map/mlp/pallas_call | solution.py:325
  173.1 14.6 %mlp.5 = f32[512,1536]{1,0:T(8,128)} custom-call(bf16[256,1536]{1,0:T(8,128)(2,1)} %conv.2.refs_0_, bf16[256,1536]{1,0:T(8,128)(2,1)} %conv.3.refs_1_, f32[2,1536]{1,0:T(2,128)} %get-tuple-element.14.refs_2_, bf16[384,1536]{1,0:T(8,128)(2,1)} %copy-done.12, bf16[384,1536]{1,0:T(8,128)(2,1)} %collective-permute-done.9.refs_4_, ...), custom_call_target="tpu_custom_call" | custom-call | flops 4831838208 | bytes 9437184 | tf_op jit(solution)/shard_map/mlp/pallas_call | solution.py:325
  187.7 3.8 %add_convert_fusion = bf16[512,1536]{1,0:T(8,128)(2,1)} fusion(f32[512,1536]{1,0:T(8,128)} %mlp.5, bf16[512,1536]{1,0:T(8,128)(2,1)S(1)} %collective-permute-done.20, bf16[512,1536]{1,0:T(8,128)(2,1)S(1)} %copy-done.1, f32[1536]{0:T(1024)S(1)} %copy-done.10, f32[1536]{0:T(1024)S(1)} %copy-done.11), kind=kLoop, calls=%fused_computation.1 | loop fusion | flops 5505024 | bytes 7876608 | tf_op jit(solution)/shard_map/convert_element_type | solution.py:426
  (85 shorter events, 18.2 us)
Async XLA Ops:
  6.2 52.1 %all-to-all-start = ((bf16[16,48,1664]{2,1,0:T(8,128)(2,1)}), bf16[16,48,1664]{2,1,0:T(8,128)(2,1)S(1)}, u32[]{:S(2)}, u32[]{:S(2)}) async-start(bf16[16,48,1664]{2,1,0:T(8,128)(2,1)} %bitcast.15), calls=%async_computation | async-start | bytes 5111808 | tf_op jit(solution)/shard_map/all_to_all | solution.py:370
  13.2 6.8 %collective-permute-start.6 = (bf16[384,1536]{1,0:T(8,128)(2,1)}, bf16[384,1536]{1,0:T(8,128)(2,1)}, u32[]{:S(2)}, u32[]{:S(2)}) collective-permute-start(bf16[384,1536]{1,0:T(8,128)(2,1)} %refs_3_.3), channel_id=1, source_target_pairs={{0,1},{1,0},{32,33},{33,32},{64,65},{65,64},{96,97},{97,96},{4,5},... | collective-permute-start | bytes 3538952 | tf_op jit(solution)/shard_map/ppermute | solution.py:39
  13.3 6.6 %collective-permute-start.7 = (bf16[384,1536]{1,0:T(8,128)(2,1)}, bf16[384,1536]{1,0:T(8,128)(2,1)}, u32[]{:S(2)}, u32[]{:S(2)}) collective-permute-start(bf16[384,1536]{1,0:T(8,128)(2,1)} %refs_4_.3), channel_id=1, source_target_pairs={{0,1},{1,0},{32,33},{33,32},{64,65},{65,64},{96,97},{97,96},{4,5},... | collective-permute-start | bytes 3538952 | tf_op jit(solution)/shard_map/ppermute | solution.py:39
  16.0 40.1 %collective-permute-start.4 = (bf16[384,1536]{1,0:T(8,128)(2,1)}, bf16[384,1536]{1,0:T(8,128)(2,1)}, u32[]{:S(2)}, u32[]{:S(2)}) collective-permute-start(bf16[384,1536]{1,0:T(8,128)(2,1)} %stack.38), channel_id=1, source_target_pairs={{0,4},{1,13},{32,36},{33,45},{64,68},{65,77},{96,100},{97,109},{4,... | collective-permute-start | bytes 3538952 | tf_op jit(solution)/shard_map/ppermute | solution.py:39
  22.3 41.0 %copy-start.15 = (bf16[1536]{0:T(1024)(128)(2,1)S(1)}, bf16[1536]{0:T(1024)(128)(2,1)}, u32[]{:S(2)}) copy-start(bf16[1536]{0:T(1024)(128)(2,1)} %param.14) | copy-start | bytes 9220
  22.3 64.0 %collective-permute-start.8 = (bf16[384,1536]{1,0:T(8,128)(2,1)}, bf16[384,1536]{1,0:T(8,128)(2,1)}, u32[]{:S(2)}, u32[]{:S(2)}) collective-permute-start(bf16[384,1536]{1,0:T(8,128)(2,1)} %stack.39), channel_id=1, source_target_pairs={{0,4},{1,13},{32,36},{33,45},{64,68},{65,77},{96,100},{97,109},{4,... | collective-permute-start | bytes 3538952 | tf_op jit(solution)/shard_map/ppermute | solution.py:39
  56.2 49.5 %collective-permute-start.16 = (bf16[384,1536]{1,0:T(8,128)(2,1)}, bf16[384,1536]{1,0:T(8,128)(2,1)}, u32[]{:S(2)}, u32[]{:S(2)}) collective-permute-start(bf16[384,1536]{1,0:T(8,128)(2,1)} %collective-permute-done.4.refs_7_), channel_id=1, source_target_pairs={{0,1},{1,0},{32,33},{33,32},{64,65},{65,64},{96,97},{97,96},{4,5},... | collective-permute-start | bytes 3538952 | tf_op jit(solution)/shard_map/ppermute | solution.py:39
  57.7 32.3 %collective-permute-start.12 = (bf16[384,1536]{1,0:T(8,128)(2,1)}, bf16[384,1536]{1,0:T(8,128)(2,1)}, u32[]{:S(2)}, u32[]{:S(2)}) collective-permute-start(bf16[384,1536]{1,0:T(8,128)(2,1)} %collective-permute-done.4.refs_7_), channel_id=1, source_target_pairs={{0,4},{1,13},{32,36},{33,45},{64,68},{65,77},{96,100},{97,109},{4,... | collective-permute-start | bytes 3538952 | tf_op jit(solution)/shard_map/ppermute | solution.py:39
  66.4 7.8 %collective-permute-start = (bf16[3,16,1536]{2,1,0:T(8,128)(2,1)S(1)}, bf16[3,16,1536]{2,1,0:T(8,128)(2,1)S(1)}, u32[]{:S(2)}, u32[]{:S(2)}) collective-permute-start(bf16[3,16,1536]{2,1,0:T(8,128)(2,1)S(1)} %bitcast.17), channel_id=1, source_target_pairs={{0,16},{16,32},{32,48},{48,64},{64,80},{80,96},{96,112},{1,17},{17... | collective-permute-start | bytes 442376 | tf_op jit(solution)/shard_map/ppermute | solution.py:68
  71.1 8.8 %collective-permute-start.1 = (bf16[3,16,1536]{2,1,0:T(8,128)(2,1)S(1)}, bf16[3,16,1536]{2,1,0:T(8,128)(2,1)S(1)}, u32[]{:S(2)}, u32[]{:S(2)}) collective-permute-start(bf16[3,16,1536]{2,1,0:T(8,128)(2,1)S(1)} %bitcast.16), channel_id=1, source_target_pairs={{16,0},{32,16},{48,32},{64,48},{80,64},{96,80},{112,96},{17,1},{33... | collective-permute-start | bytes 442376 | tf_op jit(solution)/shard_map/ppermute | solution.py:69
  74.2 31.4 %copy-start.5 = (bf16[3,16,1536]{2,1,0:T(8,128)(2,1)}, bf16[3,16,1536]{2,1,0:T(8,128)(2,1)S(1)}, u32[]{:S(2)}) copy-start(bf16[3,16,1536]{2,1,0:T(8,128)(2,1)S(1)} %collective-permute-done.edge_ref) | copy-start | bytes 442372
  80.2 10.7 %collective-permute-start.3 = (bf16[38,3,1536]{2,1,0:T(4,128)(2,1)S(1)}, bf16[38,3,1536]{2,1,0:T(4,128)(2,1)S(1)}, u32[]{:S(2)}, u32[]{:S(2)}) collective-permute-start(bf16[38,3,1536]{2,1,0:T(4,128)(2,1)S(1)} %pad_maximum_fusion.1), channel_id=1, source_target_pairs={{1,0},{2,1},{3,2},{4,3},{5,4},{6,5},{7,6},{8,7},{9,8},{10,9},{11,1... | collective-permute-start | bytes 1050632 | tf_op jit(solution)/shard_map/ppermute | solution.py:413
  83.4 12.2 %collective-permute-start.2 = (bf16[38,3,1536]{2,1,0:T(4,128)(2,1)S(1)}, bf16[38,3,1536]{2,1,0:T(4,128)(2,1)S(1)}, u32[]{:S(2)}, u32[]{:S(2)}) collective-permute-start(bf16[38,3,1536]{2,1,0:T(4,128)(2,1)S(1)} %pad_maximum_fusion), channel_id=1, source_target_pairs={{0,1},{1,2},{2,3},{3,4},{4,5},{5,6},{6,7},{7,8},{8,9},{9,10},{10,1... | collective-permute-start | bytes 1050632 | tf_op jit(solution)/shard_map/ppermute | solution.py:412
  86.3 33.4 %collective-permute-start.5 = (bf16[384,1536]{1,0:T(8,128)(2,1)}, bf16[384,1536]{1,0:T(8,128)(2,1)S(1)}, u32[]{:S(2)}, u32[]{:S(2)}) collective-permute-start(bf16[384,1536]{1,0:T(8,128)(2,1)} %collective-permute-done.4.refs_7_), channel_id=1, source_target_pairs={{0,32},{1,97},{32,64},{33,1},{64,96},{65,33},{96,0},{97,65},{4,36}... | collective-permute-start | bytes 3538952 | tf_op jit(solution)/shard_map/ppermute | solution.py:39
  90.0 29.7 %collective-permute-start.17 = (bf16[384,1536]{1,0:T(8,128)(2,1)}, bf16[384,1536]{1,0:T(8,128)(2,1)}, u32[]{:S(2)}, u32[]{:S(2)}) collective-permute-start(bf16[384,1536]{1,0:T(8,128)(2,1)} %collective-permute-done.8.refs_8_), channel_id=1, source_target_pairs={{0,1},{1,0},{32,33},{33,32},{64,65},{65,64},{96,97},{97,96},{4,5},... | collective-permute-start | bytes 3538952 | tf_op jit(solution)/shard_map/ppermute | solution.py:39
  91.0 28.8 %collective-permute-start.9 = (bf16[384,1536]{1,0:T(8,128)(2,1)}, bf16[384,1536]{1,0:T(8,128)(2,1)}, u32[]{:S(2)}, u32[]{:S(2)}) collective-permute-start(bf16[384,1536]{1,0:T(8,128)(2,1)} %collective-permute-done.8.refs_8_), channel_id=1, source_target_pairs={{0,32},{1,97},{32,64},{33,1},{64,96},{65,33},{96,0},{97,65},{4,36}... | collective-permute-start | bytes 3538952 | tf_op jit(solution)/shard_map/ppermute | solution.py:39
  95.6 33.2 %collective-permute-start.14 = (bf16[384,1536]{1,0:T(8,128)(2,1)}, bf16[384,1536]{1,0:T(8,128)(2,1)}, u32[]{:S(2)}, u32[]{:S(2)}) collective-permute-start(bf16[384,1536]{1,0:T(8,128)(2,1)} %collective-permute-done.12.refs_7_), channel_id=1, source_target_pairs={{0,32},{1,97},{32,64},{33,1},{64,96},{65,33},{96,0},{97,65},{4,36}... | collective-permute-start | bytes 3538952 | tf_op jit(solution)/shard_map/ppermute | solution.py:39
  105.6 24.1 %collective-permute-start.19 = (bf16[256,1536]{1,0:T(8,128)(2,1)}, bf16[256,1536]{1,0:T(8,128)(2,1)S(1)}, u32[]{:S(2)}, u32[]{:S(2)}) collective-permute-start(bf16[256,1536]{1,0:T(8,128)(2,1)} %conv.3.refs_1_), channel_id=1, source_target_pairs={{0,2},{1,19},{32,34},{33,51},{64,66},{65,83},{96,98},{97,115},{4,6... | collective-permute-start | bytes 2359304 | tf_op jit(solution)/shard_map/ppermute | solution.py:39
  119.7 11.2 %collective-permute-start.18 = (bf16[256,1536]{1,0:T(8,128)(2,1)}, bf16[256,1536]{1,0:T(8,128)(2,1)}, u32[]{:S(2)}, u32[]{:S(2)}) collective-permute-start(bf16[256,1536]{1,0:T(8,128)(2,1)} %conv.2.refs_0_), channel_id=1, source_target_pairs={{0,2},{1,19},{32,34},{33,51},{64,66},{65,83},{96,98},{97,115},{4,6... | collective-permute-start | bytes 2359304 | tf_op jit(solution)/shard_map/ppermute | solution.py:39
  119.7 24.4 %collective-permute-start.13 = (bf16[384,1536]{1,0:T(8,128)(2,1)}, bf16[384,1536]{1,0:T(8,128)(2,1)S(1)}, u32[]{:S(2)}, u32[]{:S(2)}) collective-permute-start(bf16[384,1536]{1,0:T(8,128)(2,1)} %collective-permute-done.12.refs_7_), channel_id=1, source_target_pairs={{0,1},{1,0},{32,33},{33,32},{64,65},{65,64},{96,97},{97,96},{4,5},... | collective-permute-start | bytes 3538952 | tf_op jit(solution)/shard_map/ppermute | solution.py:39
  119.8 24.2 %collective-permute-start.10 = (bf16[384,1536]{1,0:T(8,128)(2,1)S(1)}, bf16[384,1536]{1,0:T(8,128)(2,1)}, u32[]{:S(2)}, u32[]{:S(2)}) collective-permute-start(bf16[384,1536]{1,0:T(8,128)(2,1)S(1)} %collective-permute-done.5.refs_3_), channel_id=1, source_target_pairs={{0,1},{1,0},{32,33},{33,32},{64,65},{65,64},{96,97},{97,96},{4,5},... | collective-permute-start | bytes 3538952 | tf_op jit(solution)/shard_map/ppermute | solution.py:39
  128.7 15.3 %collective-permute-start.11 = (bf16[384,1536]{1,0:T(8,128)(2,1)}, bf16[384,1536]{1,0:T(8,128)(2,1)}, u32[]{:S(2)}, u32[]{:S(2)}) collective-permute-start(bf16[384,1536]{1,0:T(8,128)(2,1)} %collective-permute-done.9.refs_4_), channel_id=1, source_target_pairs={{0,1},{1,0},{32,33},{33,32},{64,65},{65,64},{96,97},{97,96},{4,5},... | collective-permute-start | bytes 3538952 | tf_op jit(solution)/shard_map/ppermute | solution.py:39
  129.7 14.4 %collective-permute-start.15 = (bf16[384,1536]{1,0:T(8,128)(2,1)}, bf16[384,1536]{1,0:T(8,128)(2,1)}, u32[]{:S(2)}, u32[]{:S(2)}) collective-permute-start(bf16[384,1536]{1,0:T(8,128)(2,1)} %collective-permute-done.14.refs_9_), channel_id=1, source_target_pairs={{0,1},{1,0},{32,33},{33,32},{64,65},{65,64},{96,97},{97,96},{4,5},... | collective-permute-start | bytes 3538952 | tf_op jit(solution)/shard_map/ppermute | solution.py:39
  159.1 28.6 %collective-permute-start.20 = (bf16[512,1536]{1,0:T(8,128)(2,1)}, bf16[512,1536]{1,0:T(8,128)(2,1)S(1)}, u32[]{:S(2)}, u32[]{:S(2)}) collective-permute-start(bf16[512,1536]{1,0:T(8,128)(2,1)} %mlp.7), channel_id=1, source_target_pairs={{0,18},{1,3},{32,50},{33,35},{64,82},{65,67},{96,114},{97,99},{4,2... | collective-permute-start | bytes 4718600 | tf_op jit(solution)/shard_map/ppermute | solution.py:39
  (14 other events, 122.0 us)

commit v3 on v2

--- a/solution.py
+++ b/solution.py
@@ -72,6 +72,10 @@
 
 def whole(space=VMEM):
     return pl.BlockSpec(memory_space=space)
+
+
+def grant(mib):
+    return pltpu.CompilerParams(vmem_limit_bytes=mib * 1024 * 1024)
 
 
 def join_kernel(patches_ref, head_ref, out_ref, sem):
@@ -95,6 +99,7 @@
         out_specs=whole(),
         scratch_shapes=[pltpu.SemaphoreType.DMA],
         cost_estimate=pl.CostEstimate(flops=0, bytes_accessed=4 * rows * channels, transcendentals=0),
+        compiler_params=grant(7),
         name="join",
     )(patches, head)
 
@@ -121,6 +126,7 @@
         out_specs=whole(),
         scratch_shapes=[pltpu.SemaphoreType.DMA((len(sources),))],
         cost_estimate=pl.CostEstimate(flops=0, bytes_accessed=4 * len(sources) * HALF * channels, transcendentals=0),
+        compiler_params=grant(4),
         name="stack",
     )(half, *sources)
 
@@ -167,6 +173,7 @@
         in_specs=[whole(pltpu.SMEM), whole()],
         out_specs=[whole(), whole()],
         scratch_shapes=[VMEM((groups, 8, LANES), jnp.bfloat16)],
+        compiler_params=grant(7),
         name="notes",
     )(place, moved)
 
@@ -249,6 +256,7 @@
         cost_estimate=pl.CostEstimate(
             flops=100 * BAND * TW * channels, bytes_accessed=8 * BAND * TW * channels, transcendentals=0
         ),
+        compiler_params=grant(14),
         name="conv",
     )(grid, edge, left, right, weight, vectors)
 
@@ -338,6 +346,7 @@
         cost_estimate=pl.CostEstimate(
             flops=4 * m * hidden * channels, bytes_accessed=4 * hidden * channels, transcendentals=m * hidden
         ),
+        compiler_params=grant(28),
         name="mlp",
     )(*rows, bias, *pieces, *([acc] if adds else []))
 

time: 193 us -> 163 us (0.84)
  Pallas kernels: 84.4 us -> 51.9 us
  waiting for transfers between devices: 50.8 us -> 56.6 us
  other arithmetic: 7.29 us -> 3.65 us
    pallas_call x4, Pallas kernels: 54.9 us -> 34.4 us  [mlp(): pl.pallas_call(functools.partial(mlp_kernel, plan, line, len(rows), len(p...]
    ppermute x17, waiting for transfers between devices: 42.4 us -> 48.2 us  [send(): return lax.ppermute(value, ('row', 'col'), routes(move))]
    pallas_call x2, Pallas kernels: 18.5 us -> 13.1 us  [conv_norm(): pl.pallas_call(functools.partial(conv_kernel, lower), out_shape=jax.Shape...]
    pallas_call x1, Pallas kernels: 3.9 us -> 0.2 us  [join(): pl.pallas_call(join_kernel, out_shape=jax.ShapeDtypeStruct((rows, channel...]
    unnamed x32 -> x26, local copies, waits for them, and re-layouts: 3.26 us -> 5.71 us
  transfers between devices with their start and end apart: 22 -> 22, of which waited for: 6 -> 7; matrix products, arithmetic and copies ran while one was open for 3% -> 2% of each run, Pallas kernels for 35% -> 26%
where the time goes in v3:
time: 163 us
  waiting for transfers between devices  56.6 us (35%)
  Pallas kernels  51.9 us (32%)
  starting transfers between devices  41.6 us (26%)
  local copies, waits for them, and re-layouts  7.16 us (4%)
  other arithmetic  3.65 us (2%)
    ppermute x17, waiting for transfers between devices, send(): return lax.ppermute(value, ('row', 'col'), routes(move))  48.2 us
    pallas_call x4, Pallas kernels, mlp(): pl.pallas_call(functools.partial(mlp_kernel, plan, line, len(rows), len(p...  34.4 us
    ppermute x17, starting transfers between devices, send(): return lax.ppermute(value, ('row', 'col'), routes(move))  23.4 us
    pallas_call x2, Pallas kernels, conv_norm(): pl.pallas_call(functools.partial(conv_kernel, lower), out_shape=jax.Shape...  13.1 us
    all_to_all x1, starting transfers between devices, local(): lax.all_to_all(join(patches, head), 'col', split_axis=0, concat_axis=0, t...  6.9 us
    unnamed x26, local copies, waits for them, and re-layouts  5.71 us
    ppermute x1, waiting for transfers between devices, halo(): lax.ppermute(head, axis, [(i + 1, i) for i in range(ends)])  5.64 us
    ppermute x1, starting transfers between devices, halo(): lax.ppermute(tail, axis, [(i, i + 1) for i in range(ends)])  4.36 us
  transfers between devices with their start and end apart: 22, of which 7 were waited for; matrix products, arithmetic and copies ran while one was open for 2% of the time, Pallas kernels for 26%

profile of v3, /device:TPU:1, one launch (start us, length us, event | category | flops | bytes accessed | tf_op | source)
XLA Modules:
  0.0 162.8 jit_solution(8974725178054628614)
XLA Ops:
  1.7 1.7 %copy-done.1 = bf16[768,1536]{1,0:T(8,128)(2,1)S(1)} copy-done((bf16[768,1536]{1,0:T(8,128)(2,1)S(1)}, bf16[768,1536]{1,0:T(8,128)(2,1)}, u32[]{:S(2)}) %copy-start.1) | copy-done | bytes 2359320
  5.1 6.9 %all-to-all-start = ((bf16[16,48,1664]{2,1,0:T(8,128)(2,1)}), bf16[16,48,1664]{2,1,0:T(8,128)(2,1)S(1)}, u32[]{:S(2)}, u32[]{:S(2)}) async-start(bf16[16,48,1664]{2,1,0:T(8,128)(2,1)} %bitcast.15), calls=%async_computation | async-start | bytes 5111808 | tf_op jit(solution)/shard_map/all_to_all | solution.py:379
  16.3 2.6 %collective-permute-start.4 = (bf16[384,1536]{1,0:T(8,128)(2,1)}, bf16[384,1536]{1,0:T(8,128)(2,1)}, u32[]{:S(2)}, u32[]{:S(2)}) collective-permute-start(bf16[384,1536]{1,0:T(8,128)(2,1)} %stack.38), channel_id=1, source_target_pairs={{0,4},{1,13},{32,36},{33,45},{64,68},{65,77},{96,100},{97,109},{4,... | collective-permute-start | bytes 3538952 | tf_op jit(solution)/shard_map/ppermute | solution.py:39
  19.2 2.3 %stack.39 = bf16[384,1536]{1,0:T(8,128)(2,1)} custom-call(s32[1]{0:T(128)} %bitcast.5.half_ref, bf16[384,1536]{1,0:T(8,128)(2,1)} %collective-permute-done.6.refs_0_.refs_5_, bf16[384,1536]{1,0:T(8,128)(2,1)} %collective-permute-done.7.refs_1_.refs_6_), custom_call_target="tpu_custom_call" | custom-call | bytes 2359296 | tf_op jit(solution)/shard_map/stack/pallas_call | solution.py:122
  22.1 32.9 %collective-permute-done.4.refs_7_ = bf16[384,1536]{1,0:T(8,128)(2,1)} collective-permute-done((bf16[384,1536]{1,0:T(8,128)(2,1)}, bf16[384,1536]{1,0:T(8,128)(2,1)}, u32[]{:S(2)}, u32[]{:S(2)}) %collective-permute-start.4) | collective-permute-done | bytes 1179680 | tf_op jit(solution)/shard_map/ppermute | solution.py:39
  59.6 4.4 %collective-permute-start = (bf16[3,16,1536]{2,1,0:T(8,128)(2,1)S(1)}, bf16[3,16,1536]{2,1,0:T(8,128)(2,1)S(1)}, u32[]{:S(2)}, u32[]{:S(2)}) collective-permute-start(bf16[3,16,1536]{2,1,0:T(8,128)(2,1)S(1)} %bitcast.17), channel_id=1, source_target_pairs={{0,16},{16,32},{32,48},{48,64},{64,80},{80,96},{96,112},{1,17},{17... | collective-permute-start | bytes 442376 | tf_op jit(solution)/shard_map/ppermute | solution.py:68
  65.6 1.8 %collective-permute-done.edge_ref = bf16[3,16,1536]{2,1,0:T(8,128)(2,1)S(1)} collective-permute-done((bf16[3,16,1536]{2,1,0:T(8,128)(2,1)S(1)}, bf16[3,16,1536]{2,1,0:T(8,128)(2,1)S(1)}, u32[]{:S(2)}, u32[]{:S(2)}) %collective-permute-start) | collective-permute-done | bytes 147488 | tf_op jit(solution)/shard_map/ppermute | solution.py:68
  67.4 5.6 %collective-permute-done.1.edge_ref = bf16[3,16,1536]{2,1,0:T(8,128)(2,1)S(1)} collective-permute-done((bf16[3,16,1536]{2,1,0:T(8,128)(2,1)S(1)}, bf16[3,16,1536]{2,1,0:T(8,128)(2,1)S(1)}, u32[]{:S(2)}, u32[]{:S(2)}) %collective-permute-start.1) | collective-permute-done | bytes 147488 | tf_op jit(solution)/shard_map/ppermute | solution.py:69
  73.4 2.8 %collective-permute-start.3 = (bf16[38,3,1536]{2,1,0:T(4,128)(2,1)S(1)}, bf16[38,3,1536]{2,1,0:T(4,128)(2,1)S(1)}, u32[]{:S(2)}, u32[]{:S(2)}) collective-permute-start(bf16[38,3,1536]{2,1,0:T(4,128)(2,1)S(1)} %pad_maximum_fusion.1), channel_id=1, source_target_pairs={{1,0},{2,1},{3,2},{4,3},{5,4},{6,5},{7,6},{8,7},{9,8},{10,9},{11,1... | collective-permute-start | bytes 1050632 | tf_op jit(solution)/shard_map/ppermute | solution.py:422
  76.6 2.8 %collective-permute-start.2 = (bf16[38,3,1536]{2,1,0:T(4,128)(2,1)S(1)}, bf16[38,3,1536]{2,1,0:T(4,128)(2,1)S(1)}, u32[]{:S(2)}, u32[]{:S(2)}) collective-permute-start(bf16[38,3,1536]{2,1,0:T(4,128)(2,1)S(1)} %pad_maximum_fusion), channel_id=1, source_target_pairs={{0,1},{1,2},{2,3},{3,4},{4,5},{5,6},{6,7},{7,8},{8,9},{9,10},{10,1... | collective-permute-start | bytes 1050632 | tf_op jit(solution)/shard_map/ppermute | solution.py:421
  79.4 3.7 %collective-permute-start.5 = (bf16[384,1536]{1,0:T(8,128)(2,1)}, bf16[384,1536]{1,0:T(8,128)(2,1)S(1)}, u32[]{:S(2)}, u32[]{:S(2)}) collective-permute-start(bf16[384,1536]{1,0:T(8,128)(2,1)} %collective-permute-done.4.refs_7_), channel_id=1, source_target_pairs={{0,32},{1,97},{32,64},{33,1},{64,96},{65,33},{96,0},{97,65},{4,36}... | collective-permute-start | bytes 3538952 | tf_op jit(solution)/shard_map/ppermute | solution.py:39
  84.1 4.6 %collective-permute-start.9 = (bf16[384,1536]{1,0:T(8,128)(2,1)}, bf16[384,1536]{1,0:T(8,128)(2,1)S(1)}, u32[]{:S(2)}, u32[]{:S(2)}) collective-permute-start(bf16[384,1536]{1,0:T(8,128)(2,1)} %collective-permute-done.8.refs_8_), channel_id=1, source_target_pairs={{0,32},{1,97},{32,64},{33,1},{64,96},{65,33},{96,0},{97,65},{4,36}... | collective-permute-start | bytes 3538952 | tf_op jit(solution)/shard_map/ppermute | solution.py:39
  88.7 6.6 %conv.3.refs_1_ = bf16[256,1536]{1,0:T(8,128)(2,1)S(1)} custom-call(bf16[32,16,1536]{2,1,0:T(8,128)(2,1)S(1)} %bitcast.12, bf16[3,16,1536]{2,1,0:T(8,128)(2,1)S(1)} %collective-permute-done.1.edge_ref, bf16[38,3,1536]{2,1,0:T(4,128)(2,1)S(1)} %collective-permute-done.2.left_ref, bf16[38,3,1536]{2,1,0:T(4,128)(2,1)S(1)} %collective-permute-done.3.right_ref, ...), custom_call_target="tpu_custom_call" | custom-call | flops 39321600 | bytes 3145728 | tf_op jit(solution)/shard_map/conv/pallas_call | solution.py:250
  95.3 5.5 %collective-permute-start.19 = (bf16[256,1536]{1,0:T(8,128)(2,1)S(1)}, bf16[256,1536]{1,0:T(8,128)(2,1)S(1)}, u32[]{:S(2)}, u32[]{:S(2)}) collective-permute-start(bf16[256,1536]{1,0:T(8,128)(2,1)S(1)} %conv.3.refs_1_), channel_id=1, source_target_pairs={{0,2},{1,19},{32,34},{33,51},{64,66},{65,83},{96,98},{97,115},{4,6... | collective-permute-start | bytes 2359304 | tf_op jit(solution)/shard_map/ppermute | solution.py:39
  100.9 6.6 %conv.2.refs_0_ = bf16[256,1536]{1,0:T(8,128)(2,1)S(1)} custom-call(bf16[32,16,1536]{2,1,0:T(8,128)(2,1)S(1)} %bitcast.13, bf16[3,16,1536]{2,1,0:T(8,128)(2,1)S(1)} %collective-permute-done.edge_ref, bf16[38,3,1536]{2,1,0:T(4,128)(2,1)S(1)} %collective-permute-done.2.left_ref, bf16[38,3,1536]{2,1,0:T(4,128)(2,1)S(1)} %collective-permute-done.3.right_ref, ...), custom_call_target="tpu_custom_call" | custom-call | flops 39321600 | bytes 3145728 | tf_op jit(solution)/shard_map/conv/pallas_call | solution.py:250
  107.7 1.6 collective-permute-done.9.refs_4_
  110.2 11.8 %collective-permute-done.14.refs_9_ = bf16[384,1536]{1,0:T(8,128)(2,1)S(1)} collective-permute-done((bf16[384,1536]{1,0:T(8,128)(2,1)}, bf16[384,1536]{1,0:T(8,128)(2,1)S(1)}, u32[]{:S(2)}, u32[]{:S(2)}) %collective-permute-start.14) | collective-permute-done | bytes 1179680 | tf_op jit(solution)/shard_map/ppermute | solution.py:39
  122.8 8.5 %mlp.6.refs_11_ = f32[512,1536]{1,0:T(8,128)S(1)} custom-call(bf16[256,1536]{1,0:T(8,128)(2,1)S(1)} %collective-permute-done.18.refs_0_, bf16[256,1536]{1,0:T(8,128)(2,1)S(1)} %collective-permute-done.19.refs_1_, f32[2,1536]{1,0:T(2,128)S(1)} %get-tuple-element.14.refs_2_, bf16[384,1536]{1,0:T(8,128)(2,1)S(1)} %copy-done.4, bf16[384,1536]{1,0:T(8,128)(2,1)S(1)} %copy-done.6, ...), custom_call_target="tpu_custom_call" | custom-call | flops 4831838208 | bytes 9437184 | tf_op jit(solution)/shard_map/mlp/pallas_call | solution.py:333
  131.4 8.7 %mlp.7 = bf16[512,1536]{1,0:T(8,128)(2,1)S(1)} custom-call(bf16[256,1536]{1,0:T(8,128)(2,1)S(1)} %collective-permute-done.18.refs_0_, bf16[256,1536]{1,0:T(8,128)(2,1)S(1)} %collective-permute-done.19.refs_1_, f32[2,1536]{1,0:T(2,128)S(1)} %get-tuple-element.14.refs_2_, bf16[384,1536]{1,0:T(8,128)(2,1)S(1)} %collective-permute-done.5.refs_3_, ...), custom_call_target="tpu_custom_call" | custom-call | flops 4831838208 | bytes 9437184 | tf_op jit(solution)/shard_map/mlp/pallas_call | solution.py:333
  140.1 1.6 collective-permute-start.20
  141.7 8.5 %mlp.4.refs_11_ = f32[512,1536]{1,0:T(8,128)S(1)} custom-call(bf16[256,1536]{1,0:T(8,128)(2,1)S(1)} %conv.2.refs_0_, bf16[256,1536]{1,0:T(8,128)(2,1)S(1)} %conv.3.refs_1_, f32[2,1536]{1,0:T(2,128)S(1)} %get-tuple-element.14.refs_2_, bf16[384,1536]{1,0:T(8,128)(2,1)S(1)} %copy-done.4, bf16[384,1536]{1,0:T(8,128)(2,1)S(1)} %copy-done.6, ...), custom_call_target="tpu_custom_call" | custom-call | flops 4831838208 | bytes 9437184 | tf_op jit(solution)/shard_map/mlp/pallas_call | solution.py:333
  150.2 8.7 %mlp.5 = f32[512,1536]{1,0:T(8,128)S(1)} custom-call(bf16[256,1536]{1,0:T(8,128)(2,1)S(1)} %conv.2.refs_0_, bf16[256,1536]{1,0:T(8,128)(2,1)S(1)} %conv.3.refs_1_, f32[2,1536]{1,0:T(2,128)S(1)} %get-tuple-element.14.refs_2_, bf16[384,1536]{1,0:T(8,128)(2,1)S(1)} %collective-permute-done.5.refs_3_, bf16[384,1536]{1,0:T(8,128)(2,1)S(1)} %collective-permute-done.9.refs_4_, ...), custom_call_target="tpu_custom_call" | custom-call | flops 4831838208 | bytes 9437184 | tf_op jit(solution)/shard_map/mlp/pallas_call | solution.py:333
  158.9 1.9 %collective-permute-done.20 = bf16[512,1536]{1,0:T(8,128)(2,1)S(1)} collective-permute-done((bf16[512,1536]{1,0:T(8,128)(2,1)S(1)}, bf16[512,1536]{1,0:T(8,128)(2,1)S(1)}, u32[]{:S(2)}, u32[]{:S(2)}) %collective-permute-start.20) | collective-permute-done | bytes 1572896 | tf_op jit(solution)/shard_map/ppermute | solution.py:39
  160.9 1.9 %add_convert_fusion = bf16[512,1536]{1,0:T(8,128)(2,1)} fusion(f32[512,1536]{1,0:T(8,128)S(1)} %mlp.5, bf16[512,1536]{1,0:T(8,128)(2,1)S(1)} %collective-permute-done.20, bf16[512,1536]{1,0:T(8,128)(2,1)S(1)} %fusion, f32[1536]{0:T(1024)S(1)} %copy-done.10, f32[1536]{0:T(1024)S(1)} %copy-done.11), kind=kLoop, calls=%fused_computation.1 | loop fusion | flops 5505024 | bytes 7876608 | tf_op jit(solution)/shard_map/convert_element_type | solution.py:435
  (79 shorter events, 18.3 us)
Async XLA Ops:
  5.1 52.1 %all-to-all-start = ((bf16[16,48,1664]{2,1,0:T(8,128)(2,1)}), bf16[16,48,1664]{2,1,0:T(8,128)(2,1)S(1)}, u32[]{:S(2)}, u32[]{:S(2)}) async-start(bf16[16,48,1664]{2,1,0:T(8,128)(2,1)} %bitcast.15), calls=%async_computation | async-start | bytes 5111808 | tf_op jit(solution)/shard_map/all_to_all | solution.py:379
  12.0 7.2 %collective-permute-start.6 = (bf16[384,1536]{1,0:T(8,128)(2,1)}, bf16[384,1536]{1,0:T(8,128)(2,1)}, u32[]{:S(2)}, u32[]{:S(2)}) collective-permute-start(bf16[384,1536]{1,0:T(8,128)(2,1)} %refs_3_.3), channel_id=1, source_target_pairs={{0,1},{1,0},{32,33},{33,32},{64,65},{65,64},{96,97},{97,96},{4,5},... | collective-permute-start | bytes 3538952 | tf_op jit(solution)/shard_map/ppermute | solution.py:39
  12.2 7.0 %collective-permute-start.7 = (bf16[384,1536]{1,0:T(8,128)(2,1)}, bf16[384,1536]{1,0:T(8,128)(2,1)}, u32[]{:S(2)}, u32[]{:S(2)}) collective-permute-start(bf16[384,1536]{1,0:T(8,128)(2,1)} %refs_4_.3), channel_id=1, source_target_pairs={{0,1},{1,0},{32,33},{33,32},{64,65},{65,64},{96,97},{97,96},{4,5},... | collective-permute-start | bytes 3538952 | tf_op jit(solution)/shard_map/ppermute | solution.py:39
  16.3 38.6 %collective-permute-start.4 = (bf16[384,1536]{1,0:T(8,128)(2,1)}, bf16[384,1536]{1,0:T(8,128)(2,1)}, u32[]{:S(2)}, u32[]{:S(2)}) collective-permute-start(bf16[384,1536]{1,0:T(8,128)(2,1)} %stack.38), channel_id=1, source_target_pairs={{0,4},{1,13},{32,36},{33,45},{64,68},{65,77},{96,100},{97,109},{4,... | collective-permute-start | bytes 3538952 | tf_op jit(solution)/shard_map/ppermute | solution.py:39
  21.4 36.7 %copy-start.12 = (bf16[1536]{0:T(1024)(128)(2,1)S(1)}, bf16[1536]{0:T(1024)(128)(2,1)}, u32[]{:S(2)}) copy-start(bf16[1536]{0:T(1024)(128)(2,1)} %param.14) | copy-start | bytes 9220
  21.5 58.0 %collective-permute-start.8 = (bf16[384,1536]{1,0:T(8,128)(2,1)}, bf16[384,1536]{1,0:T(8,128)(2,1)}, u32[]{:S(2)}, u32[]{:S(2)}) collective-permute-start(bf16[384,1536]{1,0:T(8,128)(2,1)} %stack.39), channel_id=1, source_target_pairs={{0,4},{1,13},{32,36},{33,45},{64,68},{65,77},{96,100},{97,109},{4,... | collective-permute-start | bytes 3538952 | tf_op jit(solution)/shard_map/ppermute | solution.py:39
  55.0 40.4 %collective-permute-start.16 = (bf16[384,1536]{1,0:T(8,128)(2,1)}, bf16[384,1536]{1,0:T(8,128)(2,1)}, u32[]{:S(2)}, u32[]{:S(2)}) collective-permute-start(bf16[384,1536]{1,0:T(8,128)(2,1)} %collective-permute-done.4.refs_7_), channel_id=1, source_target_pairs={{0,1},{1,0},{32,33},{33,32},{64,65},{65,64},{96,97},{97,96},{4,5},... | collective-permute-start | bytes 3538952 | tf_op jit(solution)/shard_map/ppermute | solution.py:39
  56.5 26.7 %collective-permute-start.12 = (bf16[384,1536]{1,0:T(8,128)(2,1)}, bf16[384,1536]{1,0:T(8,128)(2,1)}, u32[]{:S(2)}, u32[]{:S(2)}) collective-permute-start(bf16[384,1536]{1,0:T(8,128)(2,1)} %collective-permute-done.4.refs_7_), channel_id=1, source_target_pairs={{0,4},{1,13},{32,36},{33,45},{64,68},{65,77},{96,100},{97,109},{4,... | collective-permute-start | bytes 3538952 | tf_op jit(solution)/shard_map/ppermute | solution.py:39
  59.6 7.8 %collective-permute-start = (bf16[3,16,1536]{2,1,0:T(8,128)(2,1)S(1)}, bf16[3,16,1536]{2,1,0:T(8,128)(2,1)S(1)}, u32[]{:S(2)}, u32[]{:S(2)}) collective-permute-start(bf16[3,16,1536]{2,1,0:T(8,128)(2,1)S(1)} %bitcast.17), channel_id=1, source_target_pairs={{0,16},{16,32},{32,48},{48,64},{64,80},{80,96},{96,112},{1,17},{17... | collective-permute-start | bytes 442376 | tf_op jit(solution)/shard_map/ppermute | solution.py:68
  64.3 8.8 %collective-permute-start.1 = (bf16[3,16,1536]{2,1,0:T(8,128)(2,1)S(1)}, bf16[3,16,1536]{2,1,0:T(8,128)(2,1)S(1)}, u32[]{:S(2)}, u32[]{:S(2)}) collective-permute-start(bf16[3,16,1536]{2,1,0:T(8,128)(2,1)S(1)} %bitcast.16), channel_id=1, source_target_pairs={{16,0},{32,16},{48,32},{64,48},{80,64},{96,80},{112,96},{17,1},{33... | collective-permute-start | bytes 442376 | tf_op jit(solution)/shard_map/ppermute | solution.py:69
  73.4 10.7 %collective-permute-start.3 = (bf16[38,3,1536]{2,1,0:T(4,128)(2,1)S(1)}, bf16[38,3,1536]{2,1,0:T(4,128)(2,1)S(1)}, u32[]{:S(2)}, u32[]{:S(2)}) collective-permute-start(bf16[38,3,1536]{2,1,0:T(4,128)(2,1)S(1)} %pad_maximum_fusion.1), channel_id=1, source_target_pairs={{1,0},{2,1},{3,2},{4,3},{5,4},{6,5},{7,6},{8,7},{9,8},{10,9},{11,1... | collective-permute-start | bytes 1050632 | tf_op jit(solution)/shard_map/ppermute | solution.py:422
  76.6 12.2 %collective-permute-start.2 = (bf16[38,3,1536]{2,1,0:T(4,128)(2,1)S(1)}, bf16[38,3,1536]{2,1,0:T(4,128)(2,1)S(1)}, u32[]{:S(2)}, u32[]{:S(2)}) collective-permute-start(bf16[38,3,1536]{2,1,0:T(4,128)(2,1)S(1)} %pad_maximum_fusion), channel_id=1, source_target_pairs={{0,1},{1,2},{2,3},{3,4},{4,5},{5,6},{6,7},{7,8},{8,9},{9,10},{10,1... | collective-permute-start | bytes 1050632 | tf_op jit(solution)/shard_map/ppermute | solution.py:421
  79.4 28.0 %collective-permute-start.5 = (bf16[384,1536]{1,0:T(8,128)(2,1)}, bf16[384,1536]{1,0:T(8,128)(2,1)S(1)}, u32[]{:S(2)}, u32[]{:S(2)}) collective-permute-start(bf16[384,1536]{1,0:T(8,128)(2,1)} %collective-permute-done.4.refs_7_), channel_id=1, source_target_pairs={{0,32},{1,97},{32,64},{33,1},{64,96},{65,33},{96,0},{97,65},{4,36}... | collective-permute-start | bytes 3538952 | tf_op jit(solution)/shard_map/ppermute | solution.py:39
  83.2 24.4 %collective-permute-start.17 = (bf16[384,1536]{1,0:T(8,128)(2,1)}, bf16[384,1536]{1,0:T(8,128)(2,1)S(1)}, u32[]{:S(2)}, u32[]{:S(2)}) collective-permute-start(bf16[384,1536]{1,0:T(8,128)(2,1)} %collective-permute-done.8.refs_8_), channel_id=1, source_target_pairs={{0,1},{1,0},{32,33},{33,32},{64,65},{65,64},{96,97},{97,96},{4,5},... | collective-permute-start | bytes 3538952 | tf_op jit(solution)/shard_map/ppermute | solution.py:39
  84.1 25.1 %collective-permute-start.9 = (bf16[384,1536]{1,0:T(8,128)(2,1)}, bf16[384,1536]{1,0:T(8,128)(2,1)S(1)}, u32[]{:S(2)}, u32[]{:S(2)}) collective-permute-start(bf16[384,1536]{1,0:T(8,128)(2,1)} %collective-permute-done.8.refs_8_), channel_id=1, source_target_pairs={{0,32},{1,97},{32,64},{33,1},{64,96},{65,33},{96,0},{97,65},{4,36}... | collective-permute-start | bytes 3538952 | tf_op jit(solution)/shard_map/ppermute | solution.py:39
  88.7 33.2 %collective-permute-start.14 = (bf16[384,1536]{1,0:T(8,128)(2,1)}, bf16[384,1536]{1,0:T(8,128)(2,1)S(1)}, u32[]{:S(2)}, u32[]{:S(2)}) collective-permute-start(bf16[384,1536]{1,0:T(8,128)(2,1)} %collective-permute-done.12.refs_7_), channel_id=1, source_target_pairs={{0,32},{1,97},{32,64},{33,1},{64,96},{65,33},{96,0},{97,65},{4,36}... | collective-permute-start | bytes 3538952 | tf_op jit(solution)/shard_map/ppermute | solution.py:39
  95.3 27.5 %copy-start.4 = (bf16[384,1536]{1,0:T(8,128)(2,1)S(1)}, bf16[384,1536]{1,0:T(8,128)(2,1)}, u32[]{:S(2)}) copy-start(bf16[384,1536]{1,0:T(8,128)(2,1)} %refs_3_.3) | copy-start | bytes 3538948
  95.3 27.5 %collective-permute-start.19 = (bf16[256,1536]{1,0:T(8,128)(2,1)S(1)}, bf16[256,1536]{1,0:T(8,128)(2,1)S(1)}, u32[]{:S(2)}, u32[]{:S(2)}) collective-permute-start(bf16[256,1536]{1,0:T(8,128)(2,1)S(1)} %conv.3.refs_1_), channel_id=1, source_target_pairs={{0,2},{1,19},{32,34},{33,51},{64,66},{65,83},{96,98},{97,115},{4,6... | collective-permute-start | bytes 2359304 | tf_op jit(solution)/shard_map/ppermute | solution.py:39
  107.5 15.3 %collective-permute-start.18 = (bf16[256,1536]{1,0:T(8,128)(2,1)S(1)}, bf16[256,1536]{1,0:T(8,128)(2,1)S(1)}, u32[]{:S(2)}, u32[]{:S(2)}) collective-permute-start(bf16[256,1536]{1,0:T(8,128)(2,1)S(1)} %conv.2.refs_0_), channel_id=1, source_target_pairs={{0,2},{1,19},{32,34},{33,51},{64,66},{65,83},{96,98},{97,115},{4,6... | collective-permute-start | bytes 2359304 | tf_op jit(solution)/shard_map/ppermute | solution.py:39
  107.6 23.8 %collective-permute-start.13 = (bf16[384,1536]{1,0:T(8,128)(2,1)}, bf16[384,1536]{1,0:T(8,128)(2,1)S(1)}, u32[]{:S(2)}, u32[]{:S(2)}) collective-permute-start(bf16[384,1536]{1,0:T(8,128)(2,1)} %collective-permute-done.12.refs_7_), channel_id=1, source_target_pairs={{0,1},{1,0},{32,33},{33,32},{64,65},{65,64},{96,97},{97,96},{4,5},... | collective-permute-start | bytes 3538952 | tf_op jit(solution)/shard_map/ppermute | solution.py:39
  109.3 22.1 %collective-permute-start.10 = (bf16[384,1536]{1,0:T(8,128)(2,1)S(1)}, bf16[384,1536]{1,0:T(8,128)(2,1)S(1)}, u32[]{:S(2)}, u32[]{:S(2)}) collective-permute-start(bf16[384,1536]{1,0:T(8,128)(2,1)S(1)} %collective-permute-done.5.refs_3_), channel_id=1, source_target_pairs={{0,1},{1,0},{32,33},{33,32},{64,65},{65,64},{96,97},{97,96},{4,5},... | collective-permute-start | bytes 3538952 | tf_op jit(solution)/shard_map/ppermute | solution.py:39
  121.9 9.4 %collective-permute-start.11 = (bf16[384,1536]{1,0:T(8,128)(2,1)S(1)}, bf16[384,1536]{1,0:T(8,128)(2,1)S(1)}, u32[]{:S(2)}, u32[]{:S(2)}) collective-permute-start(bf16[384,1536]{1,0:T(8,128)(2,1)S(1)} %collective-permute-done.9.refs_4_), channel_id=1, source_target_pairs={{0,1},{1,0},{32,33},{33,32},{64,65},{65,64},{96,97},{97,96},{4,5},... | collective-permute-start | bytes 3538952 | tf_op jit(solution)/shard_map/ppermute | solution.py:39
  122.8 8.6 %collective-permute-start.15 = (bf16[384,1536]{1,0:T(8,128)(2,1)S(1)}, bf16[384,1536]{1,0:T(8,128)(2,1)S(1)}, u32[]{:S(2)}, u32[]{:S(2)}) collective-permute-start(bf16[384,1536]{1,0:T(8,128)(2,1)S(1)} %collective-permute-done.14.refs_9_), channel_id=1, source_target_pairs={{0,1},{1,0},{32,33},{33,32},{64,65},{65,64},{96,97},{97,96},{4,5},... | collective-permute-start | bytes 3538952 | tf_op jit(solution)/shard_map/ppermute | solution.py:39
  140.1 20.8 %collective-permute-start.20 = (bf16[512,1536]{1,0:T(8,128)(2,1)S(1)}, bf16[512,1536]{1,0:T(8,128)(2,1)S(1)}, u32[]{:S(2)}, u32[]{:S(2)}) collective-permute-start(bf16[512,1536]{1,0:T(8,128)(2,1)S(1)} %mlp.7), channel_id=1, source_target_pairs={{0,18},{1,3},{32,50},{33,35},{64,82},{65,67},{96,114},{97,99},{4,2... | collective-permute-start | bytes 4718600 | tf_op jit(solution)/shard_map/ppermute | solution.py:39
  (11 other events, 91.2 us)

commit v4 on v3

--- a/solution.py
+++ b/solution.py
@@ -13,8 +13,9 @@
 SHARD = 384
 HALF = SHARD // 2
 LANES = 128
-BAND = TH // 2
-PAIRS = BAND // 2
+HALO = 3
+MIDDLE = ((8, 16),)
+EDGES = ((0, 8), (24, 8))
 UNITS = 256
 
 VMEM = pltpu.VMEM
@@ -59,15 +60,10 @@
     return x - 1 + 2 * core, y, z, core
 
 
-def halo(cells, axis, dim, width):
-    count = lax.axis_size(axis)
-    ends = count - 1
-    head = lax.slice_in_dim(cells, 0, width, axis=dim)
-    tail = lax.slice_in_dim(cells, cells.shape[dim] - width, cells.shape[dim], axis=dim)
-    return (
-        lax.ppermute(tail, axis, [(i, i + 1) for i in range(ends)]),
-        lax.ppermute(head, axis, [(i + 1, i) for i in range(ends)]),
-    )
+def shift(value, axis, step):
+    last = lax.axis_size(axis) - 1
+    pairs = [(i, i + 1) if step > 0 else (i + 1, i) for i in range(last)]
+    return lax.ppermute(value, axis, pairs)
 
 
 def whole(space=VMEM):
@@ -178,51 +174,56 @@
     )(place, moved)
 
 
-def conv_kernel(lower, grid_ref, edge_ref, left_ref, right_ref, weight_ref, vector_ref, out_ref, even, odd, both, conv):
+def conv_kernel(bands, *refs):
+    grid_ref, left_ref, right_ref, weight_ref, vector_ref = refs[:5]
+    out_ref, even, odd, both, conv = refs[-5:]
     channels = grid_ref.shape[2]
     tiles = channels // LANES
-    count = PAIRS + 3
+    spans = (slice(5, 8), slice(8, 24), slice(24, 27))
 
     def tile(t, carry):
         at = pl.ds(pl.multiple_of(t * LANES, LANES), LANES)
 
         def row(k):
-            if lower:
-                inside = k < BAND + 3
-                middle = grid_ref[TH - BAND - 3 + k, :, at] if inside else edge_ref[k - BAND - 3, :, at]
-                side = TH - BAND + k
+            if 0 <= k < TH:
+                parts = (left_ref[k, :, at], grid_ref[k, :, at], right_ref[k, :, at])
             else:
-                middle = edge_ref[k, :, at] if k < 3 else grid_ref[k - 3, :, at]
-                side = k
-            parts = (left_ref[side, :, at], middle, right_ref[side, :, at])
+                edge, k = (refs[5], k + HALO) if k < 0 else (refs[6], k - TH)
+                parts = (edge[k, TW : TW + HALO, at], edge[k, :TW, at], edge[k, TW + HALO :, at])
             return [part.astype(jnp.float32) for part in parts]
 
-        spans = (slice(5, 8), slice(8, 24), slice(24, 27))
-        for k in range(count):
-            for span, e, o in zip(spans, row(2 * k), row(2 * k + 1)):
-                even[k, span, :] = e
-                odd[k, span, :] = o
-                both[k, span, :] = e + o
+        base = jnp.broadcast_to(vector_ref[0:1, at], (TW, LANES))
         zero = jnp.zeros((TW, LANES), jnp.float32)
-        p, q, s = [zero] * PAIRS, [zero] * (PAIRS + 1), [zero] * PAIRS
-        for along in range(7):
-            h = [weight_ref[across, along : along + 1, at] for across in range(7)]
-            mixed = [h[0]] + [h[2 * j] + h[2 * j - 1] for j in range(1, 4)]
-            h, mixed = [[jnp.broadcast_to(v, (TW, LANES)) for v in group] for group in (h, mixed)]
-            cols = slice(5 + along, 5 + along + TW)
+        slot, line = 0, 0
+        for start, size in bands:
+            pairs = size // 2
+            count = pairs + HALO
             for k in range(count):
-                e, o, b = even[k, cols, :], odd[k, cols, :], both[k, cols, :]
-                for j in range(4):
-                    if 0 <= k - j < PAIRS:
-                        p[k - j] = p[k - j] + e * h[2 * j]
-                        s[k - j] = s[k - j] + b * mixed[j]
-                for j in range(3):
-                    if 0 <= k - j <= PAIRS:
-                        q[k - j] = q[k - j] + o * h[2 * j + 1]
-        base = jnp.broadcast_to(vector_ref[0:1, at], (TW, LANES))
-        for k in range(PAIRS):
-            conv[t, 2 * k * TW : (2 * k + 1) * TW, :] = p[k] + q[k] + base
-            conv[t, (2 * k + 1) * TW : (2 * k + 2) * TW, :] = s[k] - p[k] - q[k + 1] + base
+                top = start - HALO + 2 * k
+                for span, e, o in zip(spans, row(top), row(top + 1)):
+                    even[slot + k, span, :] = e
+                    odd[slot + k, span, :] = o
+                    both[slot + k, span, :] = e + o
+            p, q, s = [zero] * pairs, [zero] * (pairs + 1), [zero] * pairs
+            for along in range(7):
+                h = [weight_ref[across, along : along + 1, at] for across in range(7)]
+                mixed = [h[0]] + [h[2 * j] + h[2 * j - 1] for j in range(1, 4)]
+                h, mixed = [[jnp.broadcast_to(v, (TW, LANES)) for v in group] for group in (h, mixed)]
+                cols = slice(5 + along, 5 + along + TW)
+                for k in range(count):
+                    e, o, b = [ref[slot + k, cols, :] for ref in (even, odd, both)]
+                    for j in range(4):
+                        if 0 <= k - j < pairs:
+                            p[k - j] = p[k - j] + e * h[2 * j]
+                            s[k - j] = s[k - j] + b * mixed[j]
+                    for j in range(3):
+                        if 0 <= k - j <= pairs:
+                            q[k - j] = q[k - j] + o * h[2 * j + 1]
+            for k in range(pairs):
+                conv[t, line : line + TW, :] = p[k] + q[k] + base
+                conv[t, line + TW : line + 2 * TW, :] = s[k] - p[k] - q[k + 1] + base
+                line += 2 * TW
+            slot += count
         return carry
 
     lax.fori_loop(0, tiles, tile, 0)
@@ -241,24 +242,25 @@
             )
         return carry
 
-    lax.fori_loop(0, BAND * TW // 16, norm, 0, unroll=2)
-
-
-def conv_norm(lower, grid, edge, left, right, weight, vectors):
+    lax.fori_loop(0, out_ref.shape[0] // 16, norm, 0, unroll=2)
+
+
+def conv_norm(bands, grid, left, right, weight, vectors, *edges):
     channels = grid.shape[2]
-    stage = VMEM((PAIRS + 3, 32, LANES), jnp.float32)
+    rows = sum(size for _, size in bands)
+    stage = VMEM((sum(size // 2 + HALO for _, size in bands), 32, LANES), jnp.float32)
     return pl.pallas_call(
-        functools.partial(conv_kernel, lower),
-        out_shape=jax.ShapeDtypeStruct((BAND * TW, channels), jnp.bfloat16),
-        in_specs=[whole()] * 6,
+        functools.partial(conv_kernel, bands),
+        out_shape=jax.ShapeDtypeStruct((rows * TW, channels), jnp.bfloat16),
+        in_specs=[whole()] * (5 + len(edges)),
         out_specs=whole(),
-        scratch_shapes=[stage, stage, stage, VMEM((channels // LANES, BAND * TW, LANES), jnp.float32)],
+        scratch_shapes=[stage, stage, stage, VMEM((channels // LANES, rows * TW, LANES), jnp.float32)],
         cost_estimate=pl.CostEstimate(
-            flops=100 * BAND * TW * channels, bytes_accessed=8 * BAND * TW * channels, transcendentals=0
+            flops=100 * rows * TW * channels, bytes_accessed=8 * rows * TW * channels, transcendentals=0
         ),
         compiler_params=grant(14),
         name="conv",
-    )(grid, edge, left, right, weight, vectors)
+    )(grid, left, right, weight, vectors, *edges)
 
 
 PHI = (
@@ -276,7 +278,7 @@
     return half + half * jnp.tanh(pre * p)
 
 
-def mlp_kernel(plan, line, bands, count, adds, *refs):
+def mlp_kernel(plan, bias_at, bands, count, adds, *refs):
     rows_refs, bias_ref = refs[:bands], refs[bands]
     pieces = refs[bands + 1 : bands + 1 + count]
     acc_ref = refs[bands + 1 + count] if adds else None
@@ -288,11 +290,14 @@
         ins.append(pltpu.make_async_copy(pieces[a].at[pl.ds(row_a, size)], w_in.at[pl.ds(at, size)], sems.at[k, 0]))
         outs.append(pltpu.make_async_copy(pieces[b].at[pl.ds(row_b, size)], w_out.at[pl.ds(at, size)], sems.at[k, 1]))
         at += size
-    step = rows.shape[0] // bands
-    moves = [
-        pltpu.make_async_copy(ref, rows.at[pl.ds(k * step, step)], row_sems.at[k]) for k, ref in enumerate(rows_refs)
-    ]
-    early = next(k for k in range(len(plan) + 1) if sum(p[4] for p in plan[:k]) >= 3 * UNITS)
+    moves = []
+    for ref, group in zip(rows_refs, (MIDDLE, EDGES)):
+        line = 0
+        for start, size in group:
+            source, target = ref.at[pl.ds(line * TW, size * TW)], rows.at[pl.ds(start * TW, size * TW)]
+            moves.append(pltpu.make_async_copy(source, target, row_sems.at[len(moves)]))
+            line += size
+    early = next(k for k in range(len(plan) + 1) if sum(p[4] for p in plan[:k]) >= blocks // 2 * UNITS)
     for copy in moves + ins + outs:
         copy.start()
     for copy in moves + ins[:early]:
@@ -306,7 +311,7 @@
 
     def middle(h, pre):
         at = slice(h * UNITS, (h + 1) * UNITS)
-        hid[:, at] = gelu(pre + bias_ref[line : line + 1, at]).astype(jnp.bfloat16)
+        hid[:, at] = gelu(pre + bias_ref[bias_at[0] : bias_at[0] + 1, bias_at[1] + h * UNITS : bias_at[1] + (h + 1) * UNITS]).astype(jnp.bfloat16)
 
     waiting = None
     for h in range(blocks):
@@ -326,12 +331,12 @@
         out_ref[:, at] = total.astype(out_ref.dtype)
 
 
-def mlp(rows, bias, line, pieces, plan, acc=None, out_dtype=jnp.float32):
+def mlp(rows, bias, bias_at, pieces, plan, acc=None, out_dtype=jnp.float32):
     m, channels = sum(part.shape[0] for part in rows), rows[0].shape[1]
     hidden = sum(p[4] for p in plan)
     adds = acc is not None
     return pl.pallas_call(
-        functools.partial(mlp_kernel, plan, line, len(rows), len(pieces), int(adds)),
+        functools.partial(mlp_kernel, plan, bias_at, len(rows), len(pieces), int(adds)),
         out_shape=jax.ShapeDtypeStruct((m, channels), out_dtype),
         in_specs=[whole(pl.ANY)] * len(rows) + [whole()] + [whole(pl.ANY)] * len(pieces) + [whole()] * adds,
         out_specs=whole(),
@@ -341,7 +346,7 @@
             VMEM((hidden, channels), jnp.bfloat16),
             VMEM((m, hidden), jnp.bfloat16),
             pltpu.SemaphoreType.DMA((len(plan), 2)),
-            pltpu.SemaphoreType.DMA((len(rows),)),
+            pltpu.SemaphoreType.DMA((len(MIDDLE + EDGES),)),
         ],
         cost_estimate=pl.CostEstimate(
             flops=4 * m * hidden * channels, bytes_accessed=4 * hidden * channels, transcendentals=m * hidden
@@ -395,8 +400,11 @@
 
     early = (w_in, w_out, w_in_p, w_out_p, near_a, near_b, near_a_p, near_b_p)
     early_plan = ((0, 0, 1, 0, SHARD), (2, 0, 3, 0, SHARD)) + tuple((a, 0, a, HALF, HALF) for a in range(4, 8))
-    late = (near_a_z, near_b_z, near_a_zp, near_b_zp, far, far_p, far_z, far_zp)
-    late_plan = tuple((a, 0, a, HALF, HALF) for a in range(8))
+    mid = (near_a_z, near_b_z, near_a_zp, near_b_zp)
+    late = (far, far_p, far_z, far_zp)
+
+    def halves(count):
+        return tuple((a, 0, a, HALF, HALF) for a in range(count))
 
     place = jnp.stack([my_y, my_lo, my_core, my_h]).astype(jnp.int32)
     vectors = jnp.stack([conv_bias, norm_gain, norm_bias])
@@ -412,24 +420,23 @@
         jnp.bfloat16
     )
     block = grid.reshape(TH, TW, channels)
-    top, bottom = halo(block, "row", 0, 3)
-    tall = [
-        jnp.concatenate([part[:, cut] for part in (top, block, bottom)], axis=0)
-        for cut in (slice(TW - 3, TW), slice(0, 3))
+    left = shift(block[:, TW - HALO :], "col", 1)
+    right = shift(block[:, :HALO], "col", -1)
+    top, bottom = [
+        shift(jnp.concatenate([part[cut] for part in (block, left, right)], axis=1), "row", step)
+        for cut, step in ((slice(TH - HALO, TH), 1), (slice(0, HALO), -1))
     ]
-    ends = lax.axis_size("col") - 1
-    left = lax.ppermute(tall[0], "col", [(i, i + 1) for i in range(ends)])
-    right = lax.ppermute(tall[1], "col", [(i + 1, i) for i in range(ends)])
-    flat_a = conv_norm(False, block, top, left, right, conv_weight, vectors)
-    flat_b = conv_norm(True, block, bottom, left, right, conv_weight, vectors)
+    flat_a = conv_norm(MIDDLE, block, left, right, conv_weight, vectors)
+    flat_b = conv_norm(EDGES, block, left, right, conv_weight, vectors, top, bottom)
 
     flat = (flat_a, flat_b)
     other = (send(flat_a, along_x), send(flat_b, along_x))
-    mine = mlp(flat, bias, 0, early, early_plan)
-    theirs = mlp(other, bias, 0, early, early_plan)
-    theirs = mlp(other, bias, 1, late, late_plan, acc=theirs, out_dtype=jnp.bfloat16)
+    mine = mlp(flat, bias, (0, 0), early, early_plan)
+    theirs = mlp(other, bias, (0, 0), early, early_plan)
+    theirs = mlp(other, bias, (1, 0), mid, halves(4), acc=theirs)
+    theirs = mlp(other, bias, (1, 4 * HALF), late, halves(4), acc=theirs, out_dtype=jnp.bfloat16)
     returned = send(theirs, back_x)
-    mine = mlp(flat, bias, 1, late, late_plan, acc=mine)
+    mine = mlp(flat, bias, (1, 0), mid + late, halves(8), acc=mine)
     mixed = mine + returned.astype(jnp.float32)
     result = grid.astype(jnp.float32) + layer_scale * (mixed + b_out)
     return result.astype(jnp.bfloat16).reshape(TH, TW, channels)

time: 163 us -> 175 us (1.074)
  waiting for transfers between devices: 56.6 us -> 65.8 us
  Pallas kernels: 51.9 us -> 56 us
  starting transfers between devices: 41.6 us -> 39.7 us
    ppermute x4, waiting for transfers between devices: 8.39 us -> 16 us  [shift(): return lax.ppermute(value, axis, pairs)]
    pallas_call x6 -> x7, Pallas kernels: 47.5 us -> 51.5 us  [the longest x5 38.2 us: mlp(): pl.pallas_call(functools.partial(mlp_kernel, plan, bias_at, len(rows), le...]
    ppermute x17, starting transfers between devices: 23.4 us -> 21.4 us  [send(): return lax.ppermute(value, ('row', 'col'), routes(move))]
  transfers between devices with their start and end apart: 22 -> 22, of which waited for: 7 -> 8; matrix products, arithmetic and copies ran while one was open for 2% -> 1% of each run, Pallas kernels for 26% -> 29%
where the time goes in v4:
time: 175 us; the launch traced here: 174 us
  waiting for transfers between devices  65.8 us (38%)
  Pallas kernels  56 us (32%)
  starting transfers between devices  39.7 us (23%)
  local copies, waits for them, and re-layouts  7.16 us (4%)
  other arithmetic  3.07 us (2%)
    ppermute x17, waiting for transfers between devices, send(): return lax.ppermute(value, ('row', 'col'), routes(move))  49.8 us
    pallas_call x5, Pallas kernels, mlp(): pl.pallas_call(functools.partial(mlp_kernel, plan, bias_at, len(rows), le...  38.2 us
    ppermute x17, starting transfers between devices, send(): return lax.ppermute(value, ('row', 'col'), routes(move))  21.4 us
    ppermute x4, waiting for transfers between devices, shift(): return lax.ppermute(value, axis, pairs)  16 us
    pallas_call x2, Pallas kernels, conv_norm(): pl.pallas_call(functools.partial(conv_kernel, bands), out_shape=jax.Shape...  13.3 us
    ppermute x4, starting transfers between devices, shift(): return lax.ppermute(value, axis, pairs)  11.4 us
    all_to_all x1, starting transfers between devices, local(): lax.all_to_all(join(patches, head), 'col', split_axis=0, concat_axis=0, t...  6.9 us
    unnamed x26, local copies, waits for them, and re-layouts  5.72 us
  transfers between devices with their start and end apart: 22, of which 8 were waited for; matrix products, arithmetic and copies ran while one was open for 1% of the time, Pallas kernels for 29%

profile of v4, /device:TPU:1, one launch (start us, length us, event | category | flops | bytes accessed | tf_op | source)
XLA Modules:
  0.0 173.6 jit_solution(3781979864391089790)
XLA Ops:
  5.1 6.9 %all-to-all-start = ((bf16[16,48,1664]{2,1,0:T(8,128)(2,1)}), bf16[16,48,1664]{2,1,0:T(8,128)(2,1)S(1)}, u32[]{:S(2)}, u32[]{:S(2)}) async-start(bf16[16,48,1664]{2,1,0:T(8,128)(2,1)} %bitcast.15), calls=%async_computation | async-start | bytes 5111808 | tf_op jit(solution)/shard_map/all_to_all | solution.py:384
  16.3 2.6 %collective-permute-start.4 = (bf16[384,1536]{1,0:T(8,128)(2,1)}, bf16[384,1536]{1,0:T(8,128)(2,1)}, u32[]{:S(2)}, u32[]{:S(2)}) collective-permute-start(bf16[384,1536]{1,0:T(8,128)(2,1)} %stack.38), channel_id=1, source_target_pairs={{0,4},{1,13},{32,36},{33,45},{64,68},{65,77},{96,100},{97,109},{4,... | collective-permute-start | bytes 3538952 | tf_op jit(solution)/shard_map/ppermute | solution.py:40
  19.0 2.4 %stack.39 = bf16[384,1536]{1,0:T(8,128)(2,1)} custom-call(s32[1]{0:T(128)} %bitcast.5.half_ref, bf16[384,1536]{1,0:T(8,128)(2,1)} %collective-permute-done.6.refs_0_.refs_5_, bf16[384,1536]{1,0:T(8,128)(2,1)} %collective-permute-done.7.refs_1_.refs_6_), custom_call_target="tpu_custom_call" | custom-call | bytes 2359296 | tf_op jit(solution)/shard_map/stack/pallas_call | solution.py:118
  22.2 32.7 %collective-permute-done.4.refs_7_ = bf16[384,1536]{1,0:T(8,128)(2,1)} collective-permute-done((bf16[384,1536]{1,0:T(8,128)(2,1)}, bf16[384,1536]{1,0:T(8,128)(2,1)}, u32[]{:S(2)}, u32[]{:S(2)}) %collective-permute-start.4) | collective-permute-done | bytes 1179680 | tf_op jit(solution)/shard_map/ppermute | solution.py:40
  56.5 3.8 %collective-permute-start.5 = (bf16[384,1536]{1,0:T(8,128)(2,1)}, bf16[384,1536]{1,0:T(8,128)(2,1)}, u32[]{:S(2)}, u32[]{:S(2)}) collective-permute-start(bf16[384,1536]{1,0:T(8,128)(2,1)} %collective-permute-done.4.refs_7_), channel_id=1, source_target_pairs={{0,32},{1,97},{32,64},{33,1},{64,96},{65,33},{96,0},{97,65},{4,36}... | collective-permute-start | bytes 3538952 | tf_op jit(solution)/shard_map/ppermute | solution.py:40
  60.9 6.7 %collective-permute-done.8.refs_8_ = bf16[384,1536]{1,0:T(8,128)(2,1)} collective-permute-done((bf16[384,1536]{1,0:T(8,128)(2,1)}, bf16[384,1536]{1,0:T(8,128)(2,1)}, u32[]{:S(2)}, u32[]{:S(2)}) %collective-permute-start.8) | collective-permute-done | bytes 1179680 | tf_op jit(solution)/shard_map/ppermute | solution.py:40
  67.6 3.8 %collective-permute-start.9 = (bf16[384,1536]{1,0:T(8,128)(2,1)}, bf16[384,1536]{1,0:T(8,128)(2,1)}, u32[]{:S(2)}, u32[]{:S(2)}) collective-permute-start(bf16[384,1536]{1,0:T(8,128)(2,1)} %collective-permute-done.8.refs_8_), channel_id=1, source_target_pairs={{0,32},{1,97},{32,64},{33,1},{64,96},{65,33},{96,0},{97,65},{4,36}... | collective-permute-start | bytes 3538952 | tf_op jit(solution)/shard_map/ppermute | solution.py:40
  74.1 2.7 %collective-permute-start = (bf16[32,3,1536]{2,1,0:T(4,128)(2,1)S(1)}, bf16[32,3,1536]{2,1,0:T(4,128)(2,1)S(1)}, u32[]{:S(2)}, u32[]{:S(2)}) collective-permute-start(bf16[32,3,1536]{2,1,0:T(4,128)(2,1)S(1)} %get-tuple-element.18), channel_id=1, source_target_pairs={{0,1},{1,2},{2,3},{3,4},{4,5},{5,6},{6,7},{7,8},{8,9},{9,10},{10,1... | collective-permute-start | bytes 884744 | tf_op jit(solution)/shard_map/ppermute | solution.py:66
  76.8 4.7 %collective-permute-done.refs_1_ = bf16[32,3,1536]{2,1,0:T(4,128)(2,1)S(1)} collective-permute-done((bf16[32,3,1536]{2,1,0:T(4,128)(2,1)S(1)}, bf16[32,3,1536]{2,1,0:T(4,128)(2,1)S(1)}, u32[]{:S(2)}, u32[]{:S(2)}) %collective-permute-start) | collective-permute-done | bytes 294944 | tf_op jit(solution)/shard_map/ppermute | solution.py:66
  83.4 7.9 %collective-permute-done.1.refs_2_ = bf16[32,3,1536]{2,1,0:T(4,128)(2,1)S(1)} collective-permute-done((bf16[32,3,1536]{2,1,0:T(4,128)(2,1)S(1)}, bf16[32,3,1536]{2,1,0:T(4,128)(2,1)S(1)}, u32[]{:S(2)}, u32[]{:S(2)}) %collective-permute-start.1) | collective-permute-done | bytes 294944 | tf_op jit(solution)/shard_map/ppermute | solution.py:66
  92.8 5.5 %collective-permute-start.2 = (bf16[3,22,1536]{2,1,0:T(8,128)(2,1)S(1)}, bf16[3,22,1536]{2,1,0:T(8,128)(2,1)S(1)}, u32[]{:S(2)}, u32[]{:S(2)}) collective-permute-start(bf16[3,22,1536]{2,1,0:T(8,128)(2,1)S(1)} %pad_maximum_fusion), channel_id=1, source_target_pairs={{0,16},{16,32},{32,48},{48,64},{64,80},{80,96},{96,112},{1,17},{17... | collective-permute-start | bytes 608264 | tf_op jit(solution)/shard_map/ppermute | solution.py:66
  98.4 3.4 %collective-permute-done.3.refs_6_ = bf16[3,22,1536]{2,1,0:T(8,128)(2,1)S(1)} collective-permute-done((bf16[3,22,1536]{2,1,0:T(8,128)(2,1)S(1)}, bf16[3,22,1536]{2,1,0:T(8,128)(2,1)S(1)}, u32[]{:S(2)}, u32[]{:S(2)}) %collective-permute-start.3) | collective-permute-done | bytes 202784 | tf_op jit(solution)/shard_map/ppermute | solution.py:66
  101.9 6.5 %conv.2.refs_0_ = bf16[256,1536]{1,0:T(8,128)(2,1)S(1)} custom-call(bf16[32,16,1536]{2,1,0:T(8,128)(2,1)S(1)} %bitcast.12, bf16[32,3,1536]{2,1,0:T(4,128)(2,1)S(1)} %collective-permute-done.refs_1_, bf16[32,3,1536]{2,1,0:T(4,128)(2,1)S(1)} %collective-permute-done.1.refs_2_, f32[7,7,1536]{2,1,0:T(8,128)S(1)} %copy-done.2, ...), custom_call_target="tpu_custom_call" | custom-call | flops 39321600 | bytes 3145728 | tf_op jit(solution)/shard_map/conv/pallas_call | solution.py:252
  108.5 3.6 %collective-permute-start.18 = (bf16[256,1536]{1,0:T(8,128)(2,1)S(1)}, bf16[256,1536]{1,0:T(8,128)(2,1)S(1)}, u32[]{:S(2)}, u32[]{:S(2)}) collective-permute-start(bf16[256,1536]{1,0:T(8,128)(2,1)S(1)} %conv.2.refs_0_), channel_id=1, source_target_pairs={{0,2},{1,19},{32,34},{33,51},{64,66},{65,83},{96,98},{97,115},{4,6... | collective-permute-start | bytes 2359304 | tf_op jit(solution)/shard_map/ppermute | solution.py:40
  112.1 6.8 %conv.3.refs_1_ = bf16[256,1536]{1,0:T(8,128)(2,1)S(1)} custom-call(bf16[32,16,1536]{2,1,0:T(8,128)(2,1)S(1)} %bitcast.13, bf16[32,3,1536]{2,1,0:T(4,128)(2,1)S(1)} %collective-permute-done.refs_1_, bf16[32,3,1536]{2,1,0:T(4,128)(2,1)S(1)} %collective-permute-done.1.refs_2_, f32[7,7,1536]{2,1,0:T(8,128)S(1)} %copy-done.2, ...), custom_call_target="tpu_custom_call" | custom-call | flops 39321600 | bytes 3145728 | tf_op jit(solution)/shard_map/conv/pallas_call | solution.py:252
  118.9 2.1 %collective-permute-done.18.refs_0_ = bf16[256,1536]{1,0:T(8,128)(2,1)S(1)} collective-permute-done((bf16[256,1536]{1,0:T(8,128)(2,1)S(1)}, bf16[256,1536]{1,0:T(8,128)(2,1)S(1)}, u32[]{:S(2)}, u32[]{:S(2)}) %collective-permute-start.18) | collective-permute-done | bytes 786464 | tf_op jit(solution)/shard_map/ppermute | solution.py:40
  121.0 3.0 %collective-permute-start.10 = (bf16[384,1536]{1,0:T(8,128)(2,1)}, bf16[384,1536]{1,0:T(8,128)(2,1)S(1)}, u32[]{:S(2)}, u32[]{:S(2)}) collective-permute-start(bf16[384,1536]{1,0:T(8,128)(2,1)} %collective-permute-done.5.refs_3_), channel_id=1, source_target_pairs={{0,1},{1,0},{32,33},{33,32},{64,65},{65,64},{96,97},{97,96},{4,5},... | collective-permute-start | bytes 3538952 | tf_op jit(solution)/shard_map/ppermute | solution.py:40
  124.8 5.3 %collective-permute-done.19.refs_1_ = bf16[256,1536]{1,0:T(8,128)(2,1)S(1)} collective-permute-done((bf16[256,1536]{1,0:T(8,128)(2,1)S(1)}, bf16[256,1536]{1,0:T(8,128)(2,1)S(1)}, u32[]{:S(2)}, u32[]{:S(2)}) %collective-permute-start.19) | collective-permute-done | bytes 786464 | tf_op jit(solution)/shard_map/ppermute | solution.py:40
  130.1 8.8 %mlp.7.refs_7_ = f32[512,1536]{1,0:T(8,128)S(1)} custom-call(bf16[256,1536]{1,0:T(8,128)(2,1)S(1)} %collective-permute-done.18.refs_0_, bf16[256,1536]{1,0:T(8,128)(2,1)S(1)} %collective-permute-done.19.refs_1_, f32[2,1536]{1,0:T(2,128)S(1)} %get-tuple-element.14.refs_2_, bf16[384,1536]{1,0:T(8,128)(2,1)S(1)} %copy-done.4, bf16[384,1536]{1,0:T(8,128)(2,1)S(1)} %copy-done.6, ...), custom_call_target="tpu_custom_call" | custom-call | flops 4831838208 | bytes 9437184 | tf_op jit(solution)/shard_map/mlp/pallas_call | solution.py:338
  138.9 6.1 %mlp.8.refs_7_ = f32[512,1536]{1,0:T(8,128)S(1)} custom-call(bf16[256,1536]{1,0:T(8,128)(2,1)S(1)} %collective-permute-done.18.refs_0_, bf16[256,1536]{1,0:T(8,128)(2,1)S(1)} %collective-permute-done.19.refs_1_, f32[2,1536]{1,0:T(2,128)S(1)} %get-tuple-element.14.refs_2_, bf16[384,1536]{1,0:T(8,128)(2,1)} %collective-permute-done.5.refs_3_, ...), custom_call_target="tpu_custom_call" | custom-call | flops 2415919104 | bytes 4718592 | tf_op jit(solution)/shard_map/mlp/pallas_call | solution.py:338
  145.0 5.9 %mlp.9 = bf16[512,1536]{1,0:T(8,128)(2,1)S(1)} custom-call(bf16[256,1536]{1,0:T(8,128)(2,1)S(1)} %collective-permute-done.18.refs_0_, bf16[256,1536]{1,0:T(8,128)(2,1)S(1)} %collective-permute-done.19.refs_1_, f32[2,1536]{1,0:T(2,128)S(1)} %get-tuple-element.14.refs_2_, bf16[384,1536]{1,0:T(8,128)(2,1)} %collective-permute-done.12.refs_7_.refs_3_, ...), custom_call_target="tpu_custom_call" | custom-call | flops 2415919104 | bytes 4718592 | tf_op jit(solution)/shard_map/mlp/pallas_call | solution.py:338
  151.2 8.8 %mlp.5.refs_11_ = f32[512,1536]{1,0:T(8,128)S(1)} custom-call(bf16[256,1536]{1,0:T(8,128)(2,1)S(1)} %conv.2.refs_0_, bf16[256,1536]{1,0:T(8,128)(2,1)S(1)} %conv.3.refs_1_, f32[2,1536]{1,0:T(2,128)S(1)} %get-tuple-element.14.refs_2_, bf16[384,1536]{1,0:T(8,128)(2,1)S(1)} %copy-done.4, bf16[384,1536]{1,0:T(8,128)(2,1)S(1)} %copy-done.6, ...), custom_call_target="tpu_custom_call" | custom-call | flops 4831838208 | bytes 9437184 | tf_op jit(solution)/shard_map/mlp/pallas_call | solution.py:338
  160.1 8.6 %mlp.6 = f32[512,1536]{1,0:T(8,128)S(1)} custom-call(bf16[256,1536]{1,0:T(8,128)(2,1)S(1)} %conv.2.refs_0_, bf16[256,1536]{1,0:T(8,128)(2,1)S(1)} %conv.3.refs_1_, f32[2,1536]{1,0:T(2,128)S(1)} %get-tuple-element.14.refs_2_, bf16[384,1536]{1,0:T(8,128)(2,1)} %collective-permute-done.5.refs_3_, bf16[384,1536]{1,0:T(8,128)(2,1)} %collective-permute-done.9.refs_4_, ...), custom_call_target="tpu_custom_call" | custom-call | flops 4831838208 | bytes 9437184 | tf_op jit(solution)/shard_map/mlp/pallas_call | solution.py:338
  168.7 3.0 %collective-permute-done.20 = bf16[512,1536]{1,0:T(8,128)(2,1)S(1)} collective-permute-done((bf16[512,1536]{1,0:T(8,128)(2,1)S(1)}, bf16[512,1536]{1,0:T(8,128)(2,1)S(1)}, u32[]{:S(2)}, u32[]{:S(2)}) %collective-permute-start.20) | collective-permute-done | bytes 1572896 | tf_op jit(solution)/shard_map/ppermute | solution.py:40
  (80 shorter events, 21.7 us)
Async XLA Ops:
  5.1 66.3 %all-to-all-start = ((bf16[16,48,1664]{2,1,0:T(8,128)(2,1)}), bf16[16,48,1664]{2,1,0:T(8,128)(2,1)S(1)}, u32[]{:S(2)}, u32[]{:S(2)}) async-start(bf16[16,48,1664]{2,1,0:T(8,128)(2,1)} %bitcast.15), calls=%async_computation | async-start | bytes 5111808 | tf_op jit(solution)/shard_map/all_to_all | solution.py:384
  12.0 7.0 %collective-permute-start.6 = (bf16[384,1536]{1,0:T(8,128)(2,1)}, bf16[384,1536]{1,0:T(8,128)(2,1)}, u32[]{:S(2)}, u32[]{:S(2)}) collective-permute-start(bf16[384,1536]{1,0:T(8,128)(2,1)} %refs_3_.7), channel_id=1, source_target_pairs={{0,1},{1,0},{32,33},{33,32},{64,65},{65,64},{96,97},{97,96},{4,5},... | collective-permute-start | bytes 3538952 | tf_op jit(solution)/shard_map/ppermute | solution.py:40
  12.2 6.8 %collective-permute-start.7 = (bf16[384,1536]{1,0:T(8,128)(2,1)}, bf16[384,1536]{1,0:T(8,128)(2,1)}, u32[]{:S(2)}, u32[]{:S(2)}) collective-permute-start(bf16[384,1536]{1,0:T(8,128)(2,1)} %refs_4_.3), channel_id=1, source_target_pairs={{0,1},{1,0},{32,33},{33,32},{64,65},{65,64},{96,97},{97,96},{4,5},... | collective-permute-start | bytes 3538952 | tf_op jit(solution)/shard_map/ppermute | solution.py:40
  16.3 38.6 %collective-permute-start.4 = (bf16[384,1536]{1,0:T(8,128)(2,1)}, bf16[384,1536]{1,0:T(8,128)(2,1)}, u32[]{:S(2)}, u32[]{:S(2)}) collective-permute-start(bf16[384,1536]{1,0:T(8,128)(2,1)} %stack.38), channel_id=1, source_target_pairs={{0,4},{1,13},{32,36},{33,45},{64,68},{65,77},{96,100},{97,109},{4,... | collective-permute-start | bytes 3538952 | tf_op jit(solution)/shard_map/ppermute | solution.py:40
  21.4 51.0 %copy-start.12 = (bf16[1536]{0:T(1024)(128)(2,1)S(1)}, bf16[1536]{0:T(1024)(128)(2,1)}, u32[]{:S(2)}) copy-start(bf16[1536]{0:T(1024)(128)(2,1)} %param.14) | copy-start | bytes 9220
  21.4 46.2 %collective-permute-start.8 = (bf16[384,1536]{1,0:T(8,128)(2,1)}, bf16[384,1536]{1,0:T(8,128)(2,1)}, u32[]{:S(2)}, u32[]{:S(2)}) collective-permute-start(bf16[384,1536]{1,0:T(8,128)(2,1)} %stack.39), channel_id=1, source_target_pairs={{0,4},{1,13},{32,36},{33,45},{64,68},{65,77},{96,100},{97,109},{4,... | collective-permute-start | bytes 3538952 | tf_op jit(solution)/shard_map/ppermute | solution.py:40
  55.0 37.8 %collective-permute-start.16 = (bf16[384,1536]{1,0:T(8,128)(2,1)}, bf16[384,1536]{1,0:T(8,128)(2,1)}, u32[]{:S(2)}, u32[]{:S(2)}) collective-permute-start(bf16[384,1536]{1,0:T(8,128)(2,1)} %collective-permute-done.4.refs_7_), channel_id=1, source_target_pairs={{0,1},{1,0},{32,33},{33,32},{64,65},{65,64},{96,97},{97,96},{4,5},... | collective-permute-start | bytes 3538952 | tf_op jit(solution)/shard_map/ppermute | solution.py:40
  56.5 62.3 %collective-permute-start.5 = (bf16[384,1536]{1,0:T(8,128)(2,1)}, bf16[384,1536]{1,0:T(8,128)(2,1)}, u32[]{:S(2)}, u32[]{:S(2)}) collective-permute-start(bf16[384,1536]{1,0:T(8,128)(2,1)} %collective-permute-done.4.refs_7_), channel_id=1, source_target_pairs={{0,32},{1,97},{32,64},{33,1},{64,96},{65,33},{96,0},{97,65},{4,36}... | collective-permute-start | bytes 3538952 | tf_op jit(solution)/shard_map/ppermute | solution.py:40
  60.3 38.0 %collective-permute-start.12 = (bf16[384,1536]{1,0:T(8,128)(2,1)}, bf16[384,1536]{1,0:T(8,128)(2,1)}, u32[]{:S(2)}, u32[]{:S(2)}) collective-permute-start(bf16[384,1536]{1,0:T(8,128)(2,1)} %collective-permute-done.4.refs_7_), channel_id=1, source_target_pairs={{0,4},{1,13},{32,36},{33,45},{64,68},{65,77},{96,100},{97,109},{4,... | collective-permute-start | bytes 3538952 | tf_op jit(solution)/shard_map/ppermute | solution.py:40
  67.6 56.4 %collective-permute-start.9 = (bf16[384,1536]{1,0:T(8,128)(2,1)}, bf16[384,1536]{1,0:T(8,128)(2,1)}, u32[]{:S(2)}, u32[]{:S(2)}) collective-permute-start(bf16[384,1536]{1,0:T(8,128)(2,1)} %collective-permute-done.8.refs_8_), channel_id=1, source_target_pairs={{0,32},{1,97},{32,64},{33,1},{64,96},{65,33},{96,0},{97,65},{4,36}... | collective-permute-start | bytes 3538952 | tf_op jit(solution)/shard_map/ppermute | solution.py:40
  73.8 28.2 %copy-start.2 = (f32[7,7,1536]{2,1,0:T(8,128)S(1)}, f32[7,7,1536]{2,1,0:T(8,128)}, u32[]{:S(2)}) copy-start(f32[7,7,1536]{2,1,0:T(8,128)} %refs_3_.5) | copy-start | bytes 903172
  74.1 7.4 %collective-permute-start = (bf16[32,3,1536]{2,1,0:T(4,128)(2,1)S(1)}, bf16[32,3,1536]{2,1,0:T(4,128)(2,1)S(1)}, u32[]{:S(2)}, u32[]{:S(2)}) collective-permute-start(bf16[32,3,1536]{2,1,0:T(4,128)(2,1)S(1)} %get-tuple-element.18), channel_id=1, source_target_pairs={{0,1},{1,2},{2,3},{3,4},{4,5},{5,6},{6,7},{7,8},{8,9},{9,10},{10,1... | collective-permute-start | bytes 884744 | tf_op jit(solution)/shard_map/ppermute | solution.py:66
  81.5 9.8 %collective-permute-start.1 = (bf16[32,3,1536]{2,1,0:T(4,128)(2,1)S(1)}, bf16[32,3,1536]{2,1,0:T(4,128)(2,1)S(1)}, u32[]{:S(2)}, u32[]{:S(2)}) collective-permute-start(bf16[32,3,1536]{2,1,0:T(4,128)(2,1)S(1)} %get-tuple-element.17), channel_id=1, source_target_pairs={{1,0},{2,1},{3,2},{4,3},{5,4},{6,5},{7,6},{8,7},{9,8},{10,9},{11,1... | collective-permute-start | bytes 884744 | tf_op jit(solution)/shard_map/ppermute | solution.py:66
  91.4 10.4 %collective-permute-start.3 = (bf16[3,22,1536]{2,1,0:T(8,128)(2,1)S(1)}, bf16[3,22,1536]{2,1,0:T(8,128)(2,1)S(1)}, u32[]{:S(2)}, u32[]{:S(2)}) collective-permute-start(bf16[3,22,1536]{2,1,0:T(8,128)(2,1)S(1)} %pad_maximum_fusion.1), channel_id=1, source_target_pairs={{16,0},{32,16},{48,32},{64,48},{80,64},{96,80},{112,96},{17,1},{33... | collective-permute-start | bytes 608264 | tf_op jit(solution)/shard_map/ppermute | solution.py:66
  92.8 15.7 %collective-permute-start.2 = (bf16[3,22,1536]{2,1,0:T(8,128)(2,1)S(1)}, bf16[3,22,1536]{2,1,0:T(8,128)(2,1)S(1)}, u32[]{:S(2)}, u32[]{:S(2)}) collective-permute-start(bf16[3,22,1536]{2,1,0:T(8,128)(2,1)S(1)} %pad_maximum_fusion), channel_id=1, source_target_pairs={{0,16},{16,32},{32,48},{48,64},{64,80},{80,96},{96,112},{1,17},{17... | collective-permute-start | bytes 608264 | tf_op jit(solution)/shard_map/ppermute | solution.py:66
  98.3 25.7 %collective-permute-start.17 = (bf16[384,1536]{1,0:T(8,128)(2,1)}, bf16[384,1536]{1,0:T(8,128)(2,1)S(1)}, u32[]{:S(2)}, u32[]{:S(2)}) collective-permute-start(bf16[384,1536]{1,0:T(8,128)(2,1)} %collective-permute-done.8.refs_8_), channel_id=1, source_target_pairs={{0,1},{1,0},{32,33},{33,32},{64,65},{65,64},{96,97},{97,96},{4,5},... | collective-permute-start | bytes 3538952 | tf_op jit(solution)/shard_map/ppermute | solution.py:40
  101.8 22.7 %collective-permute-start.14 = (bf16[384,1536]{1,0:T(8,128)(2,1)}, bf16[384,1536]{1,0:T(8,128)(2,1)S(1)}, u32[]{:S(2)}, u32[]{:S(2)}) collective-permute-start(bf16[384,1536]{1,0:T(8,128)(2,1)} %collective-permute-done.12.refs_7_.refs_3_), channel_id=1, source_target_pairs={{0,32},{1,97},{32,64},{33,1},{64,96},{65,33},{96,0},{97,65},{4,36}... | collective-permute-start | bytes 3538952 | tf_op jit(solution)/shard_map/ppermute | solution.py:40
  108.5 12.5 %collective-permute-start.18 = (bf16[256,1536]{1,0:T(8,128)(2,1)S(1)}, bf16[256,1536]{1,0:T(8,128)(2,1)S(1)}, u32[]{:S(2)}, u32[]{:S(2)}) collective-permute-start(bf16[256,1536]{1,0:T(8,128)(2,1)S(1)} %conv.2.refs_0_), channel_id=1, source_target_pairs={{0,2},{1,19},{32,34},{33,51},{64,66},{65,83},{96,98},{97,115},{4,6... | collective-permute-start | bytes 2359304 | tf_op jit(solution)/shard_map/ppermute | solution.py:40
  118.9 11.2 %collective-permute-start.19 = (bf16[256,1536]{1,0:T(8,128)(2,1)S(1)}, bf16[256,1536]{1,0:T(8,128)(2,1)S(1)}, u32[]{:S(2)}, u32[]{:S(2)}) collective-permute-start(bf16[256,1536]{1,0:T(8,128)(2,1)S(1)} %conv.3.refs_1_), channel_id=1, source_target_pairs={{0,2},{1,19},{32,34},{33,51},{64,66},{65,83},{96,98},{97,115},{4,6... | collective-permute-start | bytes 2359304 | tf_op jit(solution)/shard_map/ppermute | solution.py:40
  121.0 17.9 %collective-permute-start.10 = (bf16[384,1536]{1,0:T(8,128)(2,1)}, bf16[384,1536]{1,0:T(8,128)(2,1)S(1)}, u32[]{:S(2)}, u32[]{:S(2)}) collective-permute-start(bf16[384,1536]{1,0:T(8,128)(2,1)} %collective-permute-done.5.refs_3_), channel_id=1, source_target_pairs={{0,1},{1,0},{32,33},{33,32},{64,65},{65,64},{96,97},{97,96},{4,5},... | collective-permute-start | bytes 3538952 | tf_op jit(solution)/shard_map/ppermute | solution.py:40
  124.0 14.9 %collective-permute-start.11 = (bf16[384,1536]{1,0:T(8,128)(2,1)}, bf16[384,1536]{1,0:T(8,128)(2,1)S(1)}, u32[]{:S(2)}, u32[]{:S(2)}) collective-permute-start(bf16[384,1536]{1,0:T(8,128)(2,1)} %collective-permute-done.9.refs_4_), channel_id=1, source_target_pairs={{0,1},{1,0},{32,33},{33,32},{64,65},{65,64},{96,97},{97,96},{4,5},... | collective-permute-start | bytes 3538952 | tf_op jit(solution)/shard_map/ppermute | solution.py:40
  124.0 21.0 %collective-permute-start.13 = (bf16[384,1536]{1,0:T(8,128)(2,1)}, bf16[384,1536]{1,0:T(8,128)(2,1)S(1)}, u32[]{:S(2)}, u32[]{:S(2)}) collective-permute-start(bf16[384,1536]{1,0:T(8,128)(2,1)} %collective-permute-done.12.refs_7_.refs_3_), channel_id=1, source_target_pairs={{0,1},{1,0},{32,33},{33,32},{64,65},{65,64},{96,97},{97,96},{4,5},... | collective-permute-start | bytes 3538952 | tf_op jit(solution)/shard_map/ppermute | solution.py:40
  124.5 20.5 %collective-permute-start.15 = (bf16[384,1536]{1,0:T(8,128)(2,1)S(1)}, bf16[384,1536]{1,0:T(8,128)(2,1)S(1)}, u32[]{:S(2)}, u32[]{:S(2)}) collective-permute-start(bf16[384,1536]{1,0:T(8,128)(2,1)S(1)} %collective-permute-done.14.refs_9_.refs_5_), channel_id=1, source_target_pairs={{0,1},{1,0},{32,33},{33,32},{64,65},{65,64},{96,97},{97,96},{4,5},... | collective-permute-start | bytes 3538952 | tf_op jit(solution)/shard_map/ppermute | solution.py:40
  150.9 20.8 %collective-permute-start.20 = (bf16[512,1536]{1,0:T(8,128)(2,1)S(1)}, bf16[512,1536]{1,0:T(8,128)(2,1)S(1)}, u32[]{:S(2)}, u32[]{:S(2)}) collective-permute-start(bf16[512,1536]{1,0:T(8,128)(2,1)S(1)} %mlp.9), channel_id=1, source_target_pairs={{0,18},{1,3},{32,50},{33,35},{64,82},{65,67},{96,114},{97,99},{4,2... | collective-permute-start | bytes 4718600 | tf_op jit(solution)/shard_map/ppermute | solution.py:40
  (11 other events, 89.4 us)

commit v5 on v4

--- a/solution.py
+++ b/solution.py
@@ -74,16 +74,26 @@
     return pltpu.CompilerParams(vmem_limit_bytes=mib * 1024 * 1024)
 
 
-def join_kernel(patches_ref, head_ref, out_ref, sem):
+def join_kernel(patches_ref, head_ref, out_ref, rows, sems):
     channels = patches_ref.shape[1]
-    copy = pltpu.make_async_copy(patches_ref, out_ref.at[:, pl.ds(0, channels)], sem)
-    copy.start()
+    parts = [pl.ds(k * rows.shape[0] // 4, rows.shape[0] // 4) for k in range(4)]
+    ins = [
+        pltpu.make_async_copy(patches_ref.at[part], rows.at[part, pl.ds(0, channels)], sems.at[0, k])
+        for k, part in enumerate(parts)
+    ]
+    outs = [pltpu.make_async_copy(rows.at[part], out_ref.at[part], sems.at[1, k]) for k, part in enumerate(parts)]
+    for copy in ins:
+        copy.start()
     groups, lines, _ = head_ref.shape
-    size = out_ref.shape[0] // groups
-    out_ref[:, channels:] = jnp.zeros((out_ref.shape[0], LANES), out_ref.dtype)
+    size = rows.shape[0] // groups
+    rows[:, channels:] = jnp.zeros((rows.shape[0], LANES), rows.dtype)
     for g in range(groups):
-        out_ref[g * size : g * size + lines, channels:] = head_ref[g]
-    copy.wait()
+        rows[g * size : g * size + lines, channels:] = head_ref[g]
+    for arrived, leaves in zip(ins, outs):
+        arrived.wait()
+        leaves.start()
+    for copy in outs:
+        copy.wait()
 
 
 def join(patches, head):
@@ -92,10 +102,9 @@
         join_kernel,
         out_shape=jax.ShapeDtypeStruct((rows, channels + LANES), patches.dtype),
         in_specs=[whole(pl.ANY), whole()],
-        out_specs=whole(),
-        scratch_shapes=[pltpu.SemaphoreType.DMA],
+        out_specs=whole(pl.ANY),
+        scratch_shapes=[VMEM((rows, channels + LANES), patches.dtype), pltpu.SemaphoreType.DMA((2, 4))],
         cost_estimate=pl.CostEstimate(flops=0, bytes_accessed=4 * rows * channels, transcendentals=0),
-        compiler_params=grant(7),
         name="join",
     )(patches, head)
 
@@ -297,38 +306,45 @@
             source, target = ref.at[pl.ds(line * TW, size * TW)], rows.at[pl.ds(start * TW, size * TW)]
             moves.append(pltpu.make_async_copy(source, target, row_sems.at[len(moves)]))
             line += size
-    early = next(k for k in range(len(plan) + 1) if sum(p[4] for p in plan[:k]) >= blocks // 2 * UNITS)
     for copy in moves + ins + outs:
         copy.start()
-    for copy in moves + ins[:early]:
+    for copy in moves + ins + outs:
         copy.wait()
 
-    def first(h):
-        return lax.dot_general(
-            rows[...], w_in[h * UNITS : (h + 1) * UNITS, :], (((1,), (1,)), ((), ())),
+    half_rows = rows.shape[0] // 2
+
+    def cut(r):
+        return slice(r * half_rows, (r + 1) * half_rows)
+
+    waiting, sent = None, 0
+    todo = [(r, n) for r in range(2) for n in range(columns)]
+
+    def finish(r, n):
+        at = slice(n * UNITS, (n + 1) * UNITS)
+        total = jnp.dot(hid[cut(r), :], w_out[:, at], preferred_element_type=jnp.float32)
+        if adds:
+            total = total + acc_ref[cut(r), at]
+        out_ref[cut(r), at] = total.astype(out_ref.dtype)
+
+    def activate(r, h, pre):
+        at = slice(h * UNITS, (h + 1) * UNITS)
+        hid[cut(r), at] = gelu(pre + bias_ref[bias_at[0] : bias_at[0] + 1, bias_at[1] + h * UNITS : bias_at[1] + (h + 1) * UNITS]).astype(jnp.bfloat16)
+
+    for k in range(2 * blocks):
+        r, h = divmod(k, blocks)
+        pre = lax.dot_general(
+            rows[cut(r), :], w_in[h * UNITS : (h + 1) * UNITS, :], (((1,), (1,)), ((), ())),
             preferred_element_type=jnp.float32,
         )
-
-    def middle(h, pre):
-        at = slice(h * UNITS, (h + 1) * UNITS)
-        hid[:, at] = gelu(pre + bias_ref[bias_at[0] : bias_at[0] + 1, bias_at[1] + h * UNITS : bias_at[1] + (h + 1) * UNITS]).astype(jnp.bfloat16)
-
-    waiting = None
-    for h in range(blocks):
-        if h == blocks // 2:
-            for copy in ins[early:] + outs:
-                copy.wait()
-        pre = first(h)
         if waiting is not None:
-            middle(*waiting)
-        waiting = (h, pre)
-    middle(*waiting)
-    for n in range(columns):
-        at = slice(n * UNITS, (n + 1) * UNITS)
-        total = jnp.dot(hid[...], w_out[:, at], preferred_element_type=jnp.float32)
-        if adds:
-            total = total + acc_ref[:, at]
-        out_ref[:, at] = total.astype(out_ref.dtype)
+            activate(*waiting)
+        waiting = (r, h, pre)
+        if k > blocks:
+            finish(*todo[sent])
+            sent += 1
+    activate(*waiting)
+    for item in todo[sent:]:
+        finish(*item)
 
 
 def mlp(rows, bias, bias_at, pieces, plan, acc=None, out_dtype=jnp.float32):
@@ -392,7 +408,7 @@
     near_a_p = send(near_a, to_partner)
     near_b_z = send(near_b, along_z)
     near_b_p = send(near_b, to_partner)
-    far_z = send(far, along_z)
+    far_z = send(near_a_z, along_y)
     far_p = send(far, to_partner)
     near_a_zp = send(near_a_z, to_partner)
     near_b_zp = send(near_b_z, to_partner)

time: 175 us -> 174 us (level)
  local copies, waits for them, and re-layouts: 7.16 us -> 4.03 us
  Pallas kernels: 56 us -> 58.5 us
    pallas_call x1, Pallas kernels: 0.2 us -> 3.37 us  [join(): pl.pallas_call(join_kernel, out_shape=jax.ShapeDtypeStruct((rows, channel...]
    unnamed x26 -> x22, local copies, waits for them, and re-layouts: 5.72 us -> 2.6 us
where the time goes in v5:
time: 174 us; the launch traced here: 173 us
  waiting for transfers between devices  66.3 us (38%)
  Pallas kernels  58.5 us (34%)
  starting transfers between devices  38.8 us (22%)
  local copies, waits for them, and re-layouts  4.03 us (2%)
  other arithmetic  3.68 us (2%)
    ppermute x17, waiting for transfers between devices, send(): return lax.ppermute(value, ('row', 'col'), routes(move))  50.3 us
    pallas_call x5, Pallas kernels, mlp(): pl.pallas_call(functools.partial(mlp_kernel, plan, bias_at, len(rows), le...  37.5 us
    ppermute x17, starting transfers between devices, send(): return lax.ppermute(value, ('row', 'col'), routes(move))  20.5 us
    ppermute x4, waiting for transfers between devices, shift(): return lax.ppermute(value, axis, pairs)  16 us
    pallas_call x2, Pallas kernels, conv_norm(): pl.pallas_call(functools.partial(conv_kernel, bands), out_shape=jax.Shape...  13.3 us
    ppermute x4, starting transfers between devices, shift(): return lax.ppermute(value, axis, pairs)  11.4 us
    all_to_all x1, starting transfers between devices, local(): lax.all_to_all(join(patches, head), 'col', split_axis=0, concat_axis=0, t...  6.91 us
    pallas_call x2, Pallas kernels, stack(): pl.pallas_call(stack_kernel, out_shape=jax.ShapeDtypeStruct((len(sources)...  3.66 us
  transfers between devices with their start and end apart: 22, of which 8 were waited for; matrix products, arithmetic and copies ran while one was open for 1% of the time, Pallas kernels for 29%

profile of v5, /device:TPU:1, one launch (start us, length us, event | category | flops | bytes accessed | tf_op | source)
XLA Modules:
  0.0 173.2 jit_solution(13349517005642984504)
XLA Ops:
  2.3 3.4 %join.1 = bf16[768,1664]{1,0:T(8,128)(2,1)} custom-call(bf16[768,1536]{1,0:T(8,128)(2,1)} %patches_ref.1, bf16[16,8,128]{2,1,0:T(8,128)(2,1)} %pad_maximum_fusion.2.head_ref), custom_call_target="tpu_custom_call" | custom-call | bytes 4718592 | tf_op jit(solution)/shard_map/join/pallas_call | solution.py:101
  5.7 6.9 %all-to-all-start = ((bf16[16,48,1664]{2,1,0:T(8,128)(2,1)}), bf16[16,48,1664]{2,1,0:T(8,128)(2,1)S(1)}, u32[]{:S(2)}, u32[]{:S(2)}) async-start(bf16[16,48,1664]{2,1,0:T(8,128)(2,1)} %bitcast.15), calls=%async_computation | async-start | bytes 5111808 | tf_op jit(solution)/shard_map/all_to_all | solution.py:400
  17.0 2.6 %collective-permute-start.4 = (bf16[384,1536]{1,0:T(8,128)(2,1)}, bf16[384,1536]{1,0:T(8,128)(2,1)}, u32[]{:S(2)}, u32[]{:S(2)}) collective-permute-start(bf16[384,1536]{1,0:T(8,128)(2,1)} %stack.38), channel_id=1, source_target_pairs={{0,4},{1,13},{32,36},{33,45},{64,68},{65,77},{96,100},{97,109},{4,... | collective-permute-start | bytes 3538952 | tf_op jit(solution)/shard_map/ppermute | solution.py:40
  19.6 2.4 %stack.39 = bf16[384,1536]{1,0:T(8,128)(2,1)} custom-call(s32[1]{0:T(128)} %bitcast.5.half_ref, bf16[384,1536]{1,0:T(8,128)(2,1)} %collective-permute-done.6.refs_0_.refs_5_, bf16[384,1536]{1,0:T(8,128)(2,1)} %collective-permute-done.7.refs_1_.refs_6_), custom_call_target="tpu_custom_call" | custom-call | bytes 2359296 | tf_op jit(solution)/shard_map/stack/pallas_call | solution.py:127
  22.9 32.7 %collective-permute-done.4.refs_7_ = bf16[384,1536]{1,0:T(8,128)(2,1)} collective-permute-done((bf16[384,1536]{1,0:T(8,128)(2,1)}, bf16[384,1536]{1,0:T(8,128)(2,1)}, u32[]{:S(2)}, u32[]{:S(2)}) %collective-permute-start.4) | collective-permute-done | bytes 1179680 | tf_op jit(solution)/shard_map/ppermute | solution.py:40
  57.2 3.8 %collective-permute-start.5 = (bf16[384,1536]{1,0:T(8,128)(2,1)}, bf16[384,1536]{1,0:T(8,128)(2,1)}, u32[]{:S(2)}, u32[]{:S(2)}) collective-permute-start(bf16[384,1536]{1,0:T(8,128)(2,1)} %collective-permute-done.4.refs_7_), channel_id=1, source_target_pairs={{0,32},{1,97},{32,64},{33,1},{64,96},{65,33},{96,0},{97,65},{4,36}... | collective-permute-start | bytes 3538952 | tf_op jit(solution)/shard_map/ppermute | solution.py:40
  61.6 6.7 %collective-permute-done.8.refs_8_ = bf16[384,1536]{1,0:T(8,128)(2,1)} collective-permute-done((bf16[384,1536]{1,0:T(8,128)(2,1)}, bf16[384,1536]{1,0:T(8,128)(2,1)}, u32[]{:S(2)}, u32[]{:S(2)}) %collective-permute-start.8) | collective-permute-done | bytes 1179680 | tf_op jit(solution)/shard_map/ppermute | solution.py:40
  68.3 3.8 %collective-permute-start.9 = (bf16[384,1536]{1,0:T(8,128)(2,1)}, bf16[384,1536]{1,0:T(8,128)(2,1)}, u32[]{:S(2)}, u32[]{:S(2)}) collective-permute-start(bf16[384,1536]{1,0:T(8,128)(2,1)} %collective-permute-done.8.refs_8_), channel_id=1, source_target_pairs={{0,32},{1,97},{32,64},{33,1},{64,96},{65,33},{96,0},{97,65},{4,36}... | collective-permute-start | bytes 3538952 | tf_op jit(solution)/shard_map/ppermute | solution.py:40
  74.8 2.7 %collective-permute-start = (bf16[32,3,1536]{2,1,0:T(4,128)(2,1)S(1)}, bf16[32,3,1536]{2,1,0:T(4,128)(2,1)S(1)}, u32[]{:S(2)}, u32[]{:S(2)}) collective-permute-start(bf16[32,3,1536]{2,1,0:T(4,128)(2,1)S(1)} %get-tuple-element.18), channel_id=1, source_target_pairs={{0,1},{1,2},{2,3},{3,4},{4,5},{5,6},{6,7},{7,8},{8,9},{9,10},{10,1... | collective-permute-start | bytes 884744 | tf_op jit(solution)/shard_map/ppermute | solution.py:66
  77.5 4.7 %collective-permute-done.refs_1_ = bf16[32,3,1536]{2,1,0:T(4,128)(2,1)S(1)} collective-permute-done((bf16[32,3,1536]{2,1,0:T(4,128)(2,1)S(1)}, bf16[32,3,1536]{2,1,0:T(4,128)(2,1)S(1)}, u32[]{:S(2)}, u32[]{:S(2)}) %collective-permute-start) | collective-permute-done | bytes 294944 | tf_op jit(solution)/shard_map/ppermute | solution.py:66
  84.1 7.9 %collective-permute-done.1.refs_2_ = bf16[32,3,1536]{2,1,0:T(4,128)(2,1)S(1)} collective-permute-done((bf16[32,3,1536]{2,1,0:T(4,128)(2,1)S(1)}, bf16[32,3,1536]{2,1,0:T(4,128)(2,1)S(1)}, u32[]{:S(2)}, u32[]{:S(2)}) %collective-permute-start.1) | collective-permute-done | bytes 294944 | tf_op jit(solution)/shard_map/ppermute | solution.py:66
  93.4 5.5 %collective-permute-start.2 = (bf16[3,22,1536]{2,1,0:T(8,128)(2,1)S(1)}, bf16[3,22,1536]{2,1,0:T(8,128)(2,1)S(1)}, u32[]{:S(2)}, u32[]{:S(2)}) collective-permute-start(bf16[3,22,1536]{2,1,0:T(8,128)(2,1)S(1)} %pad_maximum_fusion), channel_id=1, source_target_pairs={{0,16},{16,32},{32,48},{48,64},{64,80},{80,96},{96,112},{1,17},{17... | collective-permute-start | bytes 608264 | tf_op jit(solution)/shard_map/ppermute | solution.py:66
  99.0 3.4 %collective-permute-done.3.refs_6_ = bf16[3,22,1536]{2,1,0:T(8,128)(2,1)S(1)} collective-permute-done((bf16[3,22,1536]{2,1,0:T(8,128)(2,1)S(1)}, bf16[3,22,1536]{2,1,0:T(8,128)(2,1)S(1)}, u32[]{:S(2)}, u32[]{:S(2)}) %collective-permute-start.3) | collective-permute-done | bytes 202784 | tf_op jit(solution)/shard_map/ppermute | solution.py:66
  102.5 6.5 %conv.2.refs_0_ = bf16[256,1536]{1,0:T(8,128)(2,1)S(1)} custom-call(bf16[32,16,1536]{2,1,0:T(8,128)(2,1)S(1)} %bitcast.12, bf16[32,3,1536]{2,1,0:T(4,128)(2,1)S(1)} %collective-permute-done.refs_1_, bf16[32,3,1536]{2,1,0:T(4,128)(2,1)S(1)} %collective-permute-done.1.refs_2_, f32[7,7,1536]{2,1,0:T(8,128)S(1)} %copy-done, f32[3,1536]{1,0:T(4,128)S(1)} %pad_maximum_fusion.3.refs_4_), custom_call_target="tpu_custom_call" | custom-call | flops 39321600 | bytes 3145728 | tf_op jit(solution)/shard_map/conv/pallas_call | solution.py:261
  109.0 3.7 %collective-permute-start.18 = (bf16[256,1536]{1,0:T(8,128)(2,1)S(1)}, bf16[256,1536]{1,0:T(8,128)(2,1)S(1)}, u32[]{:S(2)}, u32[]{:S(2)}) collective-permute-start(bf16[256,1536]{1,0:T(8,128)(2,1)S(1)} %conv.2.refs_0_), channel_id=1, source_target_pairs={{0,2},{1,19},{32,34},{33,51},{64,66},{65,83},{96,98},{97,115},{4,6... | collective-permute-start | bytes 2359304 | tf_op jit(solution)/shard_map/ppermute | solution.py:40
  112.7 6.8 %conv.3.refs_1_ = bf16[256,1536]{1,0:T(8,128)(2,1)S(1)} custom-call(bf16[32,16,1536]{2,1,0:T(8,128)(2,1)S(1)} %bitcast.13, bf16[32,3,1536]{2,1,0:T(4,128)(2,1)S(1)} %collective-permute-done.refs_1_, bf16[32,3,1536]{2,1,0:T(4,128)(2,1)S(1)} %collective-permute-done.1.refs_2_, f32[7,7,1536]{2,1,0:T(8,128)S(1)} %copy-done, ...), custom_call_target="tpu_custom_call" | custom-call | flops 39321600 | bytes 3145728 | tf_op jit(solution)/shard_map/conv/pallas_call | solution.py:261
  121.6 2.1 %collective-permute-start.10 = (bf16[384,1536]{1,0:T(8,128)(2,1)}, bf16[384,1536]{1,0:T(8,128)(2,1)S(1)}, u32[]{:S(2)}, u32[]{:S(2)}) collective-permute-start(bf16[384,1536]{1,0:T(8,128)(2,1)} %collective-permute-done.5.refs_3_), channel_id=1, source_target_pairs={{0,1},{1,0},{32,33},{33,32},{64,65},{65,64},{96,97},{97,96},{4,5},... | collective-permute-start | bytes 3538952 | tf_op jit(solution)/shard_map/ppermute | solution.py:40
  124.6 6.1 %collective-permute-done.19.refs_1_ = bf16[256,1536]{1,0:T(8,128)(2,1)S(1)} collective-permute-done((bf16[256,1536]{1,0:T(8,128)(2,1)S(1)}, bf16[256,1536]{1,0:T(8,128)(2,1)S(1)}, u32[]{:S(2)}, u32[]{:S(2)}) %collective-permute-start.19) | collective-permute-done | bytes 786464 | tf_op jit(solution)/shard_map/ppermute | solution.py:40
  130.7 9.2 %mlp.7.refs_7_ = f32[512,1536]{1,0:T(8,128)S(1)} custom-call(bf16[256,1536]{1,0:T(8,128)(2,1)S(1)} %collective-permute-done.18.refs_0_, bf16[256,1536]{1,0:T(8,128)(2,1)S(1)} %collective-permute-done.19.refs_1_, f32[2,1536]{1,0:T(2,128)S(1)} %get-tuple-element.14.refs_2_, bf16[384,1536]{1,0:T(8,128)(2,1)S(1)} %copy-done.2, bf16[384,1536]{1,0:T(8,128)(2,1)S(1)} %copy-done.4, ...), custom_call_target="tpu_custom_call" | custom-call | flops 4831838208 | bytes 9437184 | tf_op jit(solution)/shard_map/mlp/pallas_call | solution.py:354
  140.0 5.3 %mlp.8.refs_7_ = f32[512,1536]{1,0:T(8,128)S(1)} custom-call(bf16[256,1536]{1,0:T(8,128)(2,1)S(1)} %collective-permute-done.18.refs_0_, bf16[256,1536]{1,0:T(8,128)(2,1)S(1)} %collective-permute-done.19.refs_1_, f32[2,1536]{1,0:T(2,128)S(1)} %get-tuple-element.14.refs_2_, bf16[384,1536]{1,0:T(8,128)(2,1)} %collective-permute-done.5.refs_3_, ...), custom_call_target="tpu_custom_call" | custom-call | flops 2415919104 | bytes 4718592 | tf_op jit(solution)/shard_map/mlp/pallas_call | solution.py:354
  145.3 5.2 %mlp.9 = bf16[512,1536]{1,0:T(8,128)(2,1)S(1)} custom-call(bf16[256,1536]{1,0:T(8,128)(2,1)S(1)} %collective-permute-done.18.refs_0_, bf16[256,1536]{1,0:T(8,128)(2,1)S(1)} %collective-permute-done.19.refs_1_, f32[2,1536]{1,0:T(2,128)S(1)} %get-tuple-element.14.refs_2_, bf16[384,1536]{1,0:T(8,128)(2,1)} %collective-permute-done.12.refs_7_.refs_3_, ...), custom_call_target="tpu_custom_call" | custom-call | flops 2415919104 | bytes 4718592 | tf_op jit(solution)/shard_map/mlp/pallas_call | solution.py:354
  150.8 9.2 %mlp.5.refs_11_ = f32[512,1536]{1,0:T(8,128)S(1)} custom-call(bf16[256,1536]{1,0:T(8,128)(2,1)S(1)} %conv.2.refs_0_, bf16[256,1536]{1,0:T(8,128)(2,1)S(1)} %conv.3.refs_1_, f32[2,1536]{1,0:T(2,128)S(1)} %get-tuple-element.14.refs_2_, bf16[384,1536]{1,0:T(8,128)(2,1)S(1)} %copy-done.2, bf16[384,1536]{1,0:T(8,128)(2,1)S(1)} %copy-done.4, ...), custom_call_target="tpu_custom_call" | custom-call | flops 4831838208 | bytes 9437184 | tf_op jit(solution)/shard_map/mlp/pallas_call | solution.py:354
  160.1 8.5 %mlp.6 = f32[512,1536]{1,0:T(8,128)S(1)} custom-call(bf16[256,1536]{1,0:T(8,128)(2,1)S(1)} %conv.2.refs_0_, bf16[256,1536]{1,0:T(8,128)(2,1)S(1)} %conv.3.refs_1_, f32[2,1536]{1,0:T(2,128)S(1)} %get-tuple-element.14.refs_2_, bf16[384,1536]{1,0:T(8,128)(2,1)} %collective-permute-done.5.refs_3_, bf16[384,1536]{1,0:T(8,128)(2,1)} %collective-permute-done.9.refs_4_, ...), custom_call_target="tpu_custom_call" | custom-call | flops 4831838208 | bytes 9437184 | tf_op jit(solution)/shard_map/mlp/pallas_call | solution.py:354
  168.6 2.6 %collective-permute-done.20 = bf16[512,1536]{1,0:T(8,128)(2,1)S(1)} collective-permute-done((bf16[512,1536]{1,0:T(8,128)(2,1)S(1)}, bf16[512,1536]{1,0:T(8,128)(2,1)S(1)}, u32[]{:S(2)}, u32[]{:S(2)}) %collective-permute-start.20) | collective-permute-done | bytes 1572896 | tf_op jit(solution)/shard_map/ppermute | solution.py:40
  (76 shorter events, 20.9 us)
Async XLA Ops:
  5.7 66.3 %all-to-all-start = ((bf16[16,48,1664]{2,1,0:T(8,128)(2,1)}), bf16[16,48,1664]{2,1,0:T(8,128)(2,1)S(1)}, u32[]{:S(2)}, u32[]{:S(2)}) async-start(bf16[16,48,1664]{2,1,0:T(8,128)(2,1)} %bitcast.15), calls=%async_computation | async-start | bytes 5111808 | tf_op jit(solution)/shard_map/all_to_all | solution.py:400
  12.6 7.0 %collective-permute-start.6 = (bf16[384,1536]{1,0:T(8,128)(2,1)}, bf16[384,1536]{1,0:T(8,128)(2,1)}, u32[]{:S(2)}, u32[]{:S(2)}) collective-permute-start(bf16[384,1536]{1,0:T(8,128)(2,1)} %refs_3_.7), channel_id=1, source_target_pairs={{0,1},{1,0},{32,33},{33,32},{64,65},{65,64},{96,97},{97,96},{4,5},... | collective-permute-start | bytes 3538952 | tf_op jit(solution)/shard_map/ppermute | solution.py:40
  12.8 6.8 %collective-permute-start.7 = (bf16[384,1536]{1,0:T(8,128)(2,1)}, bf16[384,1536]{1,0:T(8,128)(2,1)}, u32[]{:S(2)}, u32[]{:S(2)}) collective-permute-start(bf16[384,1536]{1,0:T(8,128)(2,1)} %refs_4_.3), channel_id=1, source_target_pairs={{0,1},{1,0},{32,33},{33,32},{64,65},{65,64},{96,97},{97,96},{4,5},... | collective-permute-start | bytes 3538952 | tf_op jit(solution)/shard_map/ppermute | solution.py:40
  17.0 38.6 %collective-permute-start.4 = (bf16[384,1536]{1,0:T(8,128)(2,1)}, bf16[384,1536]{1,0:T(8,128)(2,1)}, u32[]{:S(2)}, u32[]{:S(2)}) collective-permute-start(bf16[384,1536]{1,0:T(8,128)(2,1)} %stack.38), channel_id=1, source_target_pairs={{0,4},{1,13},{32,36},{33,45},{64,68},{65,77},{96,100},{97,109},{4,... | collective-permute-start | bytes 3538952 | tf_op jit(solution)/shard_map/ppermute | solution.py:40
  22.0 51.0 %copy-start.10 = (bf16[1536]{0:T(1024)(128)(2,1)S(1)}, bf16[1536]{0:T(1024)(128)(2,1)}, u32[]{:S(2)}) copy-start(bf16[1536]{0:T(1024)(128)(2,1)} %param.14) | copy-start | bytes 9220
  22.1 46.2 %collective-permute-start.8 = (bf16[384,1536]{1,0:T(8,128)(2,1)}, bf16[384,1536]{1,0:T(8,128)(2,1)}, u32[]{:S(2)}, u32[]{:S(2)}) collective-permute-start(bf16[384,1536]{1,0:T(8,128)(2,1)} %stack.39), channel_id=1, source_target_pairs={{0,4},{1,13},{32,36},{33,45},{64,68},{65,77},{96,100},{97,109},{4,... | collective-permute-start | bytes 3538952 | tf_op jit(solution)/shard_map/ppermute | solution.py:40
  55.6 37.8 %collective-permute-start.16 = (bf16[384,1536]{1,0:T(8,128)(2,1)}, bf16[384,1536]{1,0:T(8,128)(2,1)}, u32[]{:S(2)}, u32[]{:S(2)}) collective-permute-start(bf16[384,1536]{1,0:T(8,128)(2,1)} %collective-permute-done.4.refs_7_), channel_id=1, source_target_pairs={{0,1},{1,0},{32,33},{33,32},{64,65},{65,64},{96,97},{97,96},{4,5},... | collective-permute-start | bytes 3538952 | tf_op jit(solution)/shard_map/ppermute | solution.py:40
  57.2 41.8 %collective-permute-start.5 = (bf16[384,1536]{1,0:T(8,128)(2,1)}, bf16[384,1536]{1,0:T(8,128)(2,1)}, u32[]{:S(2)}, u32[]{:S(2)}) collective-permute-start(bf16[384,1536]{1,0:T(8,128)(2,1)} %collective-permute-done.4.refs_7_), channel_id=1, source_target_pairs={{0,32},{1,97},{32,64},{33,1},{64,96},{65,33},{96,0},{97,65},{4,36}... | collective-permute-start | bytes 3538952 | tf_op jit(solution)/shard_map/ppermute | solution.py:40
  60.9 58.6 %collective-permute-start.12 = (bf16[384,1536]{1,0:T(8,128)(2,1)}, bf16[384,1536]{1,0:T(8,128)(2,1)}, u32[]{:S(2)}, u32[]{:S(2)}) collective-permute-start(bf16[384,1536]{1,0:T(8,128)(2,1)} %collective-permute-done.4.refs_7_), channel_id=1, source_target_pairs={{0,4},{1,13},{32,36},{33,45},{64,68},{65,77},{96,100},{97,109},{4,... | collective-permute-start | bytes 3538952 | tf_op jit(solution)/shard_map/ppermute | solution.py:40
  68.3 55.5 %collective-permute-start.9 = (bf16[384,1536]{1,0:T(8,128)(2,1)}, bf16[384,1536]{1,0:T(8,128)(2,1)}, u32[]{:S(2)}, u32[]{:S(2)}) collective-permute-start(bf16[384,1536]{1,0:T(8,128)(2,1)} %collective-permute-done.8.refs_8_), channel_id=1, source_target_pairs={{0,32},{1,97},{32,64},{33,1},{64,96},{65,33},{96,0},{97,65},{4,36}... | collective-permute-start | bytes 3538952 | tf_op jit(solution)/shard_map/ppermute | solution.py:40
  74.4 28.0 %copy-start = (f32[7,7,1536]{2,1,0:T(8,128)S(1)}, f32[7,7,1536]{2,1,0:T(8,128)}, u32[]{:S(2)}) copy-start(f32[7,7,1536]{2,1,0:T(8,128)} %refs_3_.5) | copy-start | bytes 903172
  74.8 7.4 %collective-permute-start = (bf16[32,3,1536]{2,1,0:T(4,128)(2,1)S(1)}, bf16[32,3,1536]{2,1,0:T(4,128)(2,1)S(1)}, u32[]{:S(2)}, u32[]{:S(2)}) collective-permute-start(bf16[32,3,1536]{2,1,0:T(4,128)(2,1)S(1)} %get-tuple-element.18), channel_id=1, source_target_pairs={{0,1},{1,2},{2,3},{3,4},{4,5},{5,6},{6,7},{7,8},{8,9},{9,10},{10,1... | collective-permute-start | bytes 884744 | tf_op jit(solution)/shard_map/ppermute | solution.py:66
  82.1 9.8 %collective-permute-start.1 = (bf16[32,3,1536]{2,1,0:T(4,128)(2,1)S(1)}, bf16[32,3,1536]{2,1,0:T(4,128)(2,1)S(1)}, u32[]{:S(2)}, u32[]{:S(2)}) collective-permute-start(bf16[32,3,1536]{2,1,0:T(4,128)(2,1)S(1)} %get-tuple-element.17), channel_id=1, source_target_pairs={{1,0},{2,1},{3,2},{4,3},{5,4},{6,5},{7,6},{8,7},{9,8},{10,9},{11,1... | collective-permute-start | bytes 884744 | tf_op jit(solution)/shard_map/ppermute | solution.py:66
  92.1 10.4 %collective-permute-start.3 = (bf16[3,22,1536]{2,1,0:T(8,128)(2,1)S(1)}, bf16[3,22,1536]{2,1,0:T(8,128)(2,1)S(1)}, u32[]{:S(2)}, u32[]{:S(2)}) collective-permute-start(bf16[3,22,1536]{2,1,0:T(8,128)(2,1)S(1)} %pad_maximum_fusion.1), channel_id=1, source_target_pairs={{16,0},{32,16},{48,32},{64,48},{80,64},{96,80},{112,96},{17,1},{33... | collective-permute-start | bytes 608264 | tf_op jit(solution)/shard_map/ppermute | solution.py:66
  93.4 15.6 %collective-permute-start.2 = (bf16[3,22,1536]{2,1,0:T(8,128)(2,1)S(1)}, bf16[3,22,1536]{2,1,0:T(8,128)(2,1)S(1)}, u32[]{:S(2)}, u32[]{:S(2)}) collective-permute-start(bf16[3,22,1536]{2,1,0:T(8,128)(2,1)S(1)} %pad_maximum_fusion), channel_id=1, source_target_pairs={{0,16},{16,32},{32,48},{48,64},{64,80},{80,96},{96,112},{1,17},{17... | collective-permute-start | bytes 608264 | tf_op jit(solution)/shard_map/ppermute | solution.py:66
  98.9 24.9 %collective-permute-start.17 = (bf16[384,1536]{1,0:T(8,128)(2,1)}, bf16[384,1536]{1,0:T(8,128)(2,1)S(1)}, u32[]{:S(2)}, u32[]{:S(2)}) collective-permute-start(bf16[384,1536]{1,0:T(8,128)(2,1)} %collective-permute-done.8.refs_8_), channel_id=1, source_target_pairs={{0,1},{1,0},{32,33},{33,32},{64,65},{65,64},{96,97},{97,96},{4,5},... | collective-permute-start | bytes 3538952 | tf_op jit(solution)/shard_map/ppermute | solution.py:40
  102.5 21.8 %collective-permute-start.14 = (bf16[384,1536]{1,0:T(8,128)(2,1)}, bf16[384,1536]{1,0:T(8,128)(2,1)S(1)}, u32[]{:S(2)}, u32[]{:S(2)}) collective-permute-start(bf16[384,1536]{1,0:T(8,128)(2,1)} %collective-permute-done.5.refs_3_), channel_id=1, source_target_pairs={{0,4},{1,13},{32,36},{33,45},{64,68},{65,77},{96,100},{97,109},{4,... | collective-permute-start | bytes 3538952 | tf_op jit(solution)/shard_map/ppermute | solution.py:40
  109.0 12.6 %collective-permute-start.18 = (bf16[256,1536]{1,0:T(8,128)(2,1)S(1)}, bf16[256,1536]{1,0:T(8,128)(2,1)S(1)}, u32[]{:S(2)}, u32[]{:S(2)}) collective-permute-start(bf16[256,1536]{1,0:T(8,128)(2,1)S(1)} %conv.2.refs_0_), channel_id=1, source_target_pairs={{0,2},{1,19},{32,34},{33,51},{64,66},{65,83},{96,98},{97,115},{4,6... | collective-permute-start | bytes 2359304 | tf_op jit(solution)/shard_map/ppermute | solution.py:40
  119.5 11.2 %collective-permute-start.19 = (bf16[256,1536]{1,0:T(8,128)(2,1)S(1)}, bf16[256,1536]{1,0:T(8,128)(2,1)S(1)}, u32[]{:S(2)}, u32[]{:S(2)}) collective-permute-start(bf16[256,1536]{1,0:T(8,128)(2,1)S(1)} %conv.3.refs_1_), channel_id=1, source_target_pairs={{0,2},{1,19},{32,34},{33,51},{64,66},{65,83},{96,98},{97,115},{4,6... | collective-permute-start | bytes 2359304 | tf_op jit(solution)/shard_map/ppermute | solution.py:40
  121.6 18.3 %collective-permute-start.10 = (bf16[384,1536]{1,0:T(8,128)(2,1)}, bf16[384,1536]{1,0:T(8,128)(2,1)S(1)}, u32[]{:S(2)}, u32[]{:S(2)}) collective-permute-start(bf16[384,1536]{1,0:T(8,128)(2,1)} %collective-permute-done.5.refs_3_), channel_id=1, source_target_pairs={{0,1},{1,0},{32,33},{33,32},{64,65},{65,64},{96,97},{97,96},{4,5},... | collective-permute-start | bytes 3538952 | tf_op jit(solution)/shard_map/ppermute | solution.py:40
  123.8 16.2 %collective-permute-start.11 = (bf16[384,1536]{1,0:T(8,128)(2,1)}, bf16[384,1536]{1,0:T(8,128)(2,1)S(1)}, u32[]{:S(2)}, u32[]{:S(2)}) collective-permute-start(bf16[384,1536]{1,0:T(8,128)(2,1)} %collective-permute-done.9.refs_4_), channel_id=1, source_target_pairs={{0,1},{1,0},{32,33},{33,32},{64,65},{65,64},{96,97},{97,96},{4,5},... | collective-permute-start | bytes 3538952 | tf_op jit(solution)/shard_map/ppermute | solution.py:40
  123.8 21.5 %collective-permute-start.13 = (bf16[384,1536]{1,0:T(8,128)(2,1)}, bf16[384,1536]{1,0:T(8,128)(2,1)S(1)}, u32[]{:S(2)}, u32[]{:S(2)}) collective-permute-start(bf16[384,1536]{1,0:T(8,128)(2,1)} %collective-permute-done.12.refs_7_.refs_3_), channel_id=1, source_target_pairs={{0,1},{1,0},{32,33},{33,32},{64,65},{65,64},{96,97},{97,96},{4,5},... | collective-permute-start | bytes 3538952 | tf_op jit(solution)/shard_map/ppermute | solution.py:40
  124.3 21.0 %collective-permute-start.15 = (bf16[384,1536]{1,0:T(8,128)(2,1)S(1)}, bf16[384,1536]{1,0:T(8,128)(2,1)S(1)}, u32[]{:S(2)}, u32[]{:S(2)}) collective-permute-start(bf16[384,1536]{1,0:T(8,128)(2,1)S(1)} %collective-permute-done.14.refs_9_.refs_5_), channel_id=1, source_target_pairs={{0,1},{1,0},{32,33},{33,32},{64,65},{65,64},{96,97},{97,96},{4,5},... | collective-permute-start | bytes 3538952 | tf_op jit(solution)/shard_map/ppermute | solution.py:40
  150.5 20.8 %collective-permute-start.20 = (bf16[512,1536]{1,0:T(8,128)(2,1)S(1)}, bf16[512,1536]{1,0:T(8,128)(2,1)S(1)}, u32[]{:S(2)}, u32[]{:S(2)}) collective-permute-start(bf16[512,1536]{1,0:T(8,128)(2,1)S(1)} %mlp.9), channel_id=1, source_target_pairs={{0,18},{1,3},{32,50},{33,35},{64,82},{65,67},{96,114},{97,99},{4,2... | collective-permute-start | bytes 4718600 | tf_op jit(solution)/shard_map/ppermute | solution.py:40
  (9 other events, 85.6 us)
